TPU v7x, 32 devices: a whole 2x2x4 slice. The times are simulated.
32 devices in a mesh: rep: 4 (over x, core), fsdp: 4 (over z), seq: 2 (over y).
Axes of the slice: x: 2, y: 2, z: 4, core: 2. Of those that a mesh axis runs over, the one named last changes fastest.
Arguments:
- inputs: bfloat16 [2, 16, 1024, 1024], P(None, ('rep', 'fsdp'), 'seq'), may hold values from -6 to 6
- cotangent: bfloat16 [2, 16, 1024, 1024], P(None, ('rep', 'fsdp'), 'seq'), may hold values from -6 to 6
- ln_gain: bfloat16 [6, 1024], P(None, 'fsdp'), may hold values from 0.5 to 1.5
- ln_bias: bfloat16 [6, 1024], P(None, 'fsdp'), may hold values from -1.75 to 1.75
- ffn_in: bfloat16 [2, 1024, 4096], P(None, 'fsdp'), may hold values from -0.1875 to 0.1875
- ffn_in_bias: bfloat16 [2, 4096], P(None, 'fsdp'), may hold values from -3 to 3
- ffn_out: bfloat16 [2, 4096, 1024], P(None, 'fsdp'), may hold values from -0.09375 to 0.09375
- ffn_out_bias: bfloat16 [2, 1024], P(None, 'fsdp'), may hold values from -1.75 to 1.75
- qkv_weight: bfloat16 [1024, 3072], P('fsdp'), may hold values from -0.1875 to 0.1875
- attn_out: bfloat16 [1024, 1024], P('fsdp'), may hold values from -1.5 to 1.5
- attn_bias: bfloat16 [3, 1024], P(None, 'fsdp'), may hold values from -1.75 to 1.75
- dist_embed: bfloat16 [73, 64], P(None, 'fsdp'), may hold values from -6 to 6
- pw_in: bfloat16 [1024, 2048], P('fsdp'), may hold values from -0.1875 to 0.1875
- depthwise: bfloat16 [31, 1024], P(None, 'fsdp'), may hold values from -1 to 1
- pw_out: bfloat16 [1024, 1024], P('fsdp'), may hold values from -0.1875 to 0.1875
Outputs:
- activations: bfloat16 [2, 16, 1024, 1024], P(None, ('rep', 'fsdp'), 'seq')
- input_grad: float32 [2, 16, 1024, 1024], P(None, ('rep', 'fsdp'), 'seq')
- grad_ln_gain: float32 [6, 1024], P(None, 'fsdp')
- grad_ln_bias: float32 [6, 1024], P(None, 'fsdp')
- grad_ffn_in: float32 [2, 1024, 4096], P(None, 'fsdp')
- grad_ffn_in_bias: float32 [2, 4096], P(None, 'fsdp')
- grad_ffn_out: float32 [2, 4096, 1024], P(None, 'fsdp')
- grad_ffn_out_bias: float32 [2, 1024], P(None, 'fsdp')
- grad_qkv_weight: float32 [1024, 3072], P('fsdp')
- grad_attn_out: float32 [1024, 1024], P('fsdp')
- grad_attn_bias: float32 [3, 1024], P(None, 'fsdp')
- grad_dist_embed: float32 [73, 64], P(None, 'fsdp')
- grad_pw_in: float32 [1024, 2048], P('fsdp')
- grad_depthwise: float32 [31, 1024], P(None, 'fsdp')
- grad_pw_out: float32 [1024, 1024], P('fsdp')
All inputs are finite; a program needn't handle non-finite values.
Results may differ from a plain program's by a relative error of at most 0.02.
Values may be sent and summed in bfloat16 or wider, within the bound.
No kernel may reach another device: no remote copies, remote signals or barrier semaphores. Data moves between devices by JAX's collectives and lax.ppermute only.
A program may use at most 576 MiB of HBM per device.

v0:
```python
import jax
import jax.numpy as jnp
from jax import lax
from jax.sharding import PartitionSpec as P

H = 16
HD = 64
KERNEL = 31
LEFT = 64
RIGHT = 8


EPS = 1e-05
LOW = jnp.bfloat16
HIGH = jnp.float32


def from_behind(value, axis, steps):
    count = lax.axis_size(axis)
    first, last = (max(0, -steps), min(count, count - steps))
    return lax.ppermute(value, axis, [(source, source + steps) for source in range(first, last)])


def as_sent(array):
    return jax.tree.map(lambda a: a.astype(jnp.bfloat16) if a.dtype == jnp.float32 else a, array)


def layer_norm(values, gain, shift):
    mean = jnp.mean(values, axis=-1, keepdims=True)
    centred = values - mean
    var = jnp.mean(centred * centred, axis=-1, keepdims=True)
    return centred * lax.rsqrt(var + EPS) * gain + shift


def matmul(left, right):
    return jnp.dot(left, right, preferred_element_type=HIGH)


def left_t(left, right):
    return lax.dot_general(left, right, (((0,), (0,)), ((), ())), preferred_element_type=HIGH)


def right_t(left, right):
    return lax.dot_general(left, right, (((1,), (1,)), ((), ())), preferred_element_type=HIGH)


def fetch(shards):
    return (
        lax.all_gather(shards[0], "fsdp", axis=1, tiled=True),
        lax.all_gather(shards[1], "fsdp", axis=1, tiled=True),
        lax.all_gather(shards[2], "fsdp", axis=1, tiled=True),
        lax.all_gather(shards[3], "fsdp", axis=1, tiled=True),
        lax.all_gather(shards[4], "fsdp", axis=1, tiled=True),
        lax.all_gather(shards[5], "fsdp", axis=1, tiled=True),
        lax.all_gather(shards[6], "fsdp", axis=0, tiled=True),
        lax.all_gather(shards[7], "fsdp", axis=0, tiled=True),
        lax.all_gather(shards[8], "fsdp", axis=1, tiled=True),
        lax.all_gather(shards[9], "fsdp", axis=1, tiled=True),
        lax.all_gather(shards[10], "fsdp", axis=0, tiled=True),
        lax.all_gather(shards[11], "fsdp", axis=1, tiled=True),
        lax.all_gather(shards[12], "fsdp", axis=0, tiled=True),
    )


def unpack(whole):
    gains, shifts, f_in, f_in_b, f_out, f_out_b, w_qkv, w_o, a_bias, embed, c_in, kernel, c_out = (
        whole
    )
    return (
        gains.astype(HIGH),
        shifts.astype(HIGH),
        f_in,
        f_in_b.astype(HIGH),
        f_out,
        f_out_b.astype(HIGH),
        w_qkv,
        w_o,
        a_bias.astype(HIGH),
        embed,
        c_in,
        kernel.astype(HIGH),
        c_out,
    )


def ffn_forward(values, gain, shift, w_in, b_in, w_out, b_out):
    normed, norm_pull = jax.vjp(layer_norm, values, gain, shift)
    normed_low = normed.astype(LOW)
    linear = matmul(normed_low, w_in)
    active, act_pull = jax.vjp(lambda lin, bias: jax.nn.silu(lin + bias), linear, b_in)
    active_low = active.astype(LOW)
    out = matmul(active_low, w_out) + b_out
    return (out, (norm_pull, normed_low, act_pull, active_low))


def ffn_backward(grad, kept, w_in, w_out):
    norm_pull, normed_low, act_pull, active_low = kept
    grad_b_out = jnp.sum(grad, axis=0)
    grad_low = grad.astype(LOW)
    grad_w_out = left_t(active_low, grad_low)
    grad_active = right_t(grad_low, w_out)
    grad_lin, grad_b_in = act_pull(grad_active)
    lin_low = grad_lin.astype(LOW)
    grad_w_in = left_t(normed_low, lin_low)
    grad_normed = right_t(lin_low, w_in)
    grad_values, grad_gain, grad_shift = norm_pull(grad_normed)
    return (grad_values, (grad_gain, grad_shift, grad_w_in, grad_b_in, grad_w_out, grad_b_out))


def scores_of(query4, key4, embed, onehot):
    direct_path = jnp.einsum("cnhd,clhd->chnl", query4, key4, preferred_element_type=HIGH)
    rel_low = jnp.einsum("cnhd,bd->chnb", query4, embed, preferred_element_type=HIGH).astype(LOW)
    placed = jnp.einsum("chnb,nbl->chnl", rel_low, onehot, preferred_element_type=HIGH)
    return (direct_path + placed) * HD ** (-0.5)


def attn_forward(values, gain, shift, w_qkv, bias, embed, w_o, onehot):
    clips, rows, width = values.shape
    normed, norm_pull = jax.vjp(layer_norm, values, gain, shift)
    normed_low = normed.astype(LOW).reshape(clips * rows, width)
    proj = matmul(normed_low, w_qkv).reshape(clips, rows, 3 * width)
    query_rows = (proj[..., :width] + bias[0]).astype(LOW)
    key = proj[..., width : 2 * width].astype(LOW)
    value_rows = (proj[..., 2 * width :] + bias[1]).astype(LOW)
    keys, values_all = (
        lax.all_gather(key, "seq", axis=1, tiled=True),
        lax.all_gather(value_rows, "seq", axis=1, tiled=True),
    )
    span = keys.shape[1]
    query4 = query_rows.reshape(clips, rows, H, HD)
    key4 = keys.reshape(clips, span, H, HD)
    value4 = values_all.reshape(clips, span, H, HD)
    scores = scores_of(query4, key4, embed, onehot)
    total_log = jax.nn.logsumexp(scores, axis=-1)
    prob_low = jnp.exp(scores - total_log[..., None]).astype(LOW)
    mixed_precision = jnp.einsum("chnl,clhd->cnhd", prob_low, value4, preferred_element_type=HIGH)
    mixed_low = mixed_precision.astype(LOW).reshape(clips * rows, width)
    out = matmul(mixed_low, w_o) + bias[2]
    return (out, (norm_pull, normed_low, query4, key4, value4, total_log, mixed_low))


def attn_backward(grad, kept, w_qkv, w_o, embed, onehot):
    norm_pull, normed_low, query4, key4, value4, total_log, mixed_low = kept
    clips, rows = (query4.shape[0], query4.shape[1])
    span = key4.shape[1]
    width = H * HD
    scale = HD ** (-0.5)
    grad_b_o = jnp.sum(grad, axis=0)
    grad_low = grad.astype(LOW)
    grad_w_o = left_t(mixed_low, grad_low)
    grad_mixed = right_t(grad_low, w_o).astype(LOW).reshape(clips, rows, H, HD)
    scores = scores_of(query4, key4, embed, onehot)
    attention_probability = jnp.exp(scores - total_log[..., None])
    prob_low = attention_probability.astype(LOW)
    grad_prob = jnp.einsum("cnhd,clhd->chnl", grad_mixed, value4, preferred_element_type=HIGH)
    grad_value = jnp.einsum("chnl,cnhd->clhd", prob_low, grad_mixed, preferred_element_type=HIGH)
    grad_scores = (
        attention_probability
        * (grad_prob - jnp.sum(attention_probability * grad_prob, axis=-1, keepdims=True))
    ).astype(LOW)
    grad_rel = (
        jnp.einsum("chnl,nbl->chnb", grad_scores, onehot, preferred_element_type=HIGH) * scale
    ).astype(LOW)
    grad_query = scale * jnp.einsum(
        "chnl,clhd->cnhd", grad_scores, key4, preferred_element_type=HIGH
    )
    grad_query = grad_query + jnp.einsum(
        "chnb,bd->cnhd", grad_rel, embed, preferred_element_type=HIGH
    )
    grad_embed = jnp.einsum("chnb,cnhd->bd", grad_rel, query4, preferred_element_type=HIGH)
    grad_key = scale * jnp.einsum(
        "chnl,cnhd->clhd", grad_scores, query4, preferred_element_type=HIGH
    )
    mine_key, mine_value = (
        lax.psum_scatter(
            grad_key.reshape(clips, span, width).astype(jnp.bfloat16),
            "seq",
            scatter_dimension=1,
            tiled=True,
        ).astype(jnp.float32),
        lax.psum_scatter(
            grad_value.reshape(clips, span, width).astype(jnp.bfloat16),
            "seq",
            scatter_dimension=1,
            tiled=True,
        ).astype(jnp.float32),
    )
    grad_query = grad_query.reshape(clips, rows, width)
    grad_b_q = jnp.sum(grad_query, axis=(0, 1))
    grad_b_v = jnp.sum(mine_value, axis=(0, 1))
    grad_proj = (
        jnp.concatenate([grad_query, mine_key, mine_value], axis=-1)
        .astype(LOW)
        .reshape(clips * rows, 3 * width)
    )
    grad_w_qkv = left_t(normed_low, grad_proj)
    grad_normed = right_t(grad_proj, w_qkv).reshape(clips, rows, width)
    grad_values, grad_gain, grad_shift = norm_pull(grad_normed)
    grad_bias = jnp.stack([grad_b_q, grad_b_v, grad_b_o])
    return (
        grad_values.reshape(clips * rows, width),
        (grad_gain, grad_shift, grad_w_qkv, grad_bias, grad_embed, grad_w_o),
    )


def depthwise_block(extended, kernel, gain, shift):
    taps = kernel.shape[0]
    span = extended.shape[1] - taps + 1
    total = kernel[0] * extended[:, 0:span, :]
    for tap in range(1, taps):
        total = total + kernel[tap] * extended[:, tap : tap + span, :]
    return jax.nn.silu(layer_norm(total, gain, shift))


def conv_forward(values, gain, shift, w_in, kernel, gain_two, shift_two, w_out):
    clips, rows, width = values.shape
    normed, norm_pull = jax.vjp(layer_norm, values, gain, shift)
    normed_low = normed.astype(LOW).reshape(clips * rows, width)
    pre = matmul(normed_low, w_in).reshape(clips, rows, 2 * width)
    gated, gate_pull = jax.vjp(
        lambda both: both[..., :width] * jax.nn.sigmoid(both[..., width:]), pre
    )
    gated_low = gated.astype(LOW)
    rim = from_behind(gated_low[:, rows - (KERNEL - 1) :, :], "seq", 1)
    extended = jnp.concatenate([rim, gated_low], axis=1).astype(HIGH)
    mixed_precision, mix_pull = jax.vjp(depthwise_block, extended, kernel, gain_two, shift_two)
    mixed_low = mixed_precision.astype(LOW).reshape(clips * rows, width)
    out = matmul(mixed_low, w_out)
    return (out, (norm_pull, normed_low, gate_pull, mix_pull, mixed_low))


def conv_backward(grad, kept, w_in, w_out, clips, rows):
    norm_pull, normed_low, gate_pull, mix_pull, mixed_low = kept
    width = grad.shape[1]
    grad_low = grad.astype(LOW)
    grad_w_out = left_t(mixed_low, grad_low)
    grad_mixed = right_t(grad_low, w_out).reshape(clips, rows, width)
    grad_ext, grad_kernel, grad_gain_two, grad_shift_two = mix_pull(grad_mixed)
    returned = from_behind(grad_ext[:, : KERNEL - 1, :].astype(jnp.bfloat16), "seq", -1).astype(
        jnp.float32
    )
    grad_gated = grad_ext[:, KERNEL - 1 :, :] + jnp.pad(
        returned, ((0, 0), (rows - (KERNEL - 1), 0), (0, 0))
    )
    (grad_pre,) = gate_pull(grad_gated)
    pre_low = grad_pre.astype(LOW).reshape(clips * rows, 2 * width)
    grad_w_in = left_t(normed_low, pre_low)
    grad_normed = right_t(pre_low, w_in).reshape(clips, rows, width)
    grad_values, grad_gain, grad_shift = norm_pull(grad_normed)
    return (
        grad_values.reshape(clips * rows, width),
        (grad_gain, grad_shift, grad_w_in, grad_kernel, grad_gain_two, grad_shift_two, grad_w_out),
    )


def body(
    inputs,
    cotangent,
    ln_gain,
    ln_bias,
    ffn_in,
    ffn_in_bias,
    ffn_out,
    ffn_out_bias,
    qkv_weight,
    attn_out,
    attn_bias,
    dist_embed,
    pw_in,
    depthwise,
    pw_out,
):
    shards = (
        ln_gain,
        ln_bias,
        ffn_in,
        ffn_in_bias,
        ffn_out,
        ffn_out_bias,
        qkv_weight,
        attn_out,
        attn_bias,
        dist_embed,
        pw_in,
        depthwise,
        pw_out,
    )
    micro, clips, rows, width = inputs.shape
    span = rows * lax.axis_size("seq")
    positions = lax.axis_index("seq") * rows + jnp.arange(rows, dtype=jnp.int32)
    bucket = (
        jnp.clip(jnp.arange(span, dtype=jnp.int32)[None, :] - positions[:, None], -LEFT, RIGHT)
        + LEFT
    )
    onehot = (
        bucket[:, None, :] == jnp.arange(LEFT + RIGHT + 1, dtype=jnp.int32)[None, :, None]
    ).astype(LOW)
    outputs = []
    input_grads = []
    totals = None
    for step in range(micro):
        whole = fetch(shards)
        (
            gains,
            shifts,
            f_in,
            f_in_b,
            f_out,
            f_out_b,
            w_qkv,
            w_o,
            a_bias,
            embed,
            c_in,
            kernel,
            c_out,
        ) = unpack(whole)
        start_rows = inputs[step].astype(HIGH).reshape(clips * rows, width)
        branch_one, keep_one = ffn_forward(
            start_rows, gains[0], shifts[0], f_in[0], f_in_b[0], f_out[0], f_out_b[0]
        )
        first = start_rows + 0.5 * branch_one
        branch_two, keep_two = attn_forward(
            first.reshape(clips, rows, width),
            gains[1],
            shifts[1],
            w_qkv,
            a_bias,
            embed,
            w_o,
            onehot,
        )
        second = first + branch_two
        branch_three, keep_three = conv_forward(
            second.reshape(clips, rows, width),
            gains[2],
            shifts[2],
            c_in,
            kernel,
            gains[3],
            shifts[3],
            c_out,
        )
        third = second + branch_three
        branch_four, keep_four = ffn_forward(
            third, gains[4], shifts[4], f_in[1], f_in_b[1], f_out[1], f_out_b[1]
        )
        fourth = third + 0.5 * branch_four
        final, final_pull = jax.vjp(layer_norm, fourth, gains[5], shifts[5])
        outputs.append(final.astype(LOW).reshape(clips, rows, width))
        again = (
            lax.all_gather(shards[0], "fsdp", axis=1, tiled=True),
            lax.all_gather(shards[1], "fsdp", axis=1, tiled=True),
            lax.all_gather(shards[2], "fsdp", axis=1, tiled=True),
            lax.all_gather(shards[3], "fsdp", axis=1, tiled=True),
            lax.all_gather(shards[4], "fsdp", axis=1, tiled=True),
            lax.all_gather(shards[5], "fsdp", axis=1, tiled=True),
            lax.all_gather(shards[6], "fsdp", axis=0, tiled=True),
            lax.all_gather(shards[7], "fsdp", axis=0, tiled=True),
            lax.all_gather(shards[8], "fsdp", axis=1, tiled=True),
            lax.all_gather(shards[9], "fsdp", axis=1, tiled=True),
            lax.all_gather(shards[10], "fsdp", axis=0, tiled=True),
            lax.all_gather(shards[11], "fsdp", axis=1, tiled=True),
            lax.all_gather(shards[12], "fsdp", axis=0, tiled=True),
        )
        (
            gains,
            shifts,
            f_in,
            f_in_b,
            f_out,
            f_out_b,
            w_qkv,
            w_o,
            a_bias,
            embed,
            c_in,
            kernel,
            c_out,
        ) = unpack(again)
        grad_fourth, gain_five, shift_five = final_pull(
            cotangent[step].astype(HIGH).reshape(clips * rows, width)
        )
        grad_inner, four_grads = ffn_backward(0.5 * grad_fourth, keep_four, f_in[1], f_out[1])
        grad_third = grad_fourth + grad_inner
        grad_inner, three_grads = conv_backward(grad_third, keep_three, c_in, c_out, clips, rows)
        grad_second = grad_third + grad_inner
        grad_inner, two_grads = attn_backward(grad_second, keep_two, w_qkv, w_o, embed, onehot)
        grad_first = grad_second + grad_inner
        grad_inner, one_grads = ffn_backward(0.5 * grad_first, keep_one, f_in[0], f_out[0])
        input_grads.append((grad_first + grad_inner).reshape(clips, rows, width))
        grads = (
            jnp.stack(
                [
                    one_grads[0],
                    two_grads[0],
                    three_grads[0],
                    three_grads[4],
                    four_grads[0],
                    gain_five,
                ]
            ),
            jnp.stack(
                [
                    one_grads[1],
                    two_grads[1],
                    three_grads[1],
                    three_grads[5],
                    four_grads[1],
                    shift_five,
                ]
            ),
            jnp.stack([one_grads[2], four_grads[2]]),
            jnp.stack([one_grads[3], four_grads[3]]),
            jnp.stack([one_grads[4], four_grads[4]]),
            jnp.stack([one_grads[5], four_grads[5]]),
            two_grads[2],
            two_grads[5],
            two_grads[3],
            two_grads[4],
            three_grads[2],
            three_grads[3],
            three_grads[6],
        )
        totals = grads if totals is None else jax.tree.map(jnp.add, totals, grads)
    totals = (
        lax.psum_scatter(
            totals[0].astype(jnp.bfloat16), "fsdp", scatter_dimension=1, tiled=True
        ).astype(jnp.float32),
        lax.psum_scatter(
            totals[1].astype(jnp.bfloat16), "fsdp", scatter_dimension=1, tiled=True
        ).astype(jnp.float32),
        lax.psum_scatter(
            totals[2].astype(jnp.bfloat16), "fsdp", scatter_dimension=1, tiled=True
        ).astype(jnp.float32),
        lax.psum_scatter(
            totals[3].astype(jnp.bfloat16), "fsdp", scatter_dimension=1, tiled=True
        ).astype(jnp.float32),
        lax.psum_scatter(
            totals[4].astype(jnp.bfloat16), "fsdp", scatter_dimension=1, tiled=True
        ).astype(jnp.float32),
        lax.psum_scatter(
            totals[5].astype(jnp.bfloat16), "fsdp", scatter_dimension=1, tiled=True
        ).astype(jnp.float32),
        lax.psum_scatter(
            totals[6].astype(jnp.bfloat16), "fsdp", scatter_dimension=0, tiled=True
        ).astype(jnp.float32),
        lax.psum_scatter(
            totals[7].astype(jnp.bfloat16), "fsdp", scatter_dimension=0, tiled=True
        ).astype(jnp.float32),
        lax.psum_scatter(
            totals[8].astype(jnp.bfloat16), "fsdp", scatter_dimension=1, tiled=True
        ).astype(jnp.float32),
        lax.psum_scatter(
            totals[9].astype(jnp.bfloat16), "fsdp", scatter_dimension=1, tiled=True
        ).astype(jnp.float32),
        lax.psum_scatter(
            totals[10].astype(jnp.bfloat16), "fsdp", scatter_dimension=0, tiled=True
        ).astype(jnp.float32),
        lax.psum_scatter(
            totals[11].astype(jnp.bfloat16), "fsdp", scatter_dimension=1, tiled=True
        ).astype(jnp.float32),
        lax.psum_scatter(
            totals[12].astype(jnp.bfloat16), "fsdp", scatter_dimension=0, tiled=True
        ).astype(jnp.float32),
    )
    summed = jax.tree.map(
        lambda part: part.astype(jnp.float32), lax.psum(as_sent(totals), ("rep", "seq"))
    )
    return (
        jnp.stack(outputs),
        jnp.stack(input_grads),
        summed[0],
        summed[1],
        summed[2],
        summed[3],
        summed[4],
        summed[5],
        summed[6],
        summed[7],
        summed[8],
        summed[9],
        summed[10],
        summed[11],
        summed[12],
    )


def solution(mesh):
    return jax.shard_map(
        body,
        mesh=mesh,
        in_specs=(
            P(None, ("rep", "fsdp"), "seq", None),
            P(None, ("rep", "fsdp"), "seq", None),
            P(None, "fsdp"),
            P(None, "fsdp"),
            P(None, "fsdp", None),
            P(None, "fsdp"),
            P(None, "fsdp", None),
            P(None, "fsdp"),
            P("fsdp", None),
            P("fsdp", None),
            P(None, "fsdp"),
            P(None, "fsdp"),
            P("fsdp", None),
            P(None, "fsdp"),
            P("fsdp", None),
        ),
        out_specs=(
            P(None, ("rep", "fsdp"), "seq", None),
            P(None, ("rep", "fsdp"), "seq", None),
            P(None, "fsdp"),
            P(None, "fsdp"),
            P(None, "fsdp", None),
            P(None, "fsdp"),
            P(None, "fsdp", None),
            P(None, "fsdp"),
            P("fsdp", None),
            P("fsdp", None),
            P(None, "fsdp"),
            P(None, "fsdp"),
            P("fsdp", None),
            P(None, "fsdp"),
            P("fsdp", None),
        ),
        check_vma=False,
    )
```

profile of v0, /device:TPU:0, one launch (start us, length us, event | category | flops | bytes accessed | tf_op | source)
XLA Modules:
  0.0 2695.2 jit_solution(11328910851795117745)
XLA Ops:
  9.5 12.6 all_gather.39
  34.1 19.3 all_gather.34
  53.5 23.8 all_gather.35
  77.3 21.7 all_gather.37
  103.2 196.7 %all-gather.11.cloned.1.call-done = bf16[2,1024,4096]{2,1,0:T(8,128)(2,1)} async-done(((bf16[2,256,4096]{2,1,0:T(8,128)(2,1)}), bf16[2,1024,4096]{2,1,0:T(8,128)(2,1)}) %all-gather.11.cloned.1.call-update) | async-done | bytes 16777232 | tf_op jit(solution)/shard_map/all_gather | solution.py:51
  310.4 276.1 %all-gather.13.cloned.1.call-done = bf16[2,4096,1024]{2,1,0:T(8,128)(2,1)} async-done(((bf16[2,1024,1024]{2,1,0:T(8,128)(2,1)}), bf16[2,4096,1024]{2,1,0:T(8,128)(2,1)}) %all-gather.13.cloned.1.call-update) | async-done | bytes 16777232 | tf_op jit(solution)/shard_map/all_gather | solution.py:53
  599.2 102.4 %all-gather.15.cloned.1.call-done = bf16[1024,3072]{1,0:T(8,128)(2,1)} async-done(((bf16[256,3072]{1,0:T(8,128)(2,1)}), bf16[1024,3072]{1,0:T(8,128)(2,1)}) %all-gather.15.cloned.1.call-update) | async-done | bytes 6291472 | tf_op jit(solution)/shard_map/all_gather | solution.py:55
  747.4 13.1 all_gather.90
  761.9 13.3 all_gather.88
  786.3 30.9 %fusion.2 = f32[512,1024,16]{1,2,0:T(8,128)} fusion(bf16[16,512,73]{2,0,1:T(8,128)(2,1)} %copy.86, s32[512,1024]{1,0:T(8,128)} %clamp_add_fusion), kind=kOutput, calls=%fused_computation.3 | convolution fusion | flops 1263009792 | bytes 36847616 | tf_op jit(solution)/shard_map/chnb,nbl->chnl/dot_general | solution.py:113
  817.2 29.7 %fusion.3 = f32[512,1024,16]{1,2,0:T(8,128)} fusion(bf16[16,512,73]{2,0,1:T(8,128)(2,1)S(1)} %copy-done.99, s32[512,1024]{1,0:T(8,128)S(1)} %copy-done.96), kind=kOutput, calls=%fused_computation.4 | convolution fusion | flops 1263009792 | bytes 36847616 | tf_op jit(solution)/shard_map/chnb,nbl->chnl/dot_general | solution.py:113
  850.9 36.0 %fusion.270 = (f32[16,512]{1,0:T(8,128)S(1)}, f32[1,16,512,1024]{3,2,1,0:T(8,128)}) fusion(f32[512,1024,16]{1,2,0:T(8,128)} %fusion.2, bf16[512,16,64]{0,2,1:T(8,128)(2,1)S(1)} %bitcast.626, bf16[1024,16,64]{0,2,1:T(8,128)(2,1)} %bitcast.633), kind=kOutput, calls=%fused_computation.605 | convolution fusion | flops 1098899456 | bytes 70287360 | tf_op jit(solution)/shard_map/cnhd,clhd->chnl/dot_general | solution.py:111
  886.8 14.3 exponential_reduce_fusion
  904.1 15.6 fusion.144
  943.9 35.5 %fusion.266 = (f32[16,512]{1,0:T(8,128)S(1)}, f32[1,16,512,1024]{3,2,1,0:T(8,128)}) fusion(f32[512,1024,16]{1,2,0:T(8,128)} %fusion.3, bf16[512,16,64]{0,2,1:T(8,128)(2,1)S(1)} %bitcast.622, bf16[1024,16,64]{0,2,1:T(8,128)(2,1)S(1)} %bitcast.635), kind=kOutput, calls=%fused_computation.601 | convolution fusion | flops 1098899456 | bytes 70287360 | tf_op jit(solution)/shard_map/cnhd,clhd->chnl/dot_general | solution.py:111
  979.4 14.5 exponential_reduce_fusion.1
  996.9 14.6 fusion.147
  1102.5 13.8 fusion.276
  1124.5 12.7 fusion.274
  1182.1 16.2 broadcast_multiply_fusion.40
  1204.7 13.0 broadcast_multiply_fusion
  1217.8 20.5 pad_add_fusion.1
  1239.7 20.1 pad_add_fusion
  1284.7 22.4 fusion.15
  1307.1 27.8 %fusion.20 = bf16[16,512,1024]{2,1,0:T(8,128)(2,1)} fusion(f32[16,512,1024]{2,1,0:T(8,128)} %get-tuple-element.360, f32[1,16,512,1024]{3,2,1,0:T(8,128)} %get-tuple-element.341, f32[16,512]{1,0:T(8,128)S(1)} %get-tuple-element.359, f32[16,512]{1,0:T(8,128)S(1)} %copy-done.103), kind=kLoop, calls=%fused_computation.33 | loop fusion | flops 33554432 | bytes 83951616 | tf_op jit(solution)/shard_map/reshape.139
  1352.2 15.6 fusion.135
  1369.4 22.7 fusion.13
  1392.0 28.1 %fusion.21 = bf16[16,512,1024]{2,1,0:T(8,128)(2,1)} fusion(f32[16,512,1024]{2,1,0:T(8,128)} %get-tuple-element.363, f32[1,16,512,1024]{3,2,1,0:T(8,128)} %get-tuple-element.349, f32[16,512]{1,0:T(8,128)S(1)} %get-tuple-element.362, f32[16,512]{1,0:T(8,128)S(1)} %copy-done.101), kind=kLoop, calls=%fused_computation.34 | loop fusion | flops 33554432 | bytes 83951616 | tf_op jit(solution)/shard_map/reshape.362
  1430.4 15.5 fusion.132
  1454.3 14.9 convolution_bitcast_fusion
  1475.3 38.4 %fusion.138 = bf16[16,512,73]{2,0,1:T(8,128)(2,1)} fusion(bf16[16,512,1024]{2,1,0:T(8,128)(2,1)} %fusion.20, s32[512,1024]{1,0:T(8,128)S(1)} %copy-done.97), kind=kOutput, calls=%fused_computation.354 | convolution fusion | flops 1264205824 | bytes 20070400 | tf_op jit(solution)/shard_map/chnl,nbl->chnb/dot_general | solution.py:162
  1529.2 38.5 %fusion.141 = bf16[16,512,73]{2,0,1:T(8,128)(2,1)} fusion(bf16[16,512,1024]{2,1,0:T(8,128)(2,1)} %fusion.21, s32[512,1024]{1,0:T(8,128)S(1)} %copy-done.98), kind=kOutput, calls=%fused_computation.355 | convolution fusion | flops 1264205824 | bytes 20070400 | tf_op jit(solution)/shard_map/chnl,nbl->chnb/dot_general | solution.py:162
  1629.2 14.9 convolution_bitcast_fusion.2
  1663.1 13.4 convolution_bitcast_fusion.1
  1684.8 28.0 %fusion.9 = bf16[2,4096,1024]{2,1,0:T(8,128)(2,1)} fusion(f32[1,4096,1024]{2,1,0:T(8,128)} %convolution_bitcast_fusion.2, f32[1,4096,1024]{2,1,0:T(8,128)} %convolution_bitcast_fusion.3, f32[1,4096,1024]{2,1,0:T(8,128)} %convolution_bitcast_fusion, f32[1,4096,1024]{2,1,0:T(8,128)} %convolution_bitcast_fusion.1), kind=kLoop, calls=%fused_computation.12 | loop fusion | flops 33554432 | bytes 83886080 | tf_op jit(solution)/shard_map/convert_element_type | solution.py:440
  1713.5 13.4 convolution_bitcast_fusion.4
  1777.3 28.5 %fusion.8 = bf16[2,1024,4096]{2,1,0:T(8,128)(2,1)} fusion(f32[1,1024,4096]{2,1,0:T(8,128)} %convolution_bitcast_fusion.6, f32[1,1024,4096]{2,1,0:T(8,128)} %convolution_bitcast_fusion.7, f32[1,1024,4096]{2,1,0:T(8,128)} %convolution_bitcast_fusion.4, f32[1,1024,4096]{2,1,0:T(8,128)} %convolution_bitcast_fusion.5), kind=kLoop, calls=%fused_computation.10 | loop fusion | flops 33554432 | bytes 83886080 | tf_op jit(solution)/shard_map/convert_element_type | solution.py:434
  1858.1 206.5 %reduce-scatter.38.cloned.1.call-done = bf16[2,1024,1024]{2,1,0:T(8,128)(2,1)} async-done(((bf16[2,4096,1024]{2,1,0:T(8,128)(2,1)}), bf16[2,1024,1024]{2,1,0:T(8,128)(2,1)}) %reduce-scatter.38.cloned.1.call-update) | async-done | bytes 4194320 | tf_op jit(solution)/shard_map/reduce_scatter | solution.py:439
  2064.6 283.3 %reduce-scatter.36.cloned.1.call-done = bf16[2,256,4096]{2,1,0:T(8,128)(2,1)} async-done(((bf16[2,1024,4096]{2,1,0:T(8,128)(2,1)}), bf16[2,256,4096]{2,1,0:T(8,128)(2,1)}) %reduce-scatter.36.cloned.1.call-update) | async-done | bytes 4194320 | tf_op jit(solution)/shard_map/reduce_scatter | solution.py:433
  2357.7 13.5 reduce-scatter.54.cloned.1.call-done
  2372.1 19.2 reduce-scatter.56.cloned.1.call-done
  2392.2 27.6 %reduce-scatter.52.cloned.1.call-done = bf16[1024,2]{1,0:T(8,128)(2,1)} async-done(((bf16[4096,2]{1,0:T(8,128)(2,1)}), bf16[1024,2]{1,0:T(8,128)(2,1)}) %reduce-scatter.52.cloned.1.call-update) | async-done | bytes 4112
  2420.8 18.6 reduce-scatter.44.cloned.1.call-done
  2439.4 19.5 reduce-scatter.48.cloned.1.call-done
  2458.9 19.8 reduce-scatter.34.cloned.1.call-done
  2478.7 19.8 reduce-scatter.32.cloned.1.call-done
  2498.6 27.1 %all-reduce.130 = (bf16[6,256]{1,0:T(8,128)(2,1)S(1)}, bf16[6,256]{1,0:T(8,128)(2,1)S(1)}, bf16[2,1024]{1,0:T(2,128)(2,1)S(1)}, bf16[2,256]{1,0:T(2,128)(2,1)S(1...) all-reduce(bf16[6,256]{1,0:T(8,128)(2,1)} %reduce-scatter.32.cloned, ...), channel_id=1, replica_groups=mesh['rep'=4,'fsdp'=4,'seq'=2] {'rep','seq'}, use_global_device_ids=true, to_apply=%region_71.72 | all-reduce | flops 15504 | bytes 62016 | tf_op jit(solution)/shard_map/psum | solution.py:468
  2529.9 141.2 %all-reduce.134.cloned.1.call-done = (bf16[2,256,4096]{2,1,0:T(8,128)(2,1)}, bf16[2,1024,1024]{2,1,0:T(8,128)(2,1)}, bf16[256,3072]{1,0:T(8,128)(2,1)}, bf16[256...) async-done(((bf16[2,256,4096]{2,1,0:T(8,128)(2,1)}, bf16[2,1024,1024]{2,1,0:T(8,128)(2,1)}, bf16[256,3072]{1,0:T(8,128)(2,1)}, ...) | async-done | bytes 12058640 | tf_op jit(solution)/shard_map/psum | solution.py:468
  (948 shorter events, 591.4 us)
Async XLA Ops:
  7.2 292.7 %all-gather.11.cloned.1.call-start = ((), (), s32[]{:S(2)}) async-start(), calls=%async_computation.17 | async-start | bytes 20971520 | tf_op jit(solution)/shard_map/all_gather | solution.py:51
  8.0 578.5 %all-gather.13.cloned.1.call-start = ((), (), s32[]{:S(2)}) async-start(), calls=%async_computation.18 | async-start | bytes 20971520 | tf_op jit(solution)/shard_map/all_gather | solution.py:53
  8.7 692.9 %all-gather.15.cloned.1.call-start = ((), (), s32[]{:S(2)}) async-start(), calls=%async_computation.19 | async-start | bytes 7864320 | tf_op jit(solution)/shard_map/all_gather | solution.py:55
  9.5 837.5 %all-gather.29.cloned.1.call-start = ((), (), s32[]{:S(2)}) async-start(), calls=%async_computation.26 | async-start | bytes 3145728 | tf_op jit(solution)/shard_map/all_gather | solution.py:126
  99.4 211.1 %copy-start.155 = (f32[512]{0:T(512)}, f32[512]{0:T(512)S(1)}, u32[]{:S(2)}) copy-start(f32[512]{0:T(512)S(1)} %broadcast_multiply_fusion.67) | copy-start | bytes 6148
  99.4 613.2 %copy-start.157 = (f32[512]{0:T(512)}, f32[512]{0:T(512)S(1)}, u32[]{:S(2)}) copy-start(f32[512]{0:T(512)S(1)} %broadcast_multiply_fusion.73) | copy-start | bytes 6148
  100.1 612.4 %copy-start.159 = (f32[512]{0:T(512)}, f32[512]{0:T(512)S(1)}, u32[]{:S(2)}) copy-start(f32[512]{0:T(512)S(1)} %fusion.215) | copy-start | bytes 6148
  100.1 210.3 %copy-start.161 = (f32[512]{0:T(512)}, f32[512]{0:T(512)S(1)}, u32[]{:S(2)}) copy-start(f32[512]{0:T(512)S(1)} %fusion.221) | copy-start | bytes 6148
  102.0 610.6 %copy-start.151 = (f32[1,1024]{1,0:T(1,128)}, f32[1,1024]{1,0:T(1,128)S(1)}, u32[]{:S(2)}) copy-start(f32[1,1024]{1,0:T(1,128)S(1)} %get-tuple-element.300) | copy-start | bytes 12292
  102.0 630.2 %copy-start.242 = (f32[1,1024]{1,0:T(1,128)}, f32[1,1024]{1,0:T(1,128)S(1)}, u32[]{:S(2)}) copy-start(f32[1,1024]{1,0:T(1,128)S(1)} %get-tuple-element.299) | copy-start | bytes 12292
  102.6 610.0 %copy-start.299 = (f32[1,1024]{1,0:T(1,128)}, f32[1,1024]{1,0:T(1,128)S(1)}, u32[]{:S(2)}) copy-start(f32[1,1024]{1,0:T(1,128)S(1)} %get-tuple-element.306) | copy-start | bytes 12292
  102.6 629.6 %copy-start.303 = (f32[1,1024]{1,0:T(1,128)}, f32[1,1024]{1,0:T(1,128)S(1)}, u32[]{:S(2)}) copy-start(f32[1,1024]{1,0:T(1,128)S(1)} %get-tuple-element.305) | copy-start | bytes 12292
  103.2 616.5 %copy-start.251 = (f32[1,4096]{1,0:T(1,128)}, f32[1,4096]{1,0:T(1,128)S(1)}, u32[]{:S(2)}) copy-start(f32[1,4096]{1,0:T(1,128)S(1)} %get-tuple-element.308) | copy-start | bytes 49156
  597.0 111.1 %copy-start.163 = (f32[512]{0:T(512)}, f32[512]{0:T(512)S(1)}, u32[]{:S(2)}) copy-start(f32[512]{0:T(512)S(1)} %broadcast_multiply_fusion.66) | copy-start | bytes 6148
  599.2 108.8 %copy-start.256 = (f32[512]{0:T(512)}, f32[512]{0:T(512)S(1)}, u32[]{:S(2)}) copy-start(f32[512]{0:T(512)S(1)} %fusion.222) | copy-start | bytes 6148
  712.0 189.2 %all-gather.27.cloned.1.call-start = ((), (), s32[]{:S(2)}) async-start(), calls=%async_computation.25 | async-start | bytes 3145728 | tf_op jit(solution)/shard_map/all_gather | solution.py:127
  741.9 177.9 %all-gather.21.cloned.1.call-start = ((), (), s32[]{:S(2)}) async-start(), calls=%async_computation.22 | async-start | bytes 2621440 | tf_op jit(solution)/shard_map/all_gather | solution.py:56
  742.5 182.5 %all-gather.23.cloned.1.call-start = ((), (), s32[]{:S(2)}) async-start(), calls=%async_computation.23 | async-start | bytes 5242880 | tf_op jit(solution)/shard_map/all_gather | solution.py:59
  743.2 197.6 %all-gather.19.cloned.1.call-start = ((), (), s32[]{:S(2)}) async-start(), calls=%async_computation.21 | async-start | bytes 3145728 | tf_op jit(solution)/shard_map/all_gather | solution.py:126
  746.0 248.0 %all-gather.17.cloned.1.call-start = ((), (), s32[]{:S(2)}) async-start(), calls=%async_computation.20 | async-start | bytes 3145728 | tf_op jit(solution)/shard_map/all_gather | solution.py:127
  746.8 288.6 %all-gather.25.cloned.1.call-start = ((), (), s32[]{:S(2)}) async-start(), calls=%async_computation.24 | async-start | bytes 2621440 | tf_op jit(solution)/shard_map/all_gather | solution.py:61
  747.4 857.8 %reduce-scatter.24.cloned.1.call-start = ((), (), s32[]{:S(2)}) async-start(), calls=%async_computation.27 | async-start | bytes 3145728 | tf_op jit(solution)/shard_map/reduce_scatter | solution.py:175
  782.7 161.2 %copy-start.12 = (bf16[1,512,1024]{1,2,0:T(8,128)(2,1)}, bf16[1,512,1024]{1,2,0:T(8,128)(2,1)S(1)}, u32[]{:S(2)}) copy-start(bf16[1,512,1024]{1,2,0:T(8,128)(2,1)S(1)} %copy.79) | copy-start | bytes 3145732
  932.6 91.8 %collective-permute-start.1 = (bf16[1,30,1024]{2,1,0:T(8,128)(2,1)S(1)}, bf16[1,30,1024]{2,1,0:T(8,128)(2,1)S(1)}, u32[]{:S(2)}, u32[]{:S(2)}) collective-permute-start(bf16[1,30,1024]{2,1,0:T(8,128)(2,1)S(1)} %slice.706), channel_id=1, source_target_pairs={{0,1},{2,3},{4,5},{6,7},{8,9},{10,11},{12,13},{14,15},{16,17},{18,... | collective-permute-start | bytes 184328 | tf_op jit(solution)/shard_map/ppermute | solution.py:21
  1020.8 38.3 %collective-permute-start = (bf16[1,30,1024]{2,1,0:T(8,128)(2,1)S(1)}, bf16[1,30,1024]{2,1,0:T(8,128)(2,1)S(1)}, u32[]{:S(2)}, u32[]{:S(2)}) collective-permute-start(bf16[1,30,1024]{2,1,0:T(8,128)(2,1)S(1)} %slice.629), channel_id=1, source_target_pairs={{0,1},{2,3},{4,5},{6,7},{8,9},{10,11},{12,13},{14,15},{16,17},{18,... | collective-permute-start | bytes 184328 | tf_op jit(solution)/shard_map/ppermute | solution.py:21
  1039.5 109.5 %copy-start.68 = (f32[512,1024]{1,0:T(8,128)}, f32[512,1024]{1,0:T(8,128)S(1)}, u32[]{:S(2)}) copy-start(f32[512,1024]{1,0:T(8,128)S(1)} %get-tuple-element.353) | copy-start | bytes 6291460
  1039.6 109.5 %copy-start.167 = (f32[512]{0:T(512)}, f32[512]{0:T(512)S(1)}, u32[]{:S(2)}) copy-start(f32[512]{0:T(512)S(1)} %broadcast_multiply_fusion.63) | copy-start | bytes 6148
  1040.0 109.1 %copy-start.260 = (f32[512]{0:T(512)}, f32[512]{0:T(512)S(1)}, u32[]{:S(2)}) copy-start(f32[512]{0:T(512)S(1)} %fusion.225) | copy-start | bytes 6148
  1059.5 104.4 %copy-start.3 = (f32[1,542,1024]{2,1,0:T(8,128)}, f32[1,542,1024]{2,1,0:T(8,128)S(1)}, u32[]{:S(2)}) copy-start(f32[1,542,1024]{2,1,0:T(8,128)S(1)} %maximum_convert_fusion) | copy-start | bytes 6660100
  1238.4 22.8 collective-permute-start.2
  1259.9 6.2 collective-permute-start.3
  1345.1 260.0 %reduce-scatter.26.cloned.1.call-start = ((), (), s32[]{:S(2)}) async-start(), calls=%async_computation.28 | async-start | bytes 3145728 | tf_op jit(solution)/shard_map/reduce_scatter | solution.py:181
  1367.8 248.9 %reduce-scatter.28.cloned.1.call-start = ((), (), s32[]{:S(2)}) async-start(), calls=%async_computation.29 | async-start | bytes 3145728 | tf_op jit(solution)/shard_map/reduce_scatter | solution.py:175
  1430.3 186.4 %reduce-scatter.30.cloned.1.call-start = ((), (), s32[]{:S(2)}) async-start(), calls=%async_computation.30 | async-start | bytes 3145728 | tf_op jit(solution)/shard_map/reduce_scatter | solution.py:181
  1446.0 412.0 %reduce-scatter.50.cloned.1.call-start = ((), (), s32[]{:S(2)}) async-start(), calls=%async_computation.40 | async-start | bytes 2621440 | tf_op jit(solution)/shard_map/reduce_scatter | solution.py:463
  1453.6 404.4 %reduce-scatter.42.cloned.1.call-start = ((), (), s32[]{:S(2)}) async-start(), calls=%async_computation.36 | async-start | bytes 2621440 | tf_op jit(solution)/shard_map/reduce_scatter | solution.py:448
  1473.7 384.3 %reduce-scatter.46.cloned.1.call-start = ((), (), s32[]{:S(2)}) async-start(), calls=%async_computation.38 | async-start | bytes 5242880 | tf_op jit(solution)/shard_map/reduce_scatter | solution.py:457
  1527.6 330.4 %reduce-scatter.40.cloned.1.call-start = ((), (), s32[]{:S(2)}) async-start(), calls=%async_computation.35 | async-start | bytes 7864320 | tf_op jit(solution)/shard_map/reduce_scatter | solution.py:445
  1628.6 436.0 %reduce-scatter.38.cloned.1.call-start = ((), (), s32[]{:S(2)}) async-start(), calls=%async_computation.34 | async-start | bytes 20971520 | tf_op jit(solution)/shard_map/reduce_scatter | solution.py:439
  1712.9 635.0 %reduce-scatter.36.cloned.1.call-start = ((), (), s32[]{:S(2)}) async-start(), calls=%async_computation.33 | async-start | bytes 20971520 | tf_op jit(solution)/shard_map/reduce_scatter | solution.py:433
  1805.8 565.4 %reduce-scatter.54.cloned.1.call-start = ((), (), s32[]{:S(2)}) async-start(), calls=%async_computation.42 | async-start | bytes 327680
  1823.2 568.0 %reduce-scatter.56.cloned.1.call-start = ((), (), s32[]{:S(2)}) async-start(), calls=%async_computation.43 | async-start | bytes 327680
  1826.8 593.0 %reduce-scatter.52.cloned.1.call-start = ((), (), s32[]{:S(2)}) async-start(), calls=%async_computation.41 | async-start | bytes 1310720
  1829.4 610.0 %reduce-scatter.44.cloned.1.call-start = ((), (), s32[]{:S(2)}) async-start(), calls=%async_computation.37 | async-start | bytes 20480 | tf_op jit(solution)/shard_map/reduce_scatter | solution.py:454
  1830.6 628.3 %reduce-scatter.48.cloned.1.call-start = ((), (), s32[]{:S(2)}) async-start(), calls=%async_computation.39 | async-start | bytes 81920 | tf_op jit(solution)/shard_map/reduce_scatter | solution.py:460
  1832.9 645.8 %reduce-scatter.34.cloned.1.call-start = ((), (), s32[]{:S(2)}) async-start(), calls=%async_computation.32 | async-start | bytes 20480 | tf_op jit(solution)/shard_map/reduce_scatter | solution.py:430
  1853.3 645.3 %reduce-scatter.32.cloned.1.call-start = ((), (), s32[]{:S(2)}) async-start(), calls=%async_computation.31 | async-start | bytes 20480 | tf_op jit(solution)/shard_map/reduce_scatter | solution.py:427
  1857.9 813.2 %all-reduce.134.cloned.1.call-start = ((), (), s32[]{:S(2)}) async-start(), calls=%async_computation.44 | async-start | bytes 24117248 | tf_op jit(solution)/shard_map/psum | solution.py:468
  (314 other events, 2931.0 us)
Sparse Core Ops, SparseCore 0:
  9.6 290.2 all-gather.10
  301.4 285.0 all-gather.12
  588.1 113.5 all-gather.14
  712.1 31.3 all-gather.28
  745.4 33.1 all-gather.26
  780.0 45.9 all-gather.20
  827.6 79.4 all-gather.22
  909.2 31.6 all-gather.18
  943.0 34.4 all-gather.16
  979.0 45.9 all-gather.24
  1345.2 33.6 reduce-scatter.23
  1381.1 31.8 reduce-scatter.25
  1430.4 33.3 reduce-scatter.27
  1466.0 31.8 reduce-scatter.29
  1500.1 43.8 reduce-scatter.49
  1546.2 43.1 reduce-scatter.41
  1591.6 76.0 reduce-scatter.45
  1669.9 111.2 reduce-scatter.39
  1783.7 280.8 reduce-scatter.37
  2066.8 281.0 reduce-scatter.35
  2350.8 20.3 reduce-scatter.53
  2373.4 17.7 reduce-scatter.55
  2394.2 25.4 reduce-scatter.51
  2421.8 17.5 reduce-scatter.43
  2441.8 17.1 reduce-scatter.47
  2461.6 17.0 reduce-scatter.33
  2481.5 17.0 reduce-scatter.31
  2503.2 167.8 all-reduce.133
where the time goes:
time: 2700 us
  waiting for transfers between devices  1360 us (50%)
  matrix products  738 us (27%)
  other arithmetic  343 us (13%)
  blocking collectives  143 us (5%)
  local copies, waits for them, and re-layouts  81.7 us (3%)
    reduce_scatter x1, waiting for transfers between devices, body(): lax.psum_scatter(totals[2].astype(jnp.bfloat16), 'fsdp', scatter_dimensio...  283 us
    all_gather x1, waiting for transfers between devices, fetch(): lax.all_gather(shards[4], 'fsdp', axis=1, tiled=True)  276 us
    reduce_scatter x1, waiting for transfers between devices, body(): lax.psum_scatter(totals[4].astype(jnp.bfloat16), 'fsdp', scatter_dimensio...  207 us
    all_gather x1, waiting for transfers between devices, fetch(): lax.all_gather(shards[2], 'fsdp', axis=1, tiled=True)  197 us
    psum x1, waiting for transfers between devices, body(): lax.psum(as_sent(totals), ('rep', 'seq'))  141 us
    dot_general x16, matrix products, left_t(): lax.dot_general(left, right, (((0,), (0,)), ((), ())), preferred_element_...  135 us
    dot_general x16, matrix products, right_t(): lax.dot_general(left, right, (((1,), (1,)), ((), ())), preferred_element_...  120 us
    dot_general x16, matrix products, matmul(): return jnp.dot(left, right, preferred_element_type=HIGH)  112 us
  transfers between devices with their start and end apart: 32, of which 15 were waited for; matrix products, arithmetic and copies ran while one was open for 32% of the time, Pallas kernels for 0%

commit v1 on v0

--- a/solution.py
+++ b/solution.py
@@ -1,6 +1,10 @@
+import functools
+
 import jax
 import jax.numpy as jnp
 from jax import lax
+from jax.experimental import pallas as pl
+from jax.experimental.pallas import tpu as pltpu
 from jax.sharding import PartitionSpec as P
 
 H = 16
@@ -253,7 +257,7 @@
     )
 
 
-def body(
+def general_body(
     inputs,
     cotangent,
     ln_gain,
@@ -486,6 +490,770 @@
     )
 
 
+SUB = 128
+PAD = 128
+FWD_ROWS = 512
+BWD_ROWS = 1024
+
+
+def dot(a, b):
+    return lax.dot_general(a, b, (((1,), (0,)), ((), ())), preferred_element_type=HIGH)
+
+
+def dot_nt(a, b):
+    return lax.dot_general(a, b, (((1,), (1,)), ((), ())), preferred_element_type=HIGH)
+
+
+def biased_scores(qs, table, kcat, s_ref, first, span):
+    count = qs.shape[0]
+    rel = dot_nt(qs, table).astype(LOW).astype(HIGH)
+    lane = lax.broadcasted_iota(jnp.int32, (count, 128), 1)
+    block = first + lax.broadcasted_iota(jnp.int32, (count, 128), 0) // SUB
+    far = jnp.where(lane < block - 1, rel[:, 384:512], jnp.where(lane > block + 1, rel[:, 128:256], 0.0))
+    s_ref[:, PAD : PAD + span] = dot_nt(jnp.concatenate([qs, far.astype(LOW)], axis=1), kcat)
+    for sub in range(count // SUB):
+        rows = slice(sub * SUB, (sub + 1) * SUB)
+        band = pltpu.roll(rel[rows], LEFT, 1, stride=1, stride_axis=0)
+        at = pl.multiple_of((first + sub) * SUB, 128)
+        s_ref[rows, pl.ds(at, 384)] += band[:, :384]
+
+
+def blocks_onehot(span):
+    row = lax.broadcasted_iota(jnp.int32, (span, 128), 0)
+    lane = lax.broadcasted_iota(jnp.int32, (span, 128), 1)
+    return (row // SUB == lane).astype(HIGH).astype(LOW)
+
+
+def attn_fwd_kernel(q_ref, k_ref, v_ref, table_ref, o_ref, lse_ref, kcat, vcat, s_ref):
+    span = k_ref.shape[0]
+    kcat[:, :128] = k_ref[...]
+    kcat[:, 128:] = blocks_onehot(span)
+    vcat[:, :128] = v_ref[...]
+    vcat[:, 128:] = jnp.ones((span, 128), LOW)
+    lane = lax.broadcasted_iota(jnp.int32, (FWD_ROWS, 128), 1)
+
+    def body(qb, carry):
+        rows = pl.ds(pl.multiple_of(qb * FWD_ROWS, FWD_ROWS), FWD_ROWS)
+        q = q_ref[rows, :].astype(HIGH) * (HD**-0.5)
+        outs, logs = [], []
+        for h in range(2):
+            mine = (lane < HD) if h == 0 else (lane >= HD)
+            qs = jnp.where(mine, q, 0.0).astype(LOW)
+            sr = s_ref.at[h]
+            biased_scores(qs, table_ref[...], kcat[...], sr, qb * (FWD_ROWS // SUB), span)
+        for h in range(2):
+            s = s_ref[h, :, PAD : PAD + span]
+            top = jnp.max(s, axis=-1, keepdims=True)
+            p = jnp.exp(s - top).astype(LOW)
+            mixed = dot(p, vcat[...])
+            total = mixed[:, 128:]
+            outs.append(mixed[:, :128] / total)
+            logs.append(top + jnp.log(total))
+        o_ref[rows, :] = jnp.where(lane < HD, outs[0], outs[1]).astype(o_ref.dtype)
+        lse_ref[rows, :] = jnp.where(lane < HD, logs[0], logs[1])
+        return carry
+
+    lax.fori_loop(0, q_ref.shape[0] // FWD_ROWS, body, 0)
+
+
+def attn_forward_call(proj, table, width):
+    rows = proj.shape[0]
+    pairs = width // 128
+    col = lambda off: pl.BlockSpec((rows, 128), lambda h: (0, off * pairs + h))
+    return pl.pallas_call(
+        attn_fwd_kernel,
+        grid=(pairs,),
+        in_specs=[col(0), col(1), col(2), pl.BlockSpec((512, 128), lambda h: (0, 0))],
+        out_specs=[pl.BlockSpec((rows, 128), lambda h: (0, h))] * 2,
+        out_shape=[jax.ShapeDtypeStruct((rows, width), LOW), jax.ShapeDtypeStruct((rows, width), HIGH)],
+        scratch_shapes=[
+            pltpu.VMEM((rows, 256), LOW),
+            pltpu.VMEM((rows, 256), LOW),
+            pltpu.VMEM((2, FWD_ROWS, rows + 2 * PAD), HIGH),
+        ],
+        compiler_params=pltpu.CompilerParams(vmem_limit_bytes=40 * 1024 * 1024),
+        cost_estimate=pl.CostEstimate(
+            flops=16 * rows * rows * width, bytes_accessed=12 * rows * width, transcendentals=rows * rows * 16
+        ),
+    )(proj, proj, proj, table)
+
+
+def attn_bwd_kernel(q_ref, k_ref, v_ref, o_ref, lse_ref, do_ref, table_ref, embed_ref,
+                    g_ref, dembed_ref, bias_ref, kcat, qt, dot_t, dkt, dvt, s_ref):
+    span = k_ref.shape[0]
+    count = BWD_ROWS
+    kcat[:, :128] = k_ref[...]
+    kcat[:, 128:] = blocks_onehot(span)
+    qt[...] = (q_ref[...].astype(HIGH) * (HD**-0.5)).T.astype(LOW)
+    dot_t[...] = do_ref[...].astype(HIGH).T.astype(LOW)
+    dkt[...] = jnp.zeros_like(dkt)
+    dvt[...] = jnp.zeros_like(dvt)
+    lane = lax.broadcasted_iota(jnp.int32, (count, 128), 1)
+    block_of = lax.broadcasted_iota(jnp.int32, (count, 128), 0) // SUB
+    column = lax.broadcasted_iota(jnp.int32, (SUB, 384), 1)
+    last = q_ref.shape[0] // SUB - 1
+    turn = lax.broadcasted_iota(jnp.int32, (SUB, SUB), 0) + lax.broadcasted_iota(jnp.int32, (SUB, SUB), 1)
+    flip = (turn == SUB - 1).astype(HIGH).astype(LOW)
+    lane_sub = lax.broadcasted_iota(jnp.int32, (SUB, 128), 1)
+    edge = LEFT + RIGHT
+
+    def body(qb, carry):
+        dembed, dbias = carry
+        first = qb * (count // SUB)
+        rows = pl.ds(pl.multiple_of(qb * count, count), count)
+        q = q_ref[rows, :].astype(HIGH) * (HD**-0.5)
+        grad = do_ref[rows, :].astype(HIGH)
+        lse2 = lse_ref[rows, :]
+        weighted = grad * o_ref[rows, :].astype(HIGH)
+        block = first + block_of
+        dqs, news = [], []
+        for h in range(2):
+            mine = (lane < HD) if h == 0 else (lane >= HD)
+            qs = jnp.where(mine, q, 0.0).astype(LOW)
+            biased_scores(qs, table_ref[...], kcat[...], s_ref.at[h], first, span)
+        for h in range(2):
+            mine = (lane < HD) if h == 0 else (lane >= HD)
+            part = slice(h * HD, (h + 1) * HD)
+            sr = s_ref.at[h]
+            lse = lse2[:, h * HD : h * HD + 1]
+            p = jnp.exp(sr[:, PAD : PAD + span] - lse)
+            delta = jnp.sum(jnp.where(mine, weighted, 0.0), axis=-1, keepdims=True)
+            gs = jnp.where(mine, grad, 0.0).astype(LOW)
+            ds = p * (dot_nt(gs, v_ref[...]) - delta)
+            sr[:, PAD : PAD + span] = ds
+            ds_low = ds.astype(LOW)
+            dq = dot(ds_low, kcat[...])
+            dvt[part, :] += dot(dot_t[part, rows], p.astype(LOW))
+            dkt[part, :] += dot(qt[part, rows], ds_low)
+            tables = []
+            for sub in range(count // SUB):
+                band = sr[sub * SUB : (sub + 1) * SUB, pl.ds(pl.multiple_of((first + sub) * SUB, 128), 384)]
+                if sub == 0:
+                    band = jnp.where((column < 128) & (first == 0), 0.0, band)
+                if sub == count // SUB - 1:
+                    band = jnp.where((column >= 256) & (first + sub == last), 0.0, band)
+                turned = dot(flip, band.astype(LOW))
+                turned = jnp.concatenate([turned, jnp.zeros((SUB, 128), HIGH)], axis=1)
+                drel = pltpu.roll(turned, 512 - LEFT - SUB + 1, 1, stride=1, stride_axis=0)
+                near, middle = drel[:, :128], drel[:, 256:384]
+                left = jnp.sum(drel[:, 384:512] + jnp.where(lane_sub >= 64, middle, 0.0), axis=-1, keepdims=True)
+                right = jnp.sum(
+                    drel[:, 128:256] + jnp.where(lane_sub < 64, middle, 0.0) + jnp.where(lane_sub >= edge, near, 0.0),
+                    axis=-1,
+                    keepdims=True,
+                )
+                left_top, right_top = left.astype(LOW).astype(HIGH), right.astype(LOW).astype(HIGH)
+                packed = jnp.where(lane_sub < edge, near, 0.0)
+                for at, value in ((80, left_top), (81, left - left_top), (82, right_top), (83, right - right_top)):
+                    packed = jnp.where(lane_sub == at, value, packed)
+                tables.append(dot(flip, packed.astype(LOW)))
+            table = jnp.concatenate(tables, axis=0)
+            sums = dq[:, 128:]
+            left = jnp.sum(jnp.where(lane < block - 1, sums, 0.0) + jnp.where((lane == 80) | (lane == 81), table, 0.0), axis=-1, keepdims=True)
+            right = jnp.sum(jnp.where(lane > block + 1, sums, 0.0) + jnp.where((lane == 82) | (lane == 83), table, 0.0), axis=-1, keepdims=True)
+            drl = jnp.where(lane < edge, table, 0.0) + jnp.where(lane == 0, left, 0.0) + jnp.where(lane == edge, right, 0.0)
+            drl = drl.astype(LOW)
+            dqs.append((dq[:, :128] + dot(drl, embed_ref[...])) * (HD**-0.5))
+            news.append(dembed[part] + dot(qt[part, rows], drl))
+        dq = jnp.where(lane < HD, dqs[0], dqs[1])
+        g_ref[0, rows, :] = dq.astype(LOW)
+        return (jnp.concatenate(news, axis=0), dbias + jnp.sum(dq, axis=0, keepdims=True))
+
+    start = (jnp.zeros((128, 128), HIGH), jnp.zeros((1, 128), HIGH))
+    dembed, dbias = lax.fori_loop(0, q_ref.shape[0] // count, body, start)
+    dembed_ref[...] = dembed
+    g_ref[1, :, :] = dkt[...].T.astype(LOW)
+    dv = dvt[...].T
+    g_ref[2, :, :] = dv.astype(LOW)
+    row8 = lax.broadcasted_iota(jnp.int32, (8, 128), 0)
+    bias_ref[...] = jnp.where(row8 == 0, dbias, jnp.where(row8 == 1, jnp.sum(dv, axis=0, keepdims=True), 0.0))
+
+
+def attn_backward_call(proj, mixed, lse, grad_mixed, table, embed2, width):
+    rows = proj.shape[0]
+    pairs = width // 128
+    col = lambda off: pl.BlockSpec((rows, 128), lambda h: (0, off * pairs + h))
+    return pl.pallas_call(
+        attn_bwd_kernel,
+        grid=(pairs,),
+        in_specs=[
+            col(0), col(1), col(2), col(0), col(0), col(0),
+            pl.BlockSpec((512, 128), lambda h: (0, 0)),
+            pl.BlockSpec((128, 128), lambda h: (0, 0)),
+        ],
+        out_specs=[
+            pl.BlockSpec((3, rows, 128), lambda h: (0, 0, h)),
+            pl.BlockSpec((128, 128), lambda h: (0, h)),
+            pl.BlockSpec((8, 128), lambda h: (0, h)),
+        ],
+        out_shape=[
+            jax.ShapeDtypeStruct((3, rows, width), LOW),
+            jax.ShapeDtypeStruct((128, width), HIGH),
+            jax.ShapeDtypeStruct((8, width), HIGH),
+        ],
+        scratch_shapes=[
+            pltpu.VMEM((rows, 256), LOW),
+            pltpu.VMEM((128, rows), LOW),
+            pltpu.VMEM((128, rows), LOW),
+            pltpu.VMEM((128, rows), HIGH),
+            pltpu.VMEM((128, rows), HIGH),
+            pltpu.VMEM((2, BWD_ROWS, rows + 2 * PAD), HIGH),
+        ],
+        compiler_params=pltpu.CompilerParams(vmem_limit_bytes=48 * 1024 * 1024),
+        cost_estimate=pl.CostEstimate(
+            flops=40 * rows * rows * width, bytes_accessed=24 * rows * width, transcendentals=rows * rows * 16
+        ),
+    )(proj, proj, proj, mixed, lse, grad_mixed, table, embed2)
+
+
+def bias_tables(embed):
+    last = LEFT + RIGHT
+    tail = jnp.broadcast_to(embed[last:], (320 - last - 1, HD))
+    head = jnp.broadcast_to(embed[:1], (192, HD))
+    table = jnp.concatenate([embed, tail, head], axis=0)
+    pair = jnp.concatenate([table, table], axis=1)
+    return pair, pair[:128]
+
+
+CONV_ROWS = 64
+EDGE = 32
+
+
+def conv_fwd_kernel(u_ref, w_ref, m_ref, padded):
+    rows = u_ref.shape[0]
+    padded[:EDGE, :] = jnp.zeros((EDGE, 128), HIGH)
+    padded[EDGE:, :] = u_ref[...].astype(HIGH)
+
+    def chunk(i, carry):
+        start = pl.multiple_of(i * CONV_ROWS, CONV_ROWS)
+        total = jnp.zeros((CONV_ROWS, 128), HIGH)
+        for tap in range(KERNEL):
+            total += w_ref[tap : tap + 1, :] * padded[pl.ds(start + (EDGE - KERNEL + 1 + tap), CONV_ROWS), :]
+        m_ref[pl.ds(start, CONV_ROWS), :] = total
+        return carry
+
+    lax.fori_loop(0, rows // CONV_ROWS, chunk, 0)
+
+
+def conv_fwd_call(u, kernel):
+    rows, width = u.shape
+    return pl.pallas_call(
+        conv_fwd_kernel,
+        grid=(width // 128,),
+        in_specs=[pl.BlockSpec((rows, 128), lambda c: (0, c)), pl.BlockSpec((KERNEL, 128), lambda c: (0, c))],
+        out_specs=pl.BlockSpec((rows, 128), lambda c: (0, c)),
+        out_shape=jax.ShapeDtypeStruct((rows, width), HIGH),
+        scratch_shapes=[pltpu.VMEM((rows + EDGE, 128), HIGH)],
+        cost_estimate=pl.CostEstimate(flops=62 * rows * width, bytes_accessed=6 * rows * width, transcendentals=0),
+    )(u, kernel)
+
+
+def conv_bwd_kernel(dm_ref, u_ref, pre_a_ref, pre_b_ref, w_ref, g_ref, dw_ref, padded, acc):
+    rows = u_ref.shape[0]
+    padded[:rows, :] = dm_ref[...]
+    padded[rows:, :] = jnp.zeros((EDGE, 128), HIGH)
+    acc[...] = jnp.zeros_like(acc)
+
+    def chunk(i, carry):
+        start = pl.multiple_of(i * CONV_ROWS, CONV_ROWS)
+        at = pl.ds(start, CONV_ROWS)
+        u = u_ref[at, :].astype(HIGH)
+        total = jnp.zeros((CONV_ROWS, 128), HIGH)
+        for tap in range(KERNEL):
+            later = padded[pl.ds(start + (KERNEL - 1 - tap), CONV_ROWS), :]
+            total += w_ref[tap : tap + 1, :] * later
+            acc[tap] += jnp.sum((u * later).reshape(CONV_ROWS // 8, 8, 128), axis=0)
+        gate = jax.nn.sigmoid(pre_b_ref[at, :].astype(HIGH))
+        through = total * gate
+        g_ref[0, at, :] = through.astype(LOW)
+        g_ref[1, at, :] = (through * pre_a_ref[at, :].astype(HIGH) * (1.0 - gate)).astype(LOW)
+        return carry
+
+    lax.fori_loop(0, rows // CONV_ROWS, chunk, 0)
+    dw_ref[...] = jnp.sum(acc[...], axis=1)
+
+
+def conv_bwd_call(dm, u, pre, kernel):
+    rows, width = u.shape
+    cols = width // 128
+    block = pl.BlockSpec((rows, 128), lambda c: (0, c))
+    taps = pl.BlockSpec((KERNEL, 128), lambda c: (0, c))
+    return pl.pallas_call(
+        conv_bwd_kernel,
+        grid=(cols,),
+        in_specs=[block, block, block, pl.BlockSpec((rows, 128), lambda c: (0, cols + c)), taps],
+        out_specs=[pl.BlockSpec((2, rows, 128), lambda c: (0, 0, c)), taps],
+        out_shape=[jax.ShapeDtypeStruct((2, rows, width), LOW), jax.ShapeDtypeStruct((KERNEL, width), HIGH)],
+        scratch_shapes=[pltpu.VMEM((rows + EDGE, 128), HIGH), pltpu.VMEM((KERNEL, 8, 128), HIGH)],
+        cost_estimate=pl.CostEstimate(flops=124 * rows * width, bytes_accessed=14 * rows * width, transcendentals=rows * width),
+    )(dm, u, pre, pre, kernel)
+
+
+REPLICAS = ("rep", "seq")
+X_FLIP, CORE_FLIP = 2, 1
+
+
+def replica_index():
+    return lax.axis_index("rep") * lax.axis_size("seq") + lax.axis_index("seq")
+
+
+def hop(value, axis, flip):
+    return lax.ppermute(value, axis, [(i, i ^ flip) for i in range(lax.axis_size(axis))])
+
+
+def ring(value, axis, steps):
+    count = lax.axis_size(axis)
+    return lax.ppermute(value, axis, [(i, (i + steps) % count) for i in range(count)])
+
+
+def place():
+    rep = lax.axis_index("rep")
+    return jnp.stack([rep // 2, rep % 2, lax.axis_index("seq"), lax.axis_index("fsdp")]).astype(jnp.int32)
+
+
+def spread(first, second):
+    first_x, second_y = hop(first, "rep", X_FLIP), hop(second, "seq", 1)
+    first, second = jnp.stack([first, first_x]), jnp.stack([second, second_y])
+    first_y, second_x = hop(first, "seq", 1), hop(second, "rep", X_FLIP)
+    near = [first, first_y, second, second_x]
+    return near + [hop(value, "rep", CORE_FLIP) for value in near]
+
+
+def spread_blocks(x, core, y):
+    for other in range(2):
+        for half, moved, array in ((0, 0, 0), (0, 1, 1), (1, 0, 2), (1, 1, 3)):
+            for entry in range(2):
+                if half == 0:
+                    flip_x, flip_y = entry, moved
+                else:
+                    flip_x, flip_y = moved, entry
+                yield other * 4 + array, entry, half, x ^ flip_x, core ^ other, y ^ flip_y
+
+
+def assemble_kernel(planes, has_own, at_ref, *refs):
+    shard_ref = refs[0] if has_own else None
+    parts = refs[has_own : has_own + 8]
+    out_ref, sems = refs[has_own + 8 :]
+    x, core, y, z = (at_ref[i] for i in range(4))
+    half_rows = parts[0].shape[-2]
+    rows = 16 * half_rows
+    copies = []
+    if has_own:
+        copies.append((shard_ref, out_ref.at[pl.ds(pl.multiple_of(z * rows, rows), rows), :]))
+    for array, entry, half, bx, bc, by in spread_blocks(x, core, y):
+        for plane in range(planes):
+            base = lax.rem(z + (planes - plane), planes + 1) * rows if has_own else 0
+            row = base + (((bx * 2 + bc) * 2 + by) * 2 + half) * half_rows
+            copies.append((parts[array].at[entry, plane], out_ref.at[pl.ds(pl.multiple_of(row, half_rows), half_rows), :]))
+    started = [pltpu.make_async_copy(source, target, sems.at[i]) for i, (source, target) in enumerate(copies)]
+    for copy in started:
+        copy.start()
+    for copy in started:
+        copy.wait()
+
+
+def assemble(at, shard, parts):
+    planes, half_rows, columns = parts[0].shape[1:]
+    has_own = 0 if shard is None else 1
+    rows = 16 * half_rows * (planes + 1 if has_own else 1)
+    own = [shard] if has_own else []
+    return pl.pallas_call(
+        functools.partial(assemble_kernel, planes, has_own),
+        in_specs=[pl.BlockSpec(memory_space=pltpu.SMEM)] + [pl.BlockSpec(memory_space=pl.ANY)] * (8 + has_own),
+        out_specs=pl.BlockSpec(memory_space=pltpu.VMEM),
+        out_shape=jax.ShapeDtypeStruct((rows, columns), LOW),
+        scratch_shapes=[pltpu.SemaphoreType.DMA((16 * planes + has_own,))],
+        compiler_params=pltpu.CompilerParams(vmem_limit_bytes=12 * 1024 * 1024),
+        cost_estimate=pl.CostEstimate(flops=0, bytes_accessed=4 * rows * columns, transcendentals=0),
+    )(at, *own, *parts)
+
+
+def gather_by_hops(at, shard):
+    pieces = lax.axis_size("rep") * lax.axis_size("seq")
+    count = shard.shape[0] // pieces
+    mine = lax.dynamic_slice_in_dim(shard, replica_index() * count, count, 0)
+    got = [ring(mine, "fsdp", steps) for steps in range(1, lax.axis_size("fsdp"))]
+    half = count // 2
+    first, second = jnp.stack([g[:half] for g in got]), jnp.stack([g[half:] for g in got])
+    return assemble(at, shard, spread(first, second))
+
+
+def plus(a, b):
+    return (a.astype(HIGH) + b.astype(HIGH)).astype(LOW)
+
+
+def pick(value, index, axis):
+    return lax.dynamic_index_in_dim(value, index, axis, keepdims=False)
+
+
+def reduce_by_hops(at, grad):
+    x, core, y, z = (at[i] for i in range(4))
+    groups = lax.axis_size("fsdp")
+    rows, columns = grad.shape
+    parts = grad.reshape(groups, 2, 2, 2, 2, rows // (16 * groups), columns)
+    total = plus(pick(parts, core, 2), hop(pick(parts, 1 - core, 2), "rep", CORE_FLIP))
+    first, second = total[:, :, :, 0], total[:, :, :, 1]
+    first = plus(pick(first, x, 1), hop(pick(first, 1 - x, 1), "rep", X_FLIP))
+    second = plus(pick(second, y, 2), hop(pick(second, 1 - y, 2), "seq", 1))
+    first = plus(pick(first, y, 1), hop(pick(first, 1 - y, 1), "seq", 1))
+    second = plus(pick(second, x, 1), hop(pick(second, 1 - x, 1), "rep", X_FLIP))
+    both = jnp.stack([first, second], axis=1)
+    total = pick(both, z, 0).astype(HIGH)
+    for steps in range(1, groups):
+        total = total + ring(pick(both, (z + steps) % groups, 0), "fsdp", steps).astype(HIGH)
+    total = total.astype(LOW)[:, None]
+    return assemble(at, None, spread(total[0], total[1]))
+
+
+NORM_ROWS = 256
+
+
+def normed_of(values, gain, shift):
+    mean = jnp.mean(values, axis=-1, keepdims=True)
+    centred = values - mean
+    rstd = lax.rsqrt(jnp.mean(centred * centred, axis=-1, keepdims=True) + EPS)
+    unit = centred * rstd
+    return unit, rstd, unit * gain + shift
+
+
+def norm_fwd_kernel(active, x_ref, gain_ref, shift_ref, out_ref):
+    _, _, out = normed_of(x_ref[...].astype(HIGH), gain_ref[...], shift_ref[...])
+    out_ref[...] = (jax.nn.silu(out) if active else out).astype(LOW)
+
+
+def norm_fwd(values, gain, shift, active=False):
+    rows, width = values.shape
+    block = pl.BlockSpec((NORM_ROWS, width), lambda i: (i, 0))
+    line = pl.BlockSpec((1, width), lambda i: (0, 0))
+    return pl.pallas_call(
+        functools.partial(norm_fwd_kernel, active),
+        grid=(rows // NORM_ROWS,),
+        in_specs=[block, line, line],
+        out_specs=block,
+        out_shape=jax.ShapeDtypeStruct((rows, width), LOW),
+        cost_estimate=pl.CostEstimate(flops=10 * rows * width, bytes_accessed=6 * rows * width, transcendentals=0),
+    )(values, gain[None], shift[None])
+
+
+def norm_bwd_kernel(active, has_rest, scale, x_ref, grad_ref, gain_ref, shift_ref, *refs):
+    rest_ref = refs[0] if has_rest else None
+    out_ref, low_ref, sums_ref = refs[has_rest:]
+    unit, rstd, out = normed_of(x_ref[...].astype(HIGH), gain_ref[...], shift_ref[...])
+    grad = grad_ref[...].astype(HIGH)
+    if active:
+        gate = jax.nn.sigmoid(out)
+        grad = grad * (gate * (1.0 + out * (1.0 - gate)))
+    inner = grad * gain_ref[...]
+    back = (inner - jnp.mean(inner, axis=-1, keepdims=True) - unit * jnp.mean(inner * unit, axis=-1, keepdims=True)) * rstd
+    if has_rest:
+        back = back + rest_ref[...]
+    out_ref[...] = back
+    scaled = back * scale
+    low_ref[...] = scaled.astype(LOW)
+
+    @pl.when(pl.program_id(0) == 0)
+    def _():
+        sums_ref[...] = jnp.zeros_like(sums_ref)
+
+    sums_ref[0:1, :] += jnp.sum(grad * unit, axis=0, keepdims=True)
+    sums_ref[1:2, :] += jnp.sum(grad, axis=0, keepdims=True)
+    sums_ref[2:3, :] += jnp.sum(scaled, axis=0, keepdims=True)
+
+
+def norm_bwd(values, grad, gain, shift, rest=None, scale=1.0, active=False):
+    rows, width = values.shape
+    block = pl.BlockSpec((NORM_ROWS, width), lambda i: (i, 0))
+    line = pl.BlockSpec((1, width), lambda i: (0, 0))
+    extra = [] if rest is None else [rest]
+    return pl.pallas_call(
+        functools.partial(norm_bwd_kernel, active, len(extra), scale),
+        grid=(rows // NORM_ROWS,),
+        in_specs=[block, block, line, line] + [block] * len(extra),
+        out_specs=[block, block, pl.BlockSpec((8, width), lambda i: (0, 0))],
+        out_shape=[
+            jax.ShapeDtypeStruct((rows, width), HIGH),
+            jax.ShapeDtypeStruct((rows, width), LOW),
+            jax.ShapeDtypeStruct((8, width), HIGH),
+        ],
+        compiler_params=pltpu.CompilerParams(vmem_limit_bytes=32 * 1024 * 1024),
+        cost_estimate=pl.CostEstimate(flops=30 * rows * width, bytes_accessed=18 * rows * width, transcendentals=0),
+    )(values, grad, gain[None], shift[None], *extra)
+
+
+def weight_grads_kernel(many, g_ref, last_ref, a_ref, b_ref, out_ref):
+    step = pl.program_id(0)
+
+    @pl.when(step < many)
+    def _():
+        out_ref[...] = left_t(g_ref[...], a_ref[...]).astype(LOW)
+
+    @pl.when(step == many)
+    def _():
+        out_ref[...] = left_t(last_ref[...], b_ref[...]).astype(LOW)
+
+
+def weight_grads(grads, last, first_in, last_in):
+    many, rows, width = grads.shape
+    full = pl.BlockSpec((rows, width), lambda i: (0, 0))
+    return pl.pallas_call(
+        functools.partial(weight_grads_kernel, many),
+        grid=(many + 1,),
+        in_specs=[pl.BlockSpec((None, rows, width), lambda i: (jnp.minimum(i, many - 1), 0, 0)), full, full, full],
+        out_specs=pl.BlockSpec((width, width), lambda i: (i, 0)),
+        out_shape=jax.ShapeDtypeStruct(((many + 1) * width, width), LOW),
+        compiler_params=pltpu.CompilerParams(vmem_limit_bytes=40 * 1024 * 1024),
+        cost_estimate=pl.CostEstimate(
+            flops=2 * (many + 1) * rows * width * width, bytes_accessed=4 * (many + 2) * rows * width, transcendentals=0
+        ),
+    )(grads, last, first_in, last_in)
+
+
+def gather_weight(shard):
+    pieces = lax.axis_size("rep") * lax.axis_size("seq")
+    count = shard.shape[0] // pieces
+    piece = lax.dynamic_slice_in_dim(shard, replica_index() * count, count, 0)
+    return lax.all_gather(piece, ("fsdp",) + REPLICAS, axis=0, tiled=True)
+
+
+def reduce_replicas(grad_t):
+    return lax.psum_scatter(grad_t, REPLICAS, scatter_dimension=0, tiled=True)
+
+
+def reduce_groups(part):
+    groups = lax.axis_size("fsdp")
+    columns, rows = part.shape
+    part = jnp.swapaxes(part.reshape(columns, groups, rows // groups), 0, 1)
+    part = lax.psum_scatter(part, "fsdp", scatter_dimension=0, tiled=False)
+    return lax.all_gather(part, REPLICAS, axis=0, tiled=True)
+
+
+def reduce_weight(grad_t):
+    return reduce_groups(reduce_replicas(grad_t))
+
+
+def as_grad(grad_t):
+    return grad_t.astype(HIGH).T
+
+
+def swap_in(value):
+    count = value.shape[0]
+    rows = value.shape[1]
+    me = lax.axis_index("seq")
+    whole = jnp.zeros((count * rows,) + value.shape[2:], value.dtype)
+    own = lax.dynamic_index_in_dim(value, me, 0, keepdims=False)
+    whole = lax.dynamic_update_slice_in_dim(whole, own, me * rows, 0)
+    for steps in range(1, count):
+        sent = lax.dynamic_index_in_dim(value, (me + steps) % count, 0, keepdims=False)
+        got = ring(sent, "seq", steps)
+        whole = lax.dynamic_update_slice_in_dim(whole, got, ((me - steps) % count) * rows, 0)
+    return whole
+
+
+def swap_out(whole, count, kind, low=None):
+    low = whole if low is None else low
+    rows = whole.shape[0] // count
+    me = lax.axis_index("seq")
+    value = jnp.zeros((count, rows) + whole.shape[1:], kind)
+    own = lax.dynamic_slice_in_dim(whole, me * rows, rows, 0)
+    value = lax.dynamic_update_index_in_dim(value, own.astype(kind), me, 0)
+    for steps in range(1, count):
+        sent = lax.dynamic_slice_in_dim(low, ((me + steps) % count) * rows, rows, 0)
+        got = ring(sent, "seq", steps)
+        value = lax.dynamic_update_index_in_dim(value, got.astype(kind), (me - steps) % count, 0)
+    return value
+
+
+def pack_small(arrays, shard):
+    gains, shifts, in_bias, out_bias, a_bias, embed, kernel = arrays
+    flat = [x.reshape(-1) for x in (gains, shifts, in_bias, out_bias, a_bias, kernel, embed)]
+    total = jnp.concatenate(flat)
+    return jnp.pad(total, (0, -total.shape[0] % (16 * shard))).reshape(-1, shard)
+
+
+def unpack_small(packed, shard):
+    groups = packed.shape[0]
+    wide = lambda lo, hi: jnp.swapaxes(packed[:, lo:hi], 0, 1).reshape(hi - lo, groups * shard)
+    taken = 12
+    gains, shifts = wide(0, 6), wide(6, 12)
+    per = 4
+    in_bias = jnp.swapaxes(packed[:, taken : taken + 2 * per].reshape(groups, 2, per * shard), 0, 1).reshape(2, -1)
+    taken += 2 * per
+    out_bias = wide(taken, taken + 2)
+    a_bias = wide(taken + 2, taken + 5)
+    kernel = wide(taken + 5, taken + 5 + KERNEL)
+    taken += 5 + KERNEL
+    buckets = LEFT + RIGHT + 1
+    embed = packed[:, taken:].reshape(groups, -1)[:, : buckets * (HD // groups)].reshape(groups, buckets, HD // groups)
+    return gains, shifts, in_bias, out_bias, a_bias, jnp.swapaxes(embed, 0, 1).reshape(buckets, HD), kernel
+
+
+def split_small(whole, groups):
+    gains, shifts, in_bias, out_bias, a_bias, embed, kernel = whole
+    shard = gains.shape[1] // groups
+    cut = lambda x: jnp.swapaxes(x.reshape(x.shape[0], groups, -1), 0, 1).reshape(groups, -1)
+    flat = jnp.concatenate([cut(x) for x in (gains, shifts, in_bias, out_bias, a_bias, kernel, embed)], axis=1)
+    flat = jnp.pad(flat, ((0, 0), (0, -flat.shape[1] % (16 * shard))))
+    return flat.reshape(groups, -1, shard)
+
+
+def unsplit_small(rows, shapes):
+    flat = rows.reshape(-1)
+    out, taken = [], 0
+    for shape in shapes:
+        size = shape[0] * shape[1]
+        out.append(flat[taken : taken + size].reshape(shape))
+        taken += size
+    return out
+
+
+def gather_small(value):
+    groups, z = lax.axis_size("fsdp"), lax.axis_index("fsdp")
+    parts = [value] + [ring(value, "fsdp", steps) for steps in range(1, groups)]
+    turned = jnp.stack(parts[::-1] * 2)
+    return lax.dynamic_slice_in_dim(turned, groups - 1 - z, groups, 0)
+
+
+def reduce_small(value):
+    groups, z = lax.axis_size("fsdp"), lax.axis_index("fsdp")
+    for axis, flip in (("rep", CORE_FLIP), ("rep", X_FLIP), ("seq", 1)):
+        value = value + hop(value, axis, flip)
+    total = pick(value, z, 0)
+    for steps in range(1, groups):
+        total = total + ring(pick(value, (z + steps) % groups, 0), "fsdp", steps)
+    return total
+
+
+def fast_body(inputs, cotangent, ln_gain, ln_bias, ffn_in, ffn_in_bias, ffn_out, ffn_out_bias, qkv_weight, attn_out, attn_bias, dist_embed, pw_in, depthwise, pw_out):
+    micro, clips, rows, width = inputs.shape
+    shard = ln_gain.shape[1]
+    groups = lax.axis_size("fsdp")
+    at = place()
+    small = pack_small((ln_gain, ln_bias, ffn_in_bias, ffn_out_bias, attn_bias, dist_embed, depthwise), shard)
+    small = gather_small(small)
+    start = swap_in(inputs.reshape(micro, rows, width))
+    f_in0 = gather_by_hops(at, ffn_in[0])
+    f_out0 = gather_by_hops(at, ffn_out[0])
+    w_mid = gather_weight(jnp.concatenate([qkv_weight, attn_out, pw_in, pw_out], axis=1))
+    w_qkv, w_o, c_in, c_out = jnp.split(w_mid, [3 * width, 4 * width, 6 * width], axis=1)
+    f_in1 = gather_by_hops(at, ffn_in[1])
+    f_out1 = gather_weight(ffn_out[1])
+
+    gains, shifts, f_in_b, f_out_b, a_bias, embed, kernel = unpack_small(small, shard)
+    table, embed2 = bias_tables(embed)
+    gains, shifts, f_in_b, f_out_b, a_bias, kernel = (x.astype(HIGH) for x in (gains, shifts, f_in_b, f_out_b, a_bias, kernel))
+
+    def ffn_fwd(values, i, w_in, w_out, which):
+        normed = norm_fwd(values, gains[which], shifts[which])
+        linear = matmul(normed, w_in) + f_in_b[i]
+        active, linear = lax.optimization_barrier((jax.nn.silu(linear).astype(LOW), linear.astype(LOW)))
+        out = values.astype(HIGH) + 0.5 * (matmul(active, w_out) + f_out_b[i])
+        return out, (values, normed, linear, active)
+
+    def silu_bwd(grad, linear):
+        gate = jax.nn.sigmoid(linear)
+        return grad * (gate * (1.0 + linear * (1.0 - gate)))
+
+    def ffn_bwd(grad, grad_low, kept, which, w_in, w_out, scale, flipped):
+        values, normed, linear, active = kept
+        product = left_t if not flipped else lambda a, g: left_t(g, a)
+        d_w_out = product(active, grad_low).astype(LOW)
+        d_lin = silu_bwd(right_t(grad_low, w_out), linear.astype(HIGH))
+        d_b_in = jnp.sum(d_lin, axis=0)
+        lin_low, d_w_out = lax.optimization_barrier((d_lin.astype(LOW), d_w_out))
+        d_w_in = product(normed, lin_low).astype(LOW)
+        lin_low, d_w_in = lax.optimization_barrier((lin_low, d_w_in))
+        back = norm_bwd(values, right_t(lin_low, w_in), gains[which], shifts[which], grad, scale)
+        return back, d_w_in, d_b_in, d_w_out
+
+    first, keep_one = ffn_fwd(start, 0, f_in0, f_out0, 0)
+    n_two = norm_fwd(first, gains[1], shifts[1])
+    proj_bias = jnp.concatenate([a_bias[0], jnp.zeros_like(a_bias[0]), a_bias[1]])
+    proj = (matmul(n_two, w_qkv) + proj_bias).astype(LOW)
+    mixed, lse = attn_forward_call(proj, table, width)
+    mixed, cotangent = lax.optimization_barrier((mixed, cotangent))
+    cot = swap_in(cotangent.reshape(micro, rows, width))
+    second = first + matmul(mixed, w_o) + a_bias[2]
+    n_three = norm_fwd(second, gains[2], shifts[2])
+    pre = matmul(n_three, c_in)
+    gated, pre = lax.optimization_barrier(((pre[:, :width] * jax.nn.sigmoid(pre[:, width:])).astype(LOW), pre.astype(LOW)))
+    conv = conv_fwd_call(gated, kernel)
+    z = norm_fwd(conv, gains[3], shifts[3], True)
+    third = second + matmul(z, c_out)
+    fourth, keep_four = ffn_fwd(third, 1, f_in1, f_out1, 4)
+    final = norm_fwd(fourth, gains[5], shifts[5])
+    out_final = swap_out(final, micro, LOW)
+
+    grad_fourth, grad_low, sums_five = norm_bwd(fourth, cot, gains[5], shifts[5], None, 0.5)
+    (grad_third, grad_low, sums_four), d_in1, d_in_b1, d_out1 = ffn_bwd(grad_fourth, grad_low, keep_four, 4, f_in1, f_out1, 1.0, True)
+    r_out1, r_in1 = reduce_weight(d_out1), reduce_weight(d_in1)
+
+    conv_low = grad_low
+    grad_conv, _, sums_three = norm_bwd(conv, right_t(grad_low, c_out), gains[3], shifts[3], None, 1.0, True)
+    g_pre, d_kernel = conv_bwd_call(grad_conv, gated, pre, kernel)
+    d_conv = weight_grads(g_pre, conv_low, n_three, z)
+    d_conv, g_pre = lax.optimization_barrier((d_conv, g_pre))
+    r_conv = reduce_weight(d_conv)
+    g_pre = jnp.concatenate([g_pre[0], g_pre[1]], axis=1)
+    grad_second, grad_low, sums_two = norm_bwd(second, right_t(g_pre, c_in), gains[2], shifts[2], grad_third)
+
+    attn_low = grad_low
+    grad_mixed = right_t(grad_low, w_o).astype(LOW)
+    g_proj, d_embed, d_bias = attn_backward_call(proj, mixed, lse, grad_mixed, table, embed2, width)
+    d_embed = jnp.sum(d_embed.reshape(2, HD, width // 128, 128), axis=(0, 2)).T[: LEFT + RIGHT + 1]
+    d_attn = weight_grads(g_proj, attn_low, n_two, mixed)
+    d_attn, g_proj = lax.optimization_barrier((d_attn, g_proj))
+    r_attn = reduce_weight(d_attn)
+    g_proj = jnp.concatenate([g_proj[0], g_proj[1], g_proj[2]], axis=1)
+    grad_first, grad_low, sums_one = norm_bwd(first, right_t(g_proj, w_qkv), gains[1], shifts[1], grad_second, 0.5)
+
+    (grad_start, start_low, sums_zero), d_in0, d_in_b0, d_out0 = ffn_bwd(grad_first, grad_low, keep_one, 0, f_in0, f_out0, 1.0, False)
+    r_out0, r_in0 = reduce_by_hops(at, d_out0), reduce_by_hops(at, d_in0)
+    grad_start = swap_out(grad_start, micro, HIGH, start_low)
+
+    sums = [sums_zero, sums_one, sums_two, sums_three, sums_four, sums_five]
+    small = split_small(
+        (
+            jnp.stack([x[0] for x in sums]),
+            jnp.stack([x[1] for x in sums]),
+            jnp.stack([d_in_b0, d_in_b1]),
+            jnp.stack([sums_one[2], sums_five[2]]),
+            jnp.stack([d_bias[0], d_bias[1], sums_two[2]]),
+            d_embed,
+            d_kernel,
+        ),
+        groups,
+    )
+    small = reduce_small(small)
+    shapes = [(6, shard), (6, shard), (2, 4 * shard), (2, shard), (3, shard), (KERNEL, shard), (LEFT + RIGHT + 1, HD // groups)]
+    s_gain, s_shift, s_in_b, s_out_b, s_a, s_kernel, s_embed = unsplit_small(small, shapes)
+    g_qkv, g_o = r_attn[: 3 * width], r_attn[3 * width :]
+    g_c_in, g_c_out = r_conv[: 2 * width], r_conv[2 * width :]
+    return (
+        out_final.reshape(micro, clips, rows, width),
+        grad_start.reshape(micro, clips, rows, width),
+        s_gain,
+        s_shift,
+        jnp.stack([r_in0.astype(HIGH), as_grad(r_in1)]),
+        s_in_b,
+        jnp.stack([r_out0.astype(HIGH), as_grad(r_out1)]),
+        s_out_b,
+        as_grad(g_qkv),
+        as_grad(g_o),
+        s_a,
+        s_embed,
+        as_grad(g_c_in),
+        s_kernel,
+        as_grad(g_c_out),
+    )
+
+
+def body(inputs, *rest):
+    micro, clips, _, width = inputs.shape
+    if (lax.axis_size("seq"), lax.axis_size("rep"), micro, clips) == (2, 4, 2, 1):
+        return fast_body(inputs, *rest)
+    return general_body(inputs, *rest)
+
+
 def solution(mesh):
     return jax.shard_map(
         body,

time: 2700 us -> 1170 us (0.43)
  waiting for transfers between devices: 1360 us -> 313 us
  matrix products: 738 us -> 241 us
  other arithmetic: 343 us -> 67.1 us
  Pallas kernels: 0 us -> 274 us
  blocking collectives: 143 us -> 0 us
  starting transfers between devices: 12 us -> 113 us
  local copies, waits for them, and re-layouts: 81.7 us -> 135 us
    reduce_scatter x14 -> x8, waiting for transfers between devices: 568 us -> 0.09 us  [the longest x4 0.06 us: reduce_replicas(): return lax.psum_scatter(grad_t, REPLICAS, scatter_dimension=0, tiled=True)]
    all_gather x10 -> x6, waiting for transfers between devices: 580 us -> 39.7 us  [the longest x4 39.7 us: reduce_groups(): return lax.all_gather(part, REPLICAS, axis=0, tiled=True)]
    dot_general x22 -> x0, matrix products: 371 us -> none  [the longest x2 76.9 us: attn_backward(): jnp.einsum('chnl,nbl->chnb', grad_scores, onehot, preferred_element_type=...]
    pallas_call x0 -> x23, Pallas kernels: none -> 274 us  [the longest x1 99.6 us: attn_backward_call(): pl.pallas_call(attn_bwd_kernel, grid=(pairs,), in_specs=[col(0), col(1),...]
    ppermute x4 -> x78, waiting for transfers between devices: 3.74 us -> 272 us  [the longest x53 191 us: hop(): lax.ppermute(value, axis, [(i, i ^ flip) for i in range(lax.axis_size(axi...]
    psum x1 -> x0, waiting for transfers between devices: 141 us -> none  [body(): lax.psum(as_sent(totals), ('rep', 'seq'))]
    all_gather x7 -> x0, blocking collectives: 116 us -> none  [the longest x1 23.8 us: fetch(): lax.all_gather(shards[1], 'fsdp', axis=1, tiled=True)]
    reduce_sum x35 -> x1, other arithmetic: 105 us -> 0.08 us  [fast_body(): jnp.sum(d_embed.reshape(2, HD, width // 128, 128), axis=(0, 2))]
  transfers between devices with their start and end apart: 32 -> 92, of which waited for: 15 -> 26; matrix products, arithmetic and copies ran while one was open for 32% -> 28% of each run, Pallas kernels for 0% -> 20%
where the time goes in v1:
time: 1170 us; the launch traced here: 1160 us
  waiting for transfers between devices  313 us (27%)
  Pallas kernels  274 us (23%)
  matrix products  241 us (21%)
  local copies, waits for them, and re-layouts  135 us (12%)
  starting transfers between devices  113 us (10%)
  other arithmetic  67.1 us (6%)
  between operations  16.3 us (1%)
    ppermute x53, waiting for transfers between devices, hop(): lax.ppermute(value, axis, [(i, i ^ flip) for i in range(lax.axis_size(axi...  191 us
    pallas_call x1, Pallas kernels, attn_backward_call(): pl.pallas_call(attn_bwd_kernel, grid=(pairs,), in_specs=[col(0), col(1),...  99.6 us
    dot_general x8, matrix products, right_t(): lax.dot_general(left, right, (((1,), (1,)), ((), ())), preferred_element_...  96 us
    dot_general x8, matrix products, matmul(): return jnp.dot(left, right, preferred_element_type=HIGH)  91.1 us
    ppermute x25, waiting for transfers between devices, ring(): lax.ppermute(value, axis, [(i, (i + steps) % count) for i in range(count)])  80.7 us
    ppermute x25, starting transfers between devices, ring(): lax.ppermute(value, axis, [(i, (i + steps) % count) for i in range(count)])  73.5 us
    dot_general x4, matrix products, left_t(): lax.dot_general(left, right, (((0,), (0,)), ((), ())), preferred_element_...  53.6 us
    unnamed x254, local copies, waits for them, and re-layouts  52.5 us
  transfers between devices with their start and end apart: 92, of which 26 were waited for; matrix products, arithmetic and copies ran while one was open for 28% of the time, Pallas kernels for 20%

profile of v1, /device:TPU:0, one launch (start us, length us, event | category | flops | bytes accessed | tf_op | source)
XLA Modules:
  0.0 1159.7 jit_solution(8585619979587230778)
XLA Ops:
  34.3 11.5 collective-permute-done.1
  45.8 8.6 collective-permute-start.3
  60.5 9.1 collective-permute-done.4
  70.6 18.0 %collective-permute-done.5 = bf16[32,4096]{1,0:T(8,128)(2,1)S(1)} collective-permute-done((bf16[32,4096]{1,0:T(8,128)(2,1)S(1)}, bf16[32,4096]{1,0:T(8,128)(2,1)S(1)}, u32[]{:S(2)}, u32[]{:S(2)}) %collective-permute-start.5) | collective-permute-done | bytes 262176 | tf_op jit(solution)/shard_map/ppermute | solution.py:806
  89.3 7.9 collective-permute-start.26
  109.1 14.3 %collective-permute-done.27 = bf16[32,4096]{1,0:T(8,128)(2,1)S(1)} collective-permute-done((bf16[32,4096]{1,0:T(8,128)(2,1)}, bf16[32,4096]{1,0:T(8,128)(2,1)S(1)}, u32[]{:S(2)}, u32[]{:S(2)}) %collective-permute-start.27) | collective-permute-done | bytes 262176 | tf_op jit(solution)/shard_map/ppermute | solution.py:806
  128.0 43.8 %collective-permute-done.9 = bf16[3,16,4096]{2,1,0:T(8,128)(2,1)S(1)} collective-permute-done((bf16[3,16,4096]{2,1,0:T(8,128)(2,1)S(1)}, bf16[3,16,4096]{2,1,0:T(8,128)(2,1)S(1)}, u32[]{:S(2)}, u32[]{:S(2)}) %collective-permute-start.9) | collective-permute-done | bytes 393248 | tf_op jit(solution)/shard_map/ppermute | solution.py:801
  186.8 26.3 %collective-permute-done.31 = bf16[3,16,4096]{2,1,0:T(8,128)(2,1)} collective-permute-done((bf16[3,16,4096]{2,1,0:T(8,128)(2,1)}, bf16[3,16,4096]{2,1,0:T(8,128)(2,1)}, u32[]{:S(2)}, u32[]{:S(2)}) %collective-permute-start.31) | collective-permute-done | bytes 393248 | tf_op jit(solution)/shard_map/ppermute | solution.py:801
  219.6 21.2 %collective-permute-done.21.refs_4_ = bf16[2,3,64,1024]{3,2,1,0:T(8,128)(2,1)S(1)} collective-permute-done((bf16[2,3,64,1024]{3,2,1,0:T(8,128)(2,1)}, bf16[2,3,64,1024]{3,2,1,0:T(8,128)(2,1)S(1)}, u32[]{:S(2)}, u32[]{:S(2)}) %collective-permute-start.21) | collective-permute-done | bytes 786464 | tf_op jit(solution)/shard_map/ppermute | solution.py:801
  261.0 6.2 shard_map.263
  267.8 10.0 collective-permute-done.30.refs_2_
  278.6 15.6 %add_convert_fusion.1 = (bf16[1024,4096]{1,0:T(8,128)(2,1)}, bf16[1024,4096]{1,0:T(8,128)(2,1)}) fusion(f32[4096]{0:T(1024)S(1)} %bitcast.459, bf16[1024,1024]{1,0:T(8,128)(2,1)} %shard_map.262, bf16[1024,4096]{1,0:T(8,128)(2,1)S(1)} %shard_map.263), kind=kOutput, calls=%fused_computation.19 | convolution fusion | flops 8619294720 | bytes 27279360 | tf_op jit(solution)/shard_map/dot_general | solution.py:40
  299.4 6.3 shard_map.271
  309.0 10.4 multiply_add_fusion.1.x_ref
  324.3 10.0 add_convert_fusion.2.q_ref.k_ref.v_ref
  334.3 39.0 %shard_map.266 = (bf16[1024,1024]{1,0:T(8,128)(2,1)S(1)}, f32[1024,1024]{1,0:T(8,128)S(1)}) custom-call(bf16[1024,3072]{1,0:T(8,128)(2,1)S(1)} %add_convert_fusion.2.q_ref.k_ref.v_ref, bf16[1024,3072]{1,0:T(8,128)(2,1)S(1)} %add_convert_fusion.2.q_ref.k_ref.v_ref, bf16[1024,3072]{1,0:T(8,128)(2,1)S(1)} %add_convert_fusion.2.q_ref.k_ref.v_ref, ...), custom_call_target="tpu_custom_call" | custom-call | flops 17179869184 | bytes 12582912 | tf_op jit(solution)/shard_map/pallas_call | solution.py:563
  386.7 9.3 fusion.112
  398.5 13.3 %shard_map.268.x_ref = f32[1024,1024]{1,0:T(8,128)} custom-call(bf16[1024,1024]{1,0:T(8,128)(2,1)} %fusion.33.u_ref, f32[31,1024]{1,0:T(8,128)} %bitcast.431), custom_call_target="tpu_custom_call" | custom-call | flops 65011712 | bytes 6291456 | tf_op jit(solution)/shard_map/pallas_call | solution.py:740
  417.0 7.9 convolution_add_fusion.x_ref
  429.7 17.8 %add_convert_fusion = (bf16[1024,4096]{1,0:T(8,128)(2,1)}, bf16[1024,4096]{1,0:T(8,128)(2,1)}) fusion(f32[4096]{0:T(1024)S(1)} %bitcast.457, bf16[1024,1024]{1,0:T(8,128)(2,1)} %shard_map.270, bf16[1024,4096]{1,0:T(8,128)(2,1)} %copy-done.12), kind=kOutput, calls=%fused_computation.18 | convolution fusion | flops 8619294720 | bytes 27279360 | tf_op jit(solution)/shard_map/dot_general | solution.py:40
  447.5 14.4 %multiply_add_fusion.x_ref = f32[1024,1024]{1,0:T(8,128)S(1)} fusion(f32[1024,1024]{1,0:T(8,128)} %convolution_add_fusion.x_ref, bf16[1024,4096]{1,0:T(8,128)(2,1)} %get-tuple-element.63, bf16[1,4096,1024]{2,1,0:T(8,128)(2,1)} %all-gather.14.cloned.1.call-done, f32[1024]{0:T(1024)S(1)} %bitcast.465), kind=kOutput, calls=%fused_computation.55 | convolution fusion | flops 8593080320 | bytes 25169920 | tf_op jit(solution)/shard_map/dot_general | solution.py:40
  470.4 11.6 convolution_convert_fusion.3
  482.0 19.5 %fusion.95 = (f32[4096]{0:T(1024)}, bf16[1024,4096]{1,0:T(8,128)(2,1)}) fusion(bf16[1024,4096]{1,0:T(8,128)(2,1)} %get-tuple-element.67, bf16[1024,1024]{1,0:T(8,128)(2,1)S(1)} %get-tuple-element.66, bf16[1,4096,1024]{2,1,0:T(8,128)(2,1)} %all-gather.14.cloned.1.call-done), kind=kOutput, calls=%fused_computation.274 | convolution fusion | flops 8636067840 | bytes 27279360 | tf_op jit(solution)/shard_map/dot_general | solution.py:48
  501.5 15.1 %convolution_convert_fusion.2 = bf16[4096,1024]{1,0:T(8,128)(2,1)} fusion(bf16[1024,4096]{1,0:T(8,128)(2,1)} %get-tuple-element.69, bf16[1024,1024]{1,0:T(8,128)(2,1)S(1)} %copy-done.89), kind=kOutput, calls=%fused_computation.30 | convolution fusion | flops 8594128896 | bytes 18874368 | tf_op jit(solution)/shard_map/dot_general | solution.py:44
  516.6 12.8 %fusion.113.grad_ref = f32[1024,1024]{1,0:T(8,128)S(1)} fusion(bf16[1024,4096]{1,0:T(8,128)(2,1)} %get-tuple-element.69, bf16[1024,4096]{1,0:T(8,128)(2,1)} %copy-done.12), kind=kOutput, calls=%fused_computation.292 | convolution fusion | flops 8589934592 | bytes 20971520 | tf_op jit(solution)/shard_map/dot_general | solution.py:48
  547.2 22.3 %shard_map.276 = (bf16[2,1024,1024]{2,1,0:T(8,128)(2,1)}, f32[31,1024]{1,0:T(8,128)}) custom-call(f32[1024,1024]{1,0:T(8,128)} %copy-done.17, bf16[1024,1024]{1,0:T(8,128)(2,1)} %fusion.33.u_ref, bf16[1024,2048]{1,0:T(8,128)(2,1)} %get-tuple-element.73.pre_a_ref.pre_b_ref, bf16[1024,2048]{1,0:T(8,128)(2,1)} %get-tuple-element.73.pre_a_ref.pre_b_ref, ...), custom_call_target="tpu_custom_call" | custom-call | flops 130023424 | bytes 14680064 | tf_op jit(solution)/shard_map/pallas_call | solution.py:781
  574.9 8.4 shard_map.277
  587.3 6.8 fusion.29.grad_ref
  603.8 99.6 %shard_map.279 = (bf16[3,1024,1024]{2,1,0:T(8,128)(2,1)}, f32[128,1024]{1,0:T(8,128)S(1)}, f32[8,1024]{1,0:T(8,128)S(1)}) custom-call(bf16[1024,3072]{1,0:T(8,128)(2,1)} %copy-done.73, bf16[1024,3072]{1,0:T(8,128)(2,1)} %copy-done.73, bf16[1024,3072]{1,0:T(8,128)(2,1)} %copy-done.73, bf16[1024,1024]{1,0:T(8,128)(2,1)S(1)} %copy-done.72, ...), custom_call_target="tpu_custom_call" | custom-call | flops 42949672960 | bytes 25165824 | tf_op jit(solution)/shard_map/pallas_call | solution.py:676
  706.9 11.3 shard_map.280
  731.4 12.8 %fusion.17.grad_ref = f32[1024,1024]{1,0:T(8,128)} fusion(bf16[1024,1024]{1,0:T(8,128)(2,1)S(1)} %get-tuple-element.148, bf16[1024,1024]{1,0:T(8,128)(2,1)S(1)} %get-tuple-element.149, bf16[1024,1024]{1,0:T(8,128)(2,1)S(1)} %get-tuple-element.147, bf16[1024,7168]{1,0:T(8,128)(2,1)} %all-gather.12.cloned.1.call-done), kind=kOutput, calls=%fused_computation.32 | convolution fusion | flops 6461325312 | bytes 16777216 | tf_op jit(solution)/shard_map/dot_general | solution.py:48
  754.0 15.3 %convolution_convert_fusion.1 = bf16[4096,1024]{1,0:T(8,128)(2,1)} fusion(bf16[1024,4096]{1,0:T(8,128)(2,1)} %get-tuple-element.59, bf16[1024,1024]{1,0:T(8,128)(2,1)S(1)} %get-tuple-element.81), kind=kOutput, calls=%fused_computation.29 | convolution fusion | flops 8594128896 | bytes 18874368 | tf_op jit(solution)/shard_map/dot_general | solution.py:44
  769.3 17.9 %fusion.94 = (f32[4096]{0:T(1024)S(1)}, bf16[1024,4096]{1,0:T(8,128)(2,1)}) fusion(bf16[1024,4096]{1,0:T(8,128)(2,1)} %get-tuple-element.82, bf16[1024,1024]{1,0:T(8,128)(2,1)} %copy-done.70, bf16[4096,1024]{1,0:T(8,128)(2,1)S(1)} %bitcast.392), kind=kOutput, calls=%fused_computation.273 | convolution fusion | flops 8636067840 | bytes 27279360 | tf_op jit(solution)/shard_map/dot_general | solution.py:48
  787.2 7.0 constant_dynamic-slice_fusion.6
  796.8 11.6 convolution_convert_fusion
  816.7 15.1 %fusion.114.grad_ref = f32[1024,1024]{1,0:T(8,128)} fusion(bf16[1024,4096]{1,0:T(8,128)(2,1)} %get-tuple-element.84, bf16[1024,4096]{1,0:T(8,128)(2,1)} %copy-done.10), kind=kOutput, calls=%fused_computation.293 | convolution fusion | flops 8589934592 | bytes 20971520 | tf_op jit(solution)/shard_map/dot_general | solution.py:48
  860.2 8.0 collective-permute-done.41
  870.6 28.1 %collective-permute-done.42 = f32[4,64,256]{2,1,0:T(8,128)S(1)} collective-permute-done((f32[4,64,256]{2,1,0:T(8,128)S(1)}, f32[4,64,256]{2,1,0:T(8,128)S(1)}, u32[]{:S(2)}, u32[]{:S(2)}) %collective-permute-start.42) | collective-permute-done | bytes 262176 | tf_op jit(solution)/shard_map/ppermute | solution.py:801
  923.7 11.3 collective-permute-done.65
  942.4 15.1 %collective-permute-done.49 = bf16[4,2,16,4096]{3,2,0,1:T(8,128)(2,1)} collective-permute-done((bf16[4,2,16,4096]{3,2,0,1:T(8,128)(2,1)}, bf16[4,2,16,4096]{3,2,0,1:T(8,128)(2,1)}, u32[]{:S(2)}, u32[]{:S(2)}) %collective-permute-start.49) | collective-permute-done | bytes 1048608 | tf_op jit(solution)/shard_map/ppermute | solution.py:801
  963.6 7.0 collective-permute-done.66
  983.4 7.5 collective-permute-done.67
  991.0 7.3 collective-permute-start.52
  998.3 10.4 collective-permute-done.68
  1008.7 17.3 %collective-permute-start.53 = (bf16[2,16,4096]{2,1,0:T(8,128)(2,1)S(1)}, bf16[2,16,4096]{2,1,0:T(8,128)(2,1)S(1)}, u32[]{:S(2)}, u32[]{:S(2)}) collective-permute-start(bf16[2,16,4096]{2,1,0:T(8,128)(2,1)S(1)} %get-tuple-element.168), channel_id=1, source_target_pairs={{0,6},{2,0},{4,2},{6,4},{1,7},{3,1},{5,3},{7,5},{8,14},{10,8},{12,... | collective-permute-start | bytes 786440 | tf_op jit(solution)/shard_map/ppermute | solution.py:806
  1044.0 9.7 collective-permute-done.54
  1101.6 15.7 %all-gather.16.cloned.1.call-done = bf16[1,4096,256]{1,2,0:T(8,128)(2,1)} async-done(((bf16[1,512,256]{1,2,0:T(8,128)(2,1)}), bf16[1,4096,256]{1,2,0:T(8,128)(2,1)}) %all-gather.16.cloned.1.call-update) | async-done | bytes 2097168 | tf_op jit(solution)/shard_map/all_gather | solution.py:1027
  1123.5 24.0 %all-gather.20.cloned.1.call-done = bf16[1,4096,256]{1,2,0:T(8,128)(2,1)} async-done(((bf16[1,512,256]{1,2,0:T(8,128)(2,1)}), bf16[1,4096,256]{1,2,0:T(8,128)(2,1)}) %all-gather.20.cloned.1.call-update) | async-done | bytes 2097168 | tf_op jit(solution)/shard_map/all_gather | solution.py:1027
  (612 shorter events, 374.3 us)
Async XLA Ops:
  7.2 317.1 %all-gather.12.cloned.1.call-start = ((), (), s32[]{:S(2)}) async-start(), calls=%async_computation.8 | async-start | bytes 15138816 | tf_op jit(solution)/shard_map/all_gather | solution.py:1015
  9.1 438.3 %all-gather.14.cloned.1.call-start = ((), (), s32[]{:S(2)}) async-start(), calls=%async_computation.17 | async-start | bytes 8650752 | tf_op jit(solution)/shard_map/all_gather | solution.py:1015
  13.6 84.6 %collective-permute-start.15 = (bf16[128,1024]{1,0:T(8,128)(2,1)S(1)}, bf16[128,1024]{1,0:T(8,128)(2,1)}, u32[]{:S(2)}, u32[]{:S(2)}) collective-permute-start(bf16[128,1024]{1,0:T(8,128)(2,1)S(1)} %dynamic-slice_bitcast_fusion.11), channel_id=1, source_target_pairs={{0,2},{2,4},{4,6},{6,0},{1,3},{3,5},{5,7},{7,1},{8,10},{10,12},{12... | collective-permute-start | bytes 786440 | tf_op jit(solution)/shard_map/ppermute | solution.py:806
  16.6 85.9 %collective-permute-start.16 = (bf16[128,1024]{1,0:T(8,128)(2,1)S(1)}, bf16[128,1024]{1,0:T(8,128)(2,1)}, u32[]{:S(2)}, u32[]{:S(2)}) collective-permute-start(bf16[128,1024]{1,0:T(8,128)(2,1)S(1)} %dynamic-slice_bitcast_fusion.11), channel_id=1, source_target_pairs={{0,4},{2,6},{4,0},{6,2},{1,5},{3,7},{5,1},{7,3},{8,12},{10,14},{12... | collective-permute-start | bytes 786440 | tf_op jit(solution)/shard_map/ppermute | solution.py:806
  19.2 84.4 %collective-permute-start.17 = (bf16[128,1024]{1,0:T(8,128)(2,1)S(1)}, bf16[128,1024]{1,0:T(8,128)(2,1)}, u32[]{:S(2)}, u32[]{:S(2)}) collective-permute-start(bf16[128,1024]{1,0:T(8,128)(2,1)S(1)} %dynamic-slice_bitcast_fusion.11), channel_id=1, source_target_pairs={{0,6},{2,0},{4,2},{6,4},{1,7},{3,1},{5,3},{7,5},{8,14},{10,8},{12,... | collective-permute-start | bytes 786440 | tf_op jit(solution)/shard_map/ppermute | solution.py:806
  22.8 31.7 %collective-permute-start.2 = (bf16[64,256]{1,0:T(8,128)(2,1)S(1)}, bf16[64,256]{1,0:T(8,128)(2,1)S(1)}, u32[]{:S(2)}, u32[]{:S(2)}) collective-permute-start(bf16[64,256]{1,0:T(8,128)(2,1)S(1)} %reshape.301), channel_id=1, source_target_pairs={{0,4},{2,6},{4,0},{6,2},{1,5},{3,7},{5,1},{7,3},{8,12},{10,14},{12... | collective-permute-start | bytes 98312 | tf_op jit(solution)/shard_map/ppermute | solution.py:806
  25.2 789.0 %reduce-scatter.21.cloned.1.call-start = ((), (), s32[]{:S(2)}) async-start(), calls=%async_computation.15 | async-start | bytes 7077888 | tf_op jit(solution)/shard_map/reduce_scatter | solution.py:1019
  56.2 32.4 %collective-permute-start.5 = (bf16[32,4096]{1,0:T(8,128)(2,1)S(1)}, bf16[32,4096]{1,0:T(8,128)(2,1)S(1)}, u32[]{:S(2)}, u32[]{:S(2)}) collective-permute-start(bf16[32,4096]{1,0:T(8,128)(2,1)S(1)} %dynamic-slice_bitcast_fusion.12), channel_id=1, source_target_pairs={{0,4},{2,6},{4,0},{6,2},{1,5},{3,7},{5,1},{7,3},{8,12},{10,14},{12... | collective-permute-start | bytes 786440 | tf_op jit(solution)/shard_map/ppermute | solution.py:806
  69.6 36.8 %collective-permute-start.6 = (bf16[32,4096]{1,0:T(8,128)(2,1)S(1)}, bf16[32,4096]{1,0:T(8,128)(2,1)S(1)}, u32[]{:S(2)}, u32[]{:S(2)}) collective-permute-start(bf16[32,4096]{1,0:T(8,128)(2,1)S(1)} %dynamic-slice_bitcast_fusion.12), channel_id=1, source_target_pairs={{0,6},{2,0},{4,2},{6,4},{1,7},{3,1},{5,3},{7,5},{8,14},{10,8},{12,... | collective-permute-start | bytes 786440 | tf_op jit(solution)/shard_map/ppermute | solution.py:806
  103.6 109.5 %collective-permute-start = (bf16[512,1024]{1,0:T(8,128)(2,1)}, bf16[512,1024]{1,0:T(8,128)(2,1)}, u32[]{:S(2)}, u32[]{:S(2)}) collective-permute-start(bf16[512,1024]{1,0:T(8,128)(2,1)} %dynamic-slice_bitcast_fusion.5), channel_id=1, source_target_pairs={{0,1},{1,0},{2,3},{3,2},{4,5},{5,4},{6,7},{7,6},{8,9},{9,8},{10,11... | collective-permute-start | bytes 3145736 | tf_op jit(solution)/shard_map/ppermute | solution.py:806
  108.1 68.8 %collective-permute-start.20 = (bf16[3,64,1024]{2,1,0:T(8,128)(2,1)S(1)}, bf16[3,64,1024]{2,1,0:T(8,128)(2,1)S(1)}, u32[]{:S(2)}, u32[]{:S(2)}) collective-permute-start(bf16[3,64,1024]{2,1,0:T(8,128)(2,1)S(1)} %get-tuple-element.174), channel_id=1, source_target_pairs={{0,1},{1,0},{2,3},{3,2},{4,5},{5,4},{6,7},{7,6},{8,9},{9,8},{10,11... | collective-permute-start | bytes 1179656 | tf_op jit(solution)/shard_map/ppermute | solution.py:801
  123.4 48.5 %collective-permute-start.9 = (bf16[3,16,4096]{2,1,0:T(8,128)(2,1)S(1)}, bf16[3,16,4096]{2,1,0:T(8,128)(2,1)S(1)}, u32[]{:S(2)}, u32[]{:S(2)}) collective-permute-start(bf16[3,16,4096]{2,1,0:T(8,128)(2,1)S(1)} %get-tuple-element.178), channel_id=1, source_target_pairs={{0,1},{1,0},{2,3},{3,2},{4,5},{5,4},{6,7},{7,6},{8,9},{9,8},{10,11... | collective-permute-start | bytes 1179656 | tf_op jit(solution)/shard_map/ppermute | solution.py:801
  125.0 49.2 %collective-permute-start.7 = (bf16[3,16,4096]{2,1,0:T(8,128)(2,1)S(1)}, bf16[3,16,4096]{2,1,0:T(8,128)(2,1)S(1)}, u32[]{:S(2)}, u32[]{:S(2)}) collective-permute-start(bf16[3,16,4096]{2,1,0:T(8,128)(2,1)S(1)} %get-tuple-element.180), channel_id=1, source_target_pairs={{0,16},{8,24},{16,0},{24,8},{1,17},{9,25},{17,1},{25,9},{2,18},{10... | collective-permute-start | bytes 1179656 | tf_op jit(solution)/shard_map/ppermute | solution.py:801
  127.5 50.8 %collective-permute-start.29 = (bf16[3,16,4096]{2,1,0:T(8,128)(2,1)S(1)}, bf16[3,16,4096]{2,1,0:T(8,128)(2,1)S(1)}, u32[]{:S(2)}, u32[]{:S(2)}) collective-permute-start(bf16[3,16,4096]{2,1,0:T(8,128)(2,1)S(1)} %get-tuple-element.172), channel_id=1, source_target_pairs={{0,16},{8,24},{16,0},{24,8},{1,17},{9,25},{17,1},{25,9},{2,18},{10... | collective-permute-start | bytes 1179656 | tf_op jit(solution)/shard_map/ppermute | solution.py:801
  171.9 41.7 %collective-permute-start.19 = (bf16[2,3,64,1024]{3,2,1,0:T(8,128)(2,1)S(1)}, bf16[2,3,64,1024]{3,2,1,0:T(8,128)(2,1)}, u32[]{:S(2)}, u32[]{:S(2)}) collective-permute-start(bf16[2,3,64,1024]{3,2,1,0:T(8,128)(2,1)S(1)} %pad_maximum_fusion.2.refs_1_), channel_id=1, source_target_pairs={{0,1},{1,0},{2,3},{3,2},{4,5},{5,4},{6,7},{7,6},{8,9},{9,8},{10,11... | collective-permute-start | bytes 2359304 | tf_op jit(solution)/shard_map/ppermute | solution.py:801
  174.2 40.9 %collective-permute-start.10 = (bf16[2,3,16,4096]{3,2,1,0:T(8,128)(2,1)}, bf16[2,3,16,4096]{3,2,1,0:T(8,128)(2,1)}, u32[]{:S(2)}, u32[]{:S(2)}) collective-permute-start(bf16[2,3,16,4096]{3,2,1,0:T(8,128)(2,1)} %pad_maximum_fusion.1.refs_3_), channel_id=1, source_target_pairs={{0,16},{8,24},{16,0},{24,8},{1,17},{9,25},{17,1},{25,9},{2,18},{10... | collective-permute-start | bytes 2359304 | tf_op jit(solution)/shard_map/ppermute | solution.py:801
  176.9 38.2 %collective-permute-start.8 = (bf16[2,3,16,4096]{3,2,1,0:T(8,128)(2,1)}, bf16[2,3,16,4096]{3,2,1,0:T(8,128)(2,1)}, u32[]{:S(2)}, u32[]{:S(2)}) collective-permute-start(bf16[2,3,16,4096]{3,2,1,0:T(8,128)(2,1)} %pad_maximum_fusion.refs_1_), channel_id=1, source_target_pairs={{0,1},{1,0},{2,3},{3,2},{4,5},{5,4},{6,7},{7,6},{8,9},{9,8},{10,11... | collective-permute-start | bytes 2359304 | tf_op jit(solution)/shard_map/ppermute | solution.py:801
  179.0 34.1 %collective-permute-start.31 = (bf16[3,16,4096]{2,1,0:T(8,128)(2,1)}, bf16[3,16,4096]{2,1,0:T(8,128)(2,1)}, u32[]{:S(2)}, u32[]{:S(2)}) collective-permute-start(bf16[3,16,4096]{2,1,0:T(8,128)(2,1)} %get-tuple-element.170), channel_id=1, source_target_pairs={{0,1},{1,0},{2,3},{3,2},{4,5},{5,4},{6,7},{7,6},{8,9},{9,8},{10,11... | collective-permute-start | bytes 1179656 | tf_op jit(solution)/shard_map/ppermute | solution.py:801
  215.1 31.0 %collective-permute-start.12 = (bf16[2,3,16,4096]{3,2,1,0:T(8,128)(2,1)}, bf16[2,3,16,4096]{3,2,1,0:T(8,128)(2,1)S(1)}, u32[]{:S(2)}, u32[]{:S(2)}) collective-permute-start(bf16[2,3,16,4096]{3,2,1,0:T(8,128)(2,1)} %collective-permute-done.8.refs_2_), channel_id=1, source_target_pairs={{0,8},{8,0},{16,24},{24,16},{1,9},{9,1},{17,25},{25,17},{2,10},{10... | collective-permute-start | bytes 2359304 | tf_op jit(solution)/shard_map/ppermute | solution.py:801
  243.1 34.7 %collective-permute-start.30 = (bf16[2,3,16,4096]{3,2,1,0:T(8,128)(2,1)}, bf16[2,3,16,4096]{3,2,1,0:T(8,128)(2,1)}, u32[]{:S(2)}, u32[]{:S(2)}) collective-permute-start(bf16[2,3,16,4096]{3,2,1,0:T(8,128)(2,1)} %pad_maximum_fusion.4.refs_1_), channel_id=1, source_target_pairs={{0,1},{1,0},{2,3},{3,2},{4,5},{5,4},{6,7},{7,6},{8,9},{9,8},{10,11... | collective-permute-start | bytes 2359304 | tf_op jit(solution)/shard_map/ppermute | solution.py:801
  244.6 33.5 %collective-permute-start.32 = (bf16[2,3,16,4096]{3,2,1,0:T(8,128)(2,1)}, bf16[2,3,16,4096]{3,2,1,0:T(8,128)(2,1)}, u32[]{:S(2)}, u32[]{:S(2)}) collective-permute-start(bf16[2,3,16,4096]{3,2,1,0:T(8,128)(2,1)} %pad_maximum_fusion.5.refs_3_), channel_id=1, source_target_pairs={{0,16},{8,24},{16,0},{24,8},{1,17},{9,25},{17,1},{25,9},{2,18},{10... | collective-permute-start | bytes 2359304 | tf_op jit(solution)/shard_map/ppermute | solution.py:801
  246.1 32.3 %collective-permute-start.23 = (bf16[2,3,64,1024]{3,2,1,0:T(8,128)(2,1)}, bf16[2,3,64,1024]{3,2,1,0:T(8,128)(2,1)}, u32[]{:S(2)}, u32[]{:S(2)}) collective-permute-start(bf16[2,3,64,1024]{3,2,1,0:T(8,128)(2,1)} %collective-permute-done.19.refs_2_), channel_id=1, source_target_pairs={{0,8},{8,0},{16,24},{24,16},{1,9},{9,1},{17,25},{25,17},{2,10},{10... | collective-permute-start | bytes 2359304 | tf_op jit(solution)/shard_map/ppermute | solution.py:801
  267.2 32.1 %collective-permute-start.33 = (bf16[2,3,16,4096]{3,2,1,0:T(8,128)(2,1)}, bf16[2,3,16,4096]{3,2,1,0:T(8,128)(2,1)S(1)}, u32[]{:S(2)}, u32[]{:S(2)}) collective-permute-start(bf16[2,3,16,4096]{3,2,1,0:T(8,128)(2,1)} %pad_maximum_fusion.4.refs_1_), channel_id=1, source_target_pairs={{0,8},{8,0},{16,24},{24,16},{1,9},{9,1},{17,25},{25,17},{2,10},{10... | collective-permute-start | bytes 2359304 | tf_op jit(solution)/shard_map/ppermute | solution.py:801
  267.8 31.5 %collective-permute-start.35 = (bf16[2,3,16,4096]{3,2,1,0:T(8,128)(2,1)}, bf16[2,3,16,4096]{3,2,1,0:T(8,128)(2,1)S(1)}, u32[]{:S(2)}, u32[]{:S(2)}) collective-permute-start(bf16[2,3,16,4096]{3,2,1,0:T(8,128)(2,1)} %pad_maximum_fusion.5.refs_3_), channel_id=1, source_target_pairs={{0,8},{8,0},{16,24},{24,16},{1,9},{9,1},{17,25},{25,17},{2,10},{10... | collective-permute-start | bytes 2359304 | tf_op jit(solution)/shard_map/ppermute | solution.py:801
  374.5 87.8 %collective-permute-start.38 = (bf16[512,1024]{1,0:T(8,128)(2,1)}, bf16[512,1024]{1,0:T(8,128)(2,1)}, u32[]{:S(2)}, u32[]{:S(2)}) collective-permute-start(bf16[512,1024]{1,0:T(8,128)(2,1)} %dynamic-slice_bitcast_fusion.4), channel_id=1, source_target_pairs={{0,1},{1,0},{2,3},{3,2},{4,5},{5,4},{6,7},{7,6},{8,9},{9,8},{10,11... | collective-permute-start | bytes 3145736 | tf_op jit(solution)/shard_map/ppermute | solution.py:806
  583.3 248.5 %reduce-scatter.13.cloned.1.call-start = ((), (), s32[]{:S(2)}) async-start(), calls=%async_computation.11 | async-start | bytes 9437184 | tf_op jit(solution)/shard_map/reduce_scatter | solution.py:1019
  583.9 263.6 %reduce-scatter.9.cloned.1.call-start = ((), (), s32[]{:S(2)}) async-start(), calls=%async_computation.9 | async-start | bytes 9437184 | tf_op jit(solution)/shard_map/reduce_scatter | solution.py:1019
  584.5 314.3 %reduce-scatter.17.cloned.1.call-start = ((), (), s32[]{:S(2)}) async-start(), calls=%async_computation.13 | async-start | bytes 9437184 | tf_op jit(solution)/shard_map/reduce_scatter | solution.py:1019
  718.2 199.9 %reduce-scatter.23.cloned.1.call-start = ((), (), s32[]{:S(2)}) async-start(), calls=%async_computation.16 | async-start | bytes 983040 | tf_op jit(solution)/shard_map/reduce_scatter | solution.py:1026
  725.4 142.9 %collective-permute-start.37 = (bf16[512,1024]{1,0:T(8,128)(2,1)}, bf16[512,1024]{1,0:T(8,128)(2,1)}, u32[]{:S(2)}, u32[]{:S(2)}) collective-permute-start(bf16[512,1024]{1,0:T(8,128)(2,1)} %constant_dynamic-slice_fusion.11), channel_id=1, source_target_pairs={{0,1},{1,0},{2,3},{3,2},{4,5},{5,4},{6,7},{7,6},{8,9},{9,8},{10,11... | collective-permute-start | bytes 3145736 | tf_op jit(solution)/shard_map/ppermute | solution.py:806
  796.8 104.5 %collective-permute-start.62 = (bf16[4,2,2,2,64,1024]{5,4,0,1,3,2:T(8,128)(2,1)}, bf16[4,2,2,2,64,1024]{5,4,0,1,3,2:T(8,128)(2,1)}, u32[]{:S(2)}, u32[]{:S(2)}) collective-permute-start(bf16[4,2,2,2,64,1024]{5,4,0,1,3,2:T(8,128)(2,1)} %bitcast.386), channel_id=1, source_target_pairs={{0,8},{8,0},{16,24},{24,16},{1,9},{9,1},{17,25},{25,17},{2,10},{10... | collective-permute-start | bytes 12582920 | tf_op jit(solution)/shard_map/ppermute | solution.py:801
  813.8 98.6 %collective-permute-start.46 = (bf16[4,2,2,2,16,4096]{5,4,0,1,3,2:T(8,128)(2,1)}, bf16[4,2,2,2,16,4096]{5,4,0,1,3,2:T(8,128)(2,1)}, u32[]{:S(2)}, u32[]{:S(2)}) collective-permute-start(bf16[4,2,2,2,16,4096]{5,4,0,1,3,2:T(8,128)(2,1)} %bitcast.387), channel_id=1, source_target_pairs={{0,8},{8,0},{16,24},{24,16},{1,9},{9,1},{17,25},{25,17},{2,10},{10... | collective-permute-start | bytes 12582920 | tf_op jit(solution)/shard_map/ppermute | solution.py:801
  816.7 125.6 %reduce-scatter.15.cloned.1.call-start = ((), (), s32[]{:S(2)}) async-start(), calls=%async_computation.12 | async-start | bytes 1310720 | tf_op jit(solution)/shard_map/reduce_scatter | solution.py:1026
  834.3 147.5 %reduce-scatter.11.cloned.1.call-start = ((), (), s32[]{:S(2)}) async-start(), calls=%async_computation.10 | async-start | bytes 1310720 | tf_op jit(solution)/shard_map/reduce_scatter | solution.py:1026
  849.8 191.9 %reduce-scatter.19.cloned.1.call-start = ((), (), s32[]{:S(2)}) async-start(), calls=%async_computation.14 | async-start | bytes 1310720 | tf_op jit(solution)/shard_map/reduce_scatter | solution.py:1026
  856.1 203.8 %collective-permute-start.39 = (bf16[512,1024]{1,0:T(8,128)(2,1)}, bf16[512,1024]{1,0:T(8,128)(2,1)}, u32[]{:S(2)}, u32[]{:S(2)}) collective-permute-start(bf16[512,1024]{1,0:T(8,128)(2,1)} %constant_dynamic-slice_fusion.10), channel_id=1, source_target_pairs={{0,1},{1,0},{2,3},{3,2},{4,5},{5,4},{6,7},{7,6},{8,9},{9,8},{10,11... | collective-permute-start | bytes 3145736 | tf_op jit(solution)/shard_map/ppermute | solution.py:806
  868.2 30.5 %collective-permute-start.42 = (f32[4,64,256]{2,1,0:T(8,128)S(1)}, f32[4,64,256]{2,1,0:T(8,128)S(1)}, u32[]{:S(2)}, u32[]{:S(2)}) collective-permute-start(f32[4,64,256]{2,1,0:T(8,128)S(1)} %add.390), channel_id=1, source_target_pairs={{0,1},{1,0},{2,3},{3,2},{4,5},{5,4},{6,7},{7,6},{8,9},{9,8},{10,11... | collective-permute-start | bytes 786440 | tf_op jit(solution)/shard_map/ppermute | solution.py:801
  901.2 189.9 %all-gather.22.cloned.1.call-start = ((), (), s32[]{:S(2)}) async-start(), calls=%async_computation.21 | async-start | bytes 1769472 | tf_op jit(solution)/shard_map/all_gather | solution.py:1027
  918.1 177.9 %all-gather.18.cloned.1.call-start = ((), (), s32[]{:S(2)}) async-start(), calls=%async_computation.19 | async-start | bytes 2359296 | tf_op jit(solution)/shard_map/all_gather | solution.py:1027
  921.9 35.5 %collective-permute-start.49 = (bf16[4,2,16,4096]{3,2,0,1:T(8,128)(2,1)}, bf16[4,2,16,4096]{3,2,0,1:T(8,128)(2,1)}, u32[]{:S(2)}, u32[]{:S(2)}) collective-permute-start(bf16[4,2,16,4096]{3,2,0,1:T(8,128)(2,1)} %dynamic-slice_bitcast_fusion.2), channel_id=1, source_target_pairs={{0,1},{1,0},{2,3},{3,2},{4,5},{5,4},{6,7},{7,6},{8,9},{9,8},{10,11... | collective-permute-start | bytes 3145736 | tf_op jit(solution)/shard_map/ppermute | solution.py:801
  923.1 38.0 %collective-permute-start.47 = (bf16[4,2,16,4096]{3,2,0,1:T(8,128)(2,1)S(1)}, bf16[4,2,16,4096]{3,2,0,1:T(8,128)(2,1)}, u32[]{:S(2)}, u32[]{:S(2)}) collective-permute-start(bf16[4,2,16,4096]{3,2,0,1:T(8,128)(2,1)S(1)} %dynamic-slice_bitcast_fusion.3), channel_id=1, source_target_pairs={{0,16},{8,24},{16,0},{24,8},{1,17},{9,25},{17,1},{25,9},{2,18},{10... | collective-permute-start | bytes 3145736 | tf_op jit(solution)/shard_map/ppermute | solution.py:801
  937.5 33.1 %collective-permute-start.66 = (bf16[4,64,1024]{2,1,0:T(8,128)(2,1)}, bf16[4,64,1024]{2,1,0:T(8,128)(2,1)}, u32[]{:S(2)}, u32[]{:S(2)}) collective-permute-start(bf16[4,64,1024]{2,1,0:T(8,128)(2,1)} %dynamic-slice_bitcast_fusion.6), channel_id=1, source_target_pairs={{0,16},{8,24},{16,0},{24,8},{1,17},{9,25},{17,1},{25,9},{2,18},{10... | collective-permute-start | bytes 1572872 | tf_op jit(solution)/shard_map/ppermute | solution.py:801
  942.3 175.0 %all-gather.16.cloned.1.call-start = ((), (), s32[]{:S(2)}) async-start(), calls=%async_computation.18 | async-start | bytes 2359296 | tf_op jit(solution)/shard_map/all_gather | solution.py:1027
  975.6 33.1 %collective-permute-start.68 = (bf16[2,64,1024]{2,1,0:T(8,128)(2,1)}, bf16[2,64,1024]{2,1,0:T(8,128)(2,1)}, u32[]{:S(2)}, u32[]{:S(2)}) collective-permute-start(bf16[2,64,1024]{2,1,0:T(8,128)(2,1)} %get-tuple-element.164), channel_id=1, source_target_pairs={{0,4},{2,6},{4,0},{6,2},{1,5},{3,7},{5,1},{7,3},{8,12},{10,14},{12... | collective-permute-start | bytes 786440 | tf_op jit(solution)/shard_map/ppermute | solution.py:806
  980.9 45.1 %collective-permute-start.69 = (bf16[2,64,1024]{2,1,0:T(8,128)(2,1)}, bf16[2,64,1024]{2,1,0:T(8,128)(2,1)}, u32[]{:S(2)}, u32[]{:S(2)}) collective-permute-start(bf16[2,64,1024]{2,1,0:T(8,128)(2,1)} %get-tuple-element.165), channel_id=1, source_target_pairs={{0,6},{2,0},{4,2},{6,4},{1,7},{3,1},{5,3},{7,5},{8,14},{10,8},{12,... | collective-permute-start | bytes 786440 | tf_op jit(solution)/shard_map/ppermute | solution.py:806
  981.8 165.7 %all-gather.20.cloned.1.call-start = ((), (), s32[]{:S(2)}) async-start(), calls=%async_computation.20 | async-start | bytes 2359296 | tf_op jit(solution)/shard_map/all_gather | solution.py:1027
  982.1 46.7 %collective-permute-start.51 = (bf16[2,16,4096]{2,1,0:T(8,128)(2,1)S(1)}, bf16[2,16,4096]{2,1,0:T(8,128)(2,1)S(1)}, u32[]{:S(2)}, u32[]{:S(2)}) collective-permute-start(bf16[2,16,4096]{2,1,0:T(8,128)(2,1)S(1)} %get-tuple-element.166), channel_id=1, source_target_pairs={{0,2},{2,4},{4,6},{6,0},{1,3},{3,5},{5,7},{7,1},{8,10},{10,12},{12... | collective-permute-start | bytes 786440 | tf_op jit(solution)/shard_map/ppermute | solution.py:806
  991.0 41.6 %collective-permute-start.52 = (bf16[2,16,4096]{2,1,0:T(8,128)(2,1)S(1)}, bf16[2,16,4096]{2,1,0:T(8,128)(2,1)S(1)}, u32[]{:S(2)}, u32[]{:S(2)}) collective-permute-start(bf16[2,16,4096]{2,1,0:T(8,128)(2,1)S(1)} %get-tuple-element.167), channel_id=1, source_target_pairs={{0,4},{2,6},{4,0},{6,2},{1,5},{3,7},{5,1},{7,3},{8,12},{10,14},{12... | collective-permute-start | bytes 786440 | tf_op jit(solution)/shard_map/ppermute | solution.py:806
  (157 other events, 2713.9 us)
Sparse Core Ops, SparseCore 0:
  10.9 175.0 all-gather.11
  189.1 99.7 all-gather.13
  583.4 60.8 reduce-scatter.20
  648.0 71.2 reduce-scatter.12
  722.6 71.2 reduce-scatter.8
  797.7 85.9 reduce-scatter.16
  885.9 23.4 reduce-scatter.22
  911.7 26.3 reduce-scatter.14
  940.5 25.7 reduce-scatter.10
  968.5 41.2 reduce-scatter.18
  1011.8 42.6 all-gather.21
  1056.5 30.5 all-gather.17
  1089.1 28.1 all-gather.15
  1119.2 28.1 all-gather.19

commit v2 on v1

--- a/solution.py
+++ b/solution.py
@@ -811,14 +811,6 @@
     return jnp.stack([rep // 2, rep % 2, lax.axis_index("seq"), lax.axis_index("fsdp")]).astype(jnp.int32)
 
 
-def spread(first, second):
-    first_x, second_y = hop(first, "rep", X_FLIP), hop(second, "seq", 1)
-    first, second = jnp.stack([first, first_x]), jnp.stack([second, second_y])
-    first_y, second_x = hop(first, "seq", 1), hop(second, "rep", X_FLIP)
-    near = [first, first_y, second, second_x]
-    return near + [hop(value, "rep", CORE_FLIP) for value in near]
-
-
 def spread_blocks(x, core, y):
     for other in range(2):
         for half, moved, array in ((0, 0, 0), (0, 1, 1), (1, 0, 2), (1, 1, 3)):
@@ -830,19 +822,16 @@
                 yield other * 4 + array, entry, half, x ^ flip_x, core ^ other, y ^ flip_y
 
 
-def assemble_kernel(planes, has_own, at_ref, *refs):
-    shard_ref = refs[0] if has_own else None
-    parts = refs[has_own : has_own + 8]
-    out_ref, sems = refs[has_own + 8 :]
+def assemble_kernel(planes, at_ref, shard_ref, *refs):
+    parts = refs[:8]
+    out_ref, sems = refs[8:]
     x, core, y, z = (at_ref[i] for i in range(4))
     half_rows = parts[0].shape[-2]
     rows = 16 * half_rows
-    copies = []
-    if has_own:
-        copies.append((shard_ref, out_ref.at[pl.ds(pl.multiple_of(z * rows, rows), rows), :]))
+    copies = [(shard_ref, out_ref.at[pl.ds(pl.multiple_of(z * rows, rows), rows), :])]
     for array, entry, half, bx, bc, by in spread_blocks(x, core, y):
         for plane in range(planes):
-            base = lax.rem(z + (planes - plane), planes + 1) * rows if has_own else 0
+            base = lax.rem(z + (planes - plane), planes + 1) * rows
             row = base + (((bx * 2 + bc) * 2 + by) * 2 + half) * half_rows
             copies.append((parts[array].at[entry, plane], out_ref.at[pl.ds(pl.multiple_of(row, half_rows), half_rows), :]))
     started = [pltpu.make_async_copy(source, target, sems.at[i]) for i, (source, target) in enumerate(copies)]
@@ -854,28 +843,39 @@
 
 def assemble(at, shard, parts):
     planes, half_rows, columns = parts[0].shape[1:]
-    has_own = 0 if shard is None else 1
-    rows = 16 * half_rows * (planes + 1 if has_own else 1)
-    own = [shard] if has_own else []
+    rows = 16 * half_rows * (planes + 1)
     return pl.pallas_call(
-        functools.partial(assemble_kernel, planes, has_own),
-        in_specs=[pl.BlockSpec(memory_space=pltpu.SMEM)] + [pl.BlockSpec(memory_space=pl.ANY)] * (8 + has_own),
+        functools.partial(assemble_kernel, planes),
+        in_specs=[pl.BlockSpec(memory_space=pltpu.SMEM)] + [pl.BlockSpec(memory_space=pl.ANY)] * 9,
         out_specs=pl.BlockSpec(memory_space=pltpu.VMEM),
         out_shape=jax.ShapeDtypeStruct((rows, columns), LOW),
-        scratch_shapes=[pltpu.SemaphoreType.DMA((16 * planes + has_own,))],
+        scratch_shapes=[pltpu.SemaphoreType.DMA((16 * planes + 1,))],
         compiler_params=pltpu.CompilerParams(vmem_limit_bytes=12 * 1024 * 1024),
         cost_estimate=pl.CostEstimate(flops=0, bytes_accessed=4 * rows * columns, transcendentals=0),
-    )(at, *own, *parts)
-
-
-def gather_by_hops(at, shard):
-    pieces = lax.axis_size("rep") * lax.axis_size("seq")
-    count = shard.shape[0] // pieces
-    mine = lax.dynamic_slice_in_dim(shard, replica_index() * count, count, 0)
-    got = [ring(mine, "fsdp", steps) for steps in range(1, lax.axis_size("fsdp"))]
-    half = count // 2
-    first, second = jnp.stack([g[:half] for g in got]), jnp.stack([g[half:] for g in got])
-    return assemble(at, shard, spread(first, second))
+    )(at, shard, *parts)
+
+
+def own_piece(shard):
+    count = shard.shape[0] // (lax.axis_size("rep") * lax.axis_size("seq"))
+    return lax.dynamic_slice_in_dim(shard, replica_index() * count, count, 0)
+
+
+def from_planes(piece):
+    got = [ring(piece, "fsdp", steps) for steps in range(1, lax.axis_size("fsdp"))]
+    half = piece.shape[0] // 2
+    return jnp.stack([g[:half] for g in got]), jnp.stack([g[half:] for g in got])
+
+
+def around(halves):
+    first, second = halves
+    first_x, second_y = hop(first, "rep", X_FLIP), hop(second, "seq", 1)
+    first, second = jnp.stack([first, first_x]), jnp.stack([second, second_y])
+    first_y, second_x = hop(first, "seq", 1), hop(second, "rep", X_FLIP)
+    return [first, first_y, second, second_x]
+
+
+def both_cores(near):
+    return near + [hop(value, "rep", CORE_FLIP) for value in near]
 
 
 def plus(a, b):
@@ -886,23 +886,147 @@
     return lax.dynamic_index_in_dim(value, index, axis, keepdims=False)
 
 
-def reduce_by_hops(at, grad):
-    x, core, y, z = (at[i] for i in range(4))
+X, Y, CORE = 4, 1, 2
+
+
+def across(value, flip):
+    pieces = lax.axis_size("rep") * lax.axis_size("seq")
+    return lax.ppermute(value, REPLICAS, [(i, i ^ flip) for i in range(pieces)])
+
+
+def reduce_cores(at, grad):
     groups = lax.axis_size("fsdp")
     rows, columns = grad.shape
-    parts = grad.reshape(groups, 2, 2, 2, 2, rows // (16 * groups), columns)
-    total = plus(pick(parts, core, 2), hop(pick(parts, 1 - core, 2), "rep", CORE_FLIP))
-    first, second = total[:, :, :, 0], total[:, :, :, 1]
-    first = plus(pick(first, x, 1), hop(pick(first, 1 - x, 1), "rep", X_FLIP))
-    second = plus(pick(second, y, 2), hop(pick(second, 1 - y, 2), "seq", 1))
-    first = plus(pick(first, y, 1), hop(pick(first, 1 - y, 1), "seq", 1))
-    second = plus(pick(second, x, 1), hop(pick(second, 1 - x, 1), "rep", X_FLIP))
-    both = jnp.stack([first, second], axis=1)
-    total = pick(both, z, 0).astype(HIGH)
+    parts = grad.reshape(groups, 2, 2, 2, rows // (8 * groups), columns)
+    return plus(pick(parts, at[1], 2), across(pick(parts, 1 - at[1], 2), CORE))
+
+
+def reduce_first(at, total):
+    x, y = at[0], at[2]
+    half = total.shape[3] // 2
+    first, second = total[:, :, :, :half], total[:, :, :, half:]
+    first = plus(pick(first, x, 1), across(pick(first, 1 - x, 1), X))
+    second = plus(pick(second, y, 2), across(pick(second, 1 - y, 2), Y))
+    return first, second
+
+
+def reduce_second(at, halves):
+    x, y = at[0], at[2]
+    first, second = halves
+    first = plus(pick(first, y, 1), across(pick(first, 1 - y, 1), Y))
+    second = plus(pick(second, x, 1), across(pick(second, 1 - x, 1), X))
+    return jnp.concatenate([first, second], axis=1)
+
+
+def reduce_along(at, part):
+    groups, z = lax.axis_size("fsdp"), at[3]
+    total = pick(part, z, 0).astype(HIGH)
     for steps in range(1, groups):
-        total = total + ring(pick(both, (z + steps) % groups, 0), "fsdp", steps).astype(HIGH)
-    total = total.astype(LOW)[:, None]
-    return assemble(at, None, spread(total[0], total[1]))
+        total = total + ring(pick(part, (z + steps) % groups, 0), "fsdp", steps).astype(HIGH)
+    return total.astype(LOW)
+
+
+def spread_plane(part):
+    return jnp.stack([part] + [across(part, flip) for flip in (X, Y, X + Y)])
+
+
+def finish_kernel(at_ref, near_ref, far_ref, whole_ref, out_ref):
+    step = pl.program_id(0)
+
+    @pl.when(step < 4)
+    def _():
+        out_ref[...] = near_ref[...].astype(HIGH)
+
+    @pl.when(step >= 4)
+    def _():
+        out_ref[...] = far_ref[...].astype(HIGH)
+
+
+def finish_place(step, at):
+    x, core, y = at[0], at[1], at[2]
+    entry = step % 4
+    return ((x ^ (entry % 2)) * 2 + (core ^ (step // 4))) * 2 + (y ^ (entry // 2))
+
+
+def finish_first(at, near, far, whole):
+    _, rows, columns = near.shape
+    return pl.pallas_call(
+        finish_kernel,
+        grid_spec=pltpu.PrefetchScalarGridSpec(
+            num_scalar_prefetch=1,
+            grid=(8,),
+            in_specs=[
+                pl.BlockSpec((1, rows, columns), lambda i, at: (jnp.minimum(i, 3), 0, 0)),
+                pl.BlockSpec((1, rows, columns), lambda i, at: (jnp.maximum(i - 4, 0), 0, 0)),
+                pl.BlockSpec(memory_space=pl.ANY),
+            ],
+            out_specs=pl.BlockSpec((1, rows, columns), lambda i, at: (0, finish_place(i, at), 0)),
+        ),
+        out_shape=jax.ShapeDtypeStruct(whole.shape, HIGH),
+        input_output_aliases={3: 0},
+        cost_estimate=pl.CostEstimate(flops=0, bytes_accessed=48 * rows * columns, transcendentals=0),
+    )(at, near, far, whole)
+
+
+def turn_early_kernel(count, part_ref, out_ref, in_ref, conv_ref):
+    shard, columns = part_ref.shape[2], out_ref.shape[2]
+    for block in range(count):
+        rows = slice(block * columns, (block + 1) * columns)
+        out_ref[0, block * shard : (block + 1) * shard, :] = part_ref[0, rows, :].astype(HIGH).T
+    edge = count * columns
+    middle = edge + in_ref.shape[2]
+    in_ref[0] = part_ref[0, edge:middle, :].astype(HIGH).T
+    conv_ref[...] = part_ref[0, middle:, :].astype(HIGH).T
+
+
+def turn_early(part, width, hidden):
+    replicas, total, shard = part.shape
+    count = hidden // width
+    inner = total - (width + hidden) // replicas
+    return pl.pallas_call(
+        functools.partial(turn_early_kernel, count),
+        grid=(replicas,),
+        in_specs=[pl.BlockSpec((1, total, shard), lambda r: (r, 0, 0))],
+        out_specs=[
+            pl.BlockSpec((1, count * shard, width // replicas), lambda r: (1, 0, r)),
+            pl.BlockSpec((1, shard, hidden // replicas), lambda r: (1, 0, r)),
+            pl.BlockSpec((shard, 3 * width // replicas), lambda r: (0, r)),
+        ],
+        out_shape=[
+            jax.ShapeDtypeStruct((2, count * shard, width), HIGH),
+            jax.ShapeDtypeStruct((2, shard, hidden), HIGH),
+            jax.ShapeDtypeStruct((shard, 3 * width), HIGH),
+        ],
+        cost_estimate=pl.CostEstimate(flops=0, bytes_accessed=6 * replicas * total * shard, transcendentals=0),
+    )(part)
+
+
+def turn_attn_kernel(edge, part_ref, qkv_ref, o_ref):
+    turned = part_ref[0].astype(HIGH).T
+
+    @pl.when(pl.program_id(0) < edge)
+    def _():
+        qkv_ref[...] = turned
+
+    @pl.when(pl.program_id(0) >= edge)
+    def _():
+        o_ref[...] = turned
+
+
+def turn_attn(part, width):
+    replicas, total, shard = part.shape
+    edge = 3 * width // total
+    return pl.pallas_call(
+        functools.partial(turn_attn_kernel, edge),
+        grid=(replicas,),
+        in_specs=[pl.BlockSpec((1, total, shard), lambda r: (r, 0, 0))],
+        out_specs=[
+            pl.BlockSpec((shard, total), lambda r: (0, jnp.minimum(r, edge - 1))),
+            pl.BlockSpec((shard, total), lambda r: (0, jnp.maximum(r - edge, 0))),
+        ],
+        out_shape=[jax.ShapeDtypeStruct((shard, 3 * width), HIGH), jax.ShapeDtypeStruct((shard, width), HIGH)],
+        cost_estimate=pl.CostEstimate(flops=0, bytes_accessed=6 * replicas * total * shard, transcendentals=0),
+    )(part)
 
 
 NORM_ROWS = 256
@@ -980,27 +1104,31 @@
     )(values, grad, gain[None], shift[None], *extra)
 
 
-def weight_grads_kernel(many, g_ref, last_ref, a_ref, b_ref, out_ref):
+def weight_grads_kernel(many, flipped, g_ref, last_ref, a_ref, b_ref, out_ref):
     step = pl.program_id(0)
+
+    def product(grad, value):
+        return (left_t(grad, value) if flipped else left_t(value, grad)).astype(LOW)
 
     @pl.when(step < many)
     def _():
-        out_ref[...] = left_t(g_ref[...], a_ref[...]).astype(LOW)
+        out_ref[...] = product(g_ref[...], a_ref[...])
 
     @pl.when(step == many)
     def _():
-        out_ref[...] = left_t(last_ref[...], b_ref[...]).astype(LOW)
-
-
-def weight_grads(grads, last, first_in, last_in):
+        out_ref[...] = product(last_ref[...], b_ref[...])
+
+
+def weight_grads(grads, last, first_in, last_in, flipped):
     many, rows, width = grads.shape
     full = pl.BlockSpec((rows, width), lambda i: (0, 0))
+    shape = ((many + 1) * width, width) if flipped else (width, (many + 1) * width)
     return pl.pallas_call(
-        functools.partial(weight_grads_kernel, many),
+        functools.partial(weight_grads_kernel, many, flipped),
         grid=(many + 1,),
         in_specs=[pl.BlockSpec((None, rows, width), lambda i: (jnp.minimum(i, many - 1), 0, 0)), full, full, full],
-        out_specs=pl.BlockSpec((width, width), lambda i: (i, 0)),
-        out_shape=jax.ShapeDtypeStruct(((many + 1) * width, width), LOW),
+        out_specs=pl.BlockSpec((width, width), (lambda i: (i, 0)) if flipped else (lambda i: (0, i))),
+        out_shape=jax.ShapeDtypeStruct(shape, LOW),
         compiler_params=pltpu.CompilerParams(vmem_limit_bytes=40 * 1024 * 1024),
         cost_estimate=pl.CostEstimate(
             flops=2 * (many + 1) * rows * width * width, bytes_accessed=4 * (many + 2) * rows * width, transcendentals=0
@@ -1019,20 +1147,18 @@
     return lax.psum_scatter(grad_t, REPLICAS, scatter_dimension=0, tiled=True)
 
 
-def reduce_groups(part):
+def by_groups(part):
     groups = lax.axis_size("fsdp")
     columns, rows = part.shape
-    part = jnp.swapaxes(part.reshape(columns, groups, rows // groups), 0, 1)
-    part = lax.psum_scatter(part, "fsdp", scatter_dimension=0, tiled=False)
-    return lax.all_gather(part, REPLICAS, axis=0, tiled=True)
-
-
-def reduce_weight(grad_t):
-    return reduce_groups(reduce_replicas(grad_t))
-
-
-def as_grad(grad_t):
-    return grad_t.astype(HIGH).T
+    return jnp.swapaxes(part.reshape(columns, groups, rows // groups), 0, 1)
+
+
+def reduce_groups(part):
+    return lax.psum_scatter(part, "fsdp", scatter_dimension=0, tiled=False)
+
+
+def to_replicas(part):
+    return lax.all_gather(part, REPLICAS, axis=0, tiled=False)
 
 
 def swap_in(value):
@@ -1113,14 +1239,20 @@
     return lax.dynamic_slice_in_dim(turned, groups - 1 - z, groups, 0)
 
 
-def reduce_small(value):
+def reduce_planes(value):
     groups, z = lax.axis_size("fsdp"), lax.axis_index("fsdp")
-    for axis, flip in (("rep", CORE_FLIP), ("rep", X_FLIP), ("seq", 1)):
-        value = value + hop(value, axis, flip)
     total = pick(value, z, 0)
     for steps in range(1, groups):
         total = total + ring(pick(value, (z + steps) % groups, 0), "fsdp", steps)
     return total
+
+
+def sum_replicas(value):
+    pieces = lax.axis_size("rep") * lax.axis_size("seq")
+    terms = [value] + [across(value, flip) for flip in range(1, pieces)]
+    while len(terms) > 1:
+        terms = [a + b for a, b in zip(terms[::2], terms[1::2])]
+    return terms[0]
 
 
 def fast_body(inputs, cotangent, ln_gain, ln_bias, ffn_in, ffn_in_bias, ffn_out, ffn_out_bias, qkv_weight, attn_out, attn_bias, dist_embed, pw_in, depthwise, pw_out):
@@ -1128,71 +1260,79 @@
     shard = ln_gain.shape[1]
     groups = lax.axis_size("fsdp")
     at = place()
+    pieces = lax.axis_size("rep") * lax.axis_size("seq")
     small = pack_small((ln_gain, ln_bias, ffn_in_bias, ffn_out_bias, attn_bias, dist_embed, depthwise), shard)
     small = gather_small(small)
     start = swap_in(inputs.reshape(micro, rows, width))
-    f_in0 = gather_by_hops(at, ffn_in[0])
-    f_out0 = gather_by_hops(at, ffn_out[0])
-    w_mid = gather_weight(jnp.concatenate([qkv_weight, attn_out, pw_in, pw_out], axis=1))
-    w_qkv, w_o, c_in, c_out = jnp.split(w_mid, [3 * width, 4 * width, 6 * width], axis=1)
-    f_in1 = gather_by_hops(at, ffn_in[1])
+    tie = lax.optimization_barrier
+    piece, halves_in = tie((own_piece(ffn_out[0]), from_planes(own_piece(ffn_in[0]))))
+    halves_out = from_planes(piece)
+    near_in, halves_out, start, small = tie((around(halves_in), halves_out, start, small))
+    f_in0 = assemble(at, ffn_in[0], both_cores(near_in))
+    near_out = around(halves_out)
+    w_attn = gather_weight(jnp.concatenate([qkv_weight, attn_out], axis=1))
+    w_qkv, w_o = w_attn[:, : 3 * width], w_attn[:, 3 * width :]
+    rest = gather_weight(jnp.concatenate([pw_in, pw_out, ffn_in[1]], axis=1))
+    c_in, c_out, f_in1 = jnp.split(rest, [2 * width, 3 * width], axis=1)
     f_out1 = gather_weight(ffn_out[1])
 
     gains, shifts, f_in_b, f_out_b, a_bias, embed, kernel = unpack_small(small, shard)
     table, embed2 = bias_tables(embed)
     gains, shifts, f_in_b, f_out_b, a_bias, kernel = (x.astype(HIGH) for x in (gains, shifts, f_in_b, f_out_b, a_bias, kernel))
 
-    def ffn_fwd(values, i, w_in, w_out, which):
+    def ffn_fwd(values, i, w_in, which, w_out):
         normed = norm_fwd(values, gains[which], shifts[which])
         linear = matmul(normed, w_in) + f_in_b[i]
-        active, linear = lax.optimization_barrier((jax.nn.silu(linear).astype(LOW), linear.astype(LOW)))
+        active, linear = tie((jax.nn.silu(linear).astype(LOW), linear.astype(LOW)))
+        active, w_out = w_out(active)
         out = values.astype(HIGH) + 0.5 * (matmul(active, w_out) + f_out_b[i])
-        return out, (values, normed, linear, active)
+        return out, (values, normed, linear, active), w_out
+
+    def late_weight(active):
+        active_low, near = tie((active, near_out))
+        return active_low, assemble(at, ffn_out[0], both_cores(near))
 
     def silu_bwd(grad, linear):
         gate = jax.nn.sigmoid(linear)
         return grad * (gate * (1.0 + linear * (1.0 - gate)))
 
-    def ffn_bwd(grad, grad_low, kept, which, w_in, w_out, scale, flipped):
-        values, normed, linear, active = kept
-        product = left_t if not flipped else lambda a, g: left_t(g, a)
-        d_w_out = product(active, grad_low).astype(LOW)
-        d_lin = silu_bwd(right_t(grad_low, w_out), linear.astype(HIGH))
-        d_b_in = jnp.sum(d_lin, axis=0)
-        lin_low, d_w_out = lax.optimization_barrier((d_lin.astype(LOW), d_w_out))
-        d_w_in = product(normed, lin_low).astype(LOW)
-        lin_low, d_w_in = lax.optimization_barrier((lin_low, d_w_in))
-        back = norm_bwd(values, right_t(lin_low, w_in), gains[which], shifts[which], grad, scale)
-        return back, d_w_in, d_b_in, d_w_out
-
-    first, keep_one = ffn_fwd(start, 0, f_in0, f_out0, 0)
+    first, keep_one, f_out0 = ffn_fwd(start, 0, f_in0, 0, late_weight)
     n_two = norm_fwd(first, gains[1], shifts[1])
     proj_bias = jnp.concatenate([a_bias[0], jnp.zeros_like(a_bias[0]), a_bias[1]])
     proj = (matmul(n_two, w_qkv) + proj_bias).astype(LOW)
     mixed, lse = attn_forward_call(proj, table, width)
-    mixed, cotangent = lax.optimization_barrier((mixed, cotangent))
-    cot = swap_in(cotangent.reshape(micro, rows, width))
     second = first + matmul(mixed, w_o) + a_bias[2]
     n_three = norm_fwd(second, gains[2], shifts[2])
     pre = matmul(n_three, c_in)
     gated, pre = lax.optimization_barrier(((pre[:, :width] * jax.nn.sigmoid(pre[:, width:])).astype(LOW), pre.astype(LOW)))
-    conv = conv_fwd_call(gated, kernel)
+    conv, cotangent = tie((conv_fwd_call(gated, kernel), cotangent))
+    cot = swap_in(cotangent.reshape(micro, rows, width))
     z = norm_fwd(conv, gains[3], shifts[3], True)
     third = second + matmul(z, c_out)
-    fourth, keep_four = ffn_fwd(third, 1, f_in1, f_out1, 4)
+    fourth, keep_four, _ = ffn_fwd(third, 1, f_in1, 4, lambda active: (active, f_out1))
     final = norm_fwd(fourth, gains[5], shifts[5])
     out_final = swap_out(final, micro, LOW)
 
     grad_fourth, grad_low, sums_five = norm_bwd(fourth, cot, gains[5], shifts[5], None, 0.5)
-    (grad_third, grad_low, sums_four), d_in1, d_in_b1, d_out1 = ffn_bwd(grad_fourth, grad_low, keep_four, 4, f_in1, f_out1, 1.0, True)
-    r_out1, r_in1 = reduce_weight(d_out1), reduce_weight(d_in1)
+    tie = lax.optimization_barrier
+    values, normed, linear, active = keep_four
+    d_out1 = left_t(grad_low, active).astype(LOW)
+    d_out1, grad_low = tie((d_out1, grad_low))
+    p_out1 = reduce_replicas(d_out1)
+    d_lin = silu_bwd(right_t(grad_low, f_out1), linear.astype(HIGH))
+    d_in_b1 = jnp.sum(d_lin, axis=0)
+    lin_low = tie(d_lin.astype(LOW))
+    d_in1 = left_t(lin_low, normed).astype(LOW)
+    lin_low, d_in1 = tie((lin_low, d_in1))
+    p_in1 = reduce_replicas(d_in1)
+    grad_third, grad_low, sums_four = norm_bwd(values, right_t(lin_low, f_in1), gains[4], shifts[4], grad_fourth)
 
     conv_low = grad_low
     grad_conv, _, sums_three = norm_bwd(conv, right_t(grad_low, c_out), gains[3], shifts[3], None, 1.0, True)
     g_pre, d_kernel = conv_bwd_call(grad_conv, gated, pre, kernel)
-    d_conv = weight_grads(g_pre, conv_low, n_three, z)
-    d_conv, g_pre = lax.optimization_barrier((d_conv, g_pre))
-    r_conv = reduce_weight(d_conv)
+    d_conv = weight_grads(g_pre, conv_low, n_three, z, True)
+    d_conv, g_pre, p_out1 = tie((d_conv, g_pre, p_out1))
+    p_conv = reduce_replicas(d_conv)
     g_pre = jnp.concatenate([g_pre[0], g_pre[1]], axis=1)
     grad_second, grad_low, sums_two = norm_bwd(second, right_t(g_pre, c_in), gains[2], shifts[2], grad_third)
 
@@ -1200,15 +1340,38 @@
     grad_mixed = right_t(grad_low, w_o).astype(LOW)
     g_proj, d_embed, d_bias = attn_backward_call(proj, mixed, lse, grad_mixed, table, embed2, width)
     d_embed = jnp.sum(d_embed.reshape(2, HD, width // 128, 128), axis=(0, 2)).T[: LEFT + RIGHT + 1]
-    d_attn = weight_grads(g_proj, attn_low, n_two, mixed)
-    d_attn, g_proj = lax.optimization_barrier((d_attn, g_proj))
-    r_attn = reduce_weight(d_attn)
+    g_proj, p_out1, p_in1, p_conv = tie((g_proj, p_out1, p_in1, p_conv))
+    strips = p_out1.reshape(p_out1.shape[0], groups, -1, width // groups).transpose(1, 2, 0, 3)
+    early = jnp.concatenate([strips.reshape(groups, -1, width // groups), by_groups(p_in1), by_groups(p_conv)], axis=1)
+    g_proj, early = tie((g_proj, early))
+    early = reduce_groups(early)
+    d_attn = weight_grads(g_proj, attn_low, n_two, mixed, True)
+    d_attn, g_proj = tie((d_attn, g_proj))
+    p_attn = reduce_replicas(d_attn)
     g_proj = jnp.concatenate([g_proj[0], g_proj[1], g_proj[2]], axis=1)
-    grad_first, grad_low, sums_one = norm_bwd(first, right_t(g_proj, w_qkv), gains[1], shifts[1], grad_second, 0.5)
-
-    (grad_start, start_low, sums_zero), d_in0, d_in_b0, d_out0 = ffn_bwd(grad_first, grad_low, keep_one, 0, f_in0, f_out0, 1.0, False)
-    r_out0, r_in0 = reduce_by_hops(at, d_out0), reduce_by_hops(at, d_in0)
-    grad_start = swap_out(grad_start, micro, HIGH, start_low)
+    grad_normed = right_t(g_proj, w_qkv)
+    grad_first, grad_low, sums_one = norm_bwd(first, grad_normed, gains[1], shifts[1], grad_second, 0.5)
+
+    values, normed, linear, active = keep_one
+    d_out0 = left_t(active, grad_low).astype(LOW)
+    d_out0, grad_low = tie((d_out0, grad_low))
+    t_out0 = reduce_cores(at, d_out0)
+    d_lin = silu_bwd(right_t(grad_low, f_out0), linear.astype(HIGH))
+    d_in_b0 = jnp.sum(d_lin, axis=0)
+    lin_low, t_out0, early, out_final = tie((d_lin.astype(LOW), t_out0, early, out_final))
+    early = to_replicas(early)
+    t_out0 = reduce_first(at, t_out0)
+    d_in0 = left_t(normed, lin_low).astype(LOW)
+    d_in0, lin_low, t_out0 = tie((d_in0, lin_low, t_out0))
+    t_out0 = reduce_second(at, t_out0)
+    t_in0 = reduce_cores(at, d_in0)
+    grad_normed = right_t(lin_low, f_in0)
+    grad_normed, t_out0, t_in0, p_attn = tie((grad_normed, t_out0, t_in0, p_attn))
+    attn = to_replicas(reduce_groups(by_groups(p_attn)))
+    t_out0 = reduce_along(at, t_out0)
+    t_in0 = reduce_first(at, t_in0)
+    grad_start, start_low, sums_zero = norm_bwd(values, grad_normed, gains[0], shifts[0], grad_first)
+    start_low, t_out0, t_in0 = tie((start_low, t_out0, t_in0))
 
     sums = [sums_zero, sums_one, sums_two, sums_three, sums_four, sums_five]
     small = split_small(
@@ -1223,27 +1386,39 @@
         ),
         groups,
     )
-    small = reduce_small(small)
+    near = spread_plane(t_out0)
+    t_in0 = reduce_second(at, t_in0)
+    small = reduce_planes(small)
+    near, t_in0, start_low, small = tie((near, t_in0, start_low, small))
+    t_in0 = reduce_along(at, t_in0)
+    far = across(near, CORE)
+    small = sum_replicas(small)
+    grad_start = swap_out(grad_start, micro, HIGH, start_low)
+    far, t_in0, small = tie((far, t_in0, small))
+    near_in = spread_plane(t_in0)
+    grad_out, grad_in, g_conv = turn_early(early, width, lin_low.shape[1])
+    grad_out = finish_first(at, near, far, grad_out)
+    near_in, grad_out = tie((near_in, grad_out))
+    grad_in = finish_first(at, near_in, across(near_in, CORE), grad_in)
+    g_qkv, g_o = turn_attn(attn, width)
     shapes = [(6, shard), (6, shard), (2, 4 * shard), (2, shard), (3, shard), (KERNEL, shard), (LEFT + RIGHT + 1, HD // groups)]
     s_gain, s_shift, s_in_b, s_out_b, s_a, s_kernel, s_embed = unsplit_small(small, shapes)
-    g_qkv, g_o = r_attn[: 3 * width], r_attn[3 * width :]
-    g_c_in, g_c_out = r_conv[: 2 * width], r_conv[2 * width :]
     return (
         out_final.reshape(micro, clips, rows, width),
         grad_start.reshape(micro, clips, rows, width),
         s_gain,
         s_shift,
-        jnp.stack([r_in0.astype(HIGH), as_grad(r_in1)]),
+        grad_in,
         s_in_b,
-        jnp.stack([r_out0.astype(HIGH), as_grad(r_out1)]),
+        grad_out,
         s_out_b,
-        as_grad(g_qkv),
-        as_grad(g_o),
+        g_qkv,
+        g_o,
         s_a,
         s_embed,
-        as_grad(g_c_in),
+        g_conv[:, : 2 * width],
         s_kernel,
-        as_grad(g_c_out),
+        g_conv[:, 2 * width :],
     )
 
 

time: 1170 us -> 1020 us (0.87)
  waiting for transfers between devices: 313 us -> 211 us
  other arithmetic: 67.1 us -> 36.5 us
  starting transfers between devices: 113 us -> 94.4 us
  Pallas kernels: 274 us -> 291 us
  local copies, waits for them, and re-layouts: 135 us -> 121 us
    ppermute x53 -> x16, waiting for transfers between devices: 191 us -> 61.3 us  [hop(): lax.ppermute(value, axis, [(i, i ^ flip) for i in range(lax.axis_size(axi...]
    ppermute x0 -> x25, waiting for transfers between devices: none -> 90.7 us  [across(): return lax.ppermute(value, REPLICAS, [(i, i ^ flip) for i in range(pieces)])]
    all_gather x4 -> x2, waiting for transfers between devices: 39.7 us -> 0.02 us  [to_replicas(): return lax.all_gather(part, REPLICAS, axis=0, tiled=False)]
    ppermute x0 -> x25, starting transfers between devices: none -> 25.8 us  [across(): return lax.ppermute(value, REPLICAS, [(i, i ^ flip) for i in range(pieces)])]
    ppermute x53 -> x16, starting transfers between devices: 38.7 us -> 14.5 us  [hop(): lax.ppermute(value, axis, [(i, i ^ flip) for i in range(lax.axis_size(axi...]
    unnamed x254 -> x210, local copies, waits for them, and re-layouts: 52.5 us -> 29.6 us
    ppermute x25 -> x22, waiting for transfers between devices: 80.7 us -> 58.7 us  [ring(): lax.ppermute(value, axis, [(i, (i + steps) % count) for i in range(count)])]
    ppermute x25 -> x22, starting transfers between devices: 73.5 us -> 53.5 us  [ring(): lax.ppermute(value, axis, [(i, (i + steps) % count) for i in range(count)])]
  transfers between devices with their start and end apart: 92 -> 74, of which waited for: 26 -> 30; matrix products, arithmetic and copies ran while one was open for 28% -> 35% of each run, Pallas kernels for 20% -> 28%
where the time goes in v2:
time: 1020 us; the launch traced here: 1010 us
  Pallas kernels  291 us (29%)
  matrix products  240 us (24%)
  waiting for transfers between devices  211 us (21%)
  local copies, waits for them, and re-layouts  121 us (12%)
  starting transfers between devices  94.4 us (9%)
  other arithmetic  36.5 us (4%)
  between operations  16.2 us (2%)
    pallas_call x1, Pallas kernels, attn_backward_call(): pl.pallas_call(attn_bwd_kernel, grid=(pairs,), in_specs=[col(0), col(1),...  99.4 us
    dot_general x8, matrix products, right_t(): lax.dot_general(left, right, (((1,), (1,)), ((), ())), preferred_element_...  94.6 us
    ppermute x25, waiting for transfers between devices, across(): return lax.ppermute(value, REPLICAS, [(i, i ^ flip) for i in range(pieces)])  90.7 us
    dot_general x8, matrix products, matmul(): return jnp.dot(left, right, preferred_element_type=HIGH)  90 us
    ppermute x16, waiting for transfers between devices, hop(): lax.ppermute(value, axis, [(i, i ^ flip) for i in range(lax.axis_size(axi...  61.3 us
    ppermute x22, waiting for transfers between devices, ring(): lax.ppermute(value, axis, [(i, (i + steps) % count) for i in range(count)])  58.7 us
    dot_general x4, matrix products, left_t(): lax.dot_general(left, right, (((0,), (0,)), ((), ())), preferred_element_...  55 us
    ppermute x22, starting transfers between devices, ring(): lax.ppermute(value, axis, [(i, (i + steps) % count) for i in range(count)])  53.5 us
  transfers between devices with their start and end apart: 74, of which 30 were waited for; matrix products, arithmetic and copies ran while one was open for 35% of the time, Pallas kernels for 28%

profile of v2, /device:TPU:0, one launch (start us, length us, event | category | flops | bytes accessed | tf_op | source)
XLA Modules:
  0.0 1010.3 jit_solution(4333710962156414643)
XLA Ops:
  41.0 9.3 collective-permute-start.13
  57.5 8.5 collective-permute-done.9
  71.3 17.2 %collective-permute-done.5 = bf16[3,16,4096]{2,1,0:T(8,128)(2,1)S(1)} collective-permute-done((bf16[3,16,4096]{2,1,0:T(8,128)(2,1)S(1)}, bf16[3,16,4096]{2,1,0:T(8,128)(2,1)S(1)}, u32[]{:S(2)}, u32[]{:S(2)}) %collective-permute-start.5) | collective-permute-done | bytes 393248 | tf_op jit(solution)/shard_map/ppermute | solution.py:801
  91.1 26.6 %collective-permute-done.4.refs_1_ = bf16[2,3,16,4096]{3,2,1,0:T(8,128)(2,1)S(1)} collective-permute-done((bf16[2,3,16,4096]{3,2,1,0:T(8,128)(2,1)S(1)}, bf16[2,3,16,4096]{3,2,1,0:T(8,128)(2,1)S(1)}, u32[]{:S(2)}, u32[]{:S(2)}) %collective-permute-start.4) | collective-permute-done | bytes 786464 | tf_op jit(solution)/shard_map/ppermute | solution.py:801
  124.5 9.3 collective-permute-done.18
  155.0 7.4 shard_map.263
  162.4 14.2 %add_convert_fusion.1 = (bf16[1024,4096]{1,0:T(8,128)(2,1)}, bf16[1024,4096]{1,0:T(8,128)(2,1)}) fusion(f32[4096]{0:T(1024)S(1)} %bitcast.387, bf16[1024,1024]{1,0:T(8,128)(2,1)S(1)} %copy-done.69, bf16[1024,4096]{1,0:T(8,128)(2,1)S(1)} %shard_map.263), kind=kOutput, calls=%fused_computation.19 | convolution fusion | flops 8619294720 | bytes 27279360 | tf_op jit(solution)/shard_map/dot_general | solution.py:40
  187.2 10.4 %multiply_add_fusion.1.x_ref = f32[1024,1024]{1,0:T(8,128)} fusion(bf16[1024,1024]{1,0:T(8,128)(2,1)S(1)} %copy-done.2, f32[1024]{0:T(1024)S(1)} %bitcast.394, bf16[1024,4096]{1,0:T(8,128)(2,1)S(1)} %bitcast.399, bf16[4096,1024]{1,0:T(8,128)(2,1)S(1)} %shard_map.264), kind=kOutput, calls=%fused_computation.59 | convolution fusion | flops 8594128896 | bytes 23072768 | tf_op jit(solution)/shard_map/dot_general | solution.py:40
  202.5 9.5 add_convert_fusion.2.q_ref.k_ref.v_ref
  212.0 39.4 %shard_map.266 = (bf16[1024,1024]{1,0:T(8,128)(2,1)S(1)}, f32[1024,1024]{1,0:T(8,128)S(1)}) custom-call(bf16[1024,3072]{1,0:T(8,128)(2,1)S(1)} %add_convert_fusion.2.q_ref.k_ref.v_ref, bf16[1024,3072]{1,0:T(8,128)(2,1)S(1)} %add_convert_fusion.2.q_ref.k_ref.v_ref, bf16[1024,3072]{1,0:T(8,128)(2,1)S(1)} %add_convert_fusion.2.q_ref.k_ref.v_ref, ...), custom_call_target="tpu_custom_call" | custom-call | flops 17179869184 | bytes 12582912 | tf_op jit(solution)/shard_map/pallas_call | solution.py:563
  251.5 7.5 add_add_fusion.x_ref
  263.8 9.4 fusion.86
  275.8 13.3 %shard_map.268.x_ref = f32[1024,1024]{1,0:T(8,128)} custom-call(bf16[1024,1024]{1,0:T(8,128)(2,1)} %fusion.37.u_ref, f32[31,1024]{1,0:T(8,128)} %bitcast.353), custom_call_target="tpu_custom_call" | custom-call | flops 65011712 | bytes 6291456 | tf_op jit(solution)/shard_map/pallas_call | solution.py:740
  294.1 7.8 convolution_add_fusion.x_ref
  306.9 16.9 %add_convert_fusion = (bf16[1024,4096]{1,0:T(8,128)(2,1)}, bf16[1024,4096]{1,0:T(8,128)(2,1)}) fusion(f32[4096]{0:T(1024)S(1)} %bitcast.386, bf16[1024,1024]{1,0:T(8,128)(2,1)} %shard_map.270, bf16[1024,7168]{1,0:T(8,128)(2,1)} %all-gather.10.cloned.1.call-done), kind=kOutput, calls=%fused_computation.18 | convolution fusion | flops 8619294720 | bytes 27279360 | tf_op jit(solution)/shard_map/dot_general | solution.py:40
  324.9 14.4 %multiply_add_fusion.x_ref = f32[1024,1024]{1,0:T(8,128)S(1)} fusion(f32[1024,1024]{1,0:T(8,128)} %convolution_add_fusion.x_ref, bf16[1024,4096]{1,0:T(8,128)(2,1)} %get-tuple-element.131, bf16[1,4096,1024]{2,1,0:T(8,128)(2,1)} %all-gather.14.cloned.1.call-done, f32[1024]{0:T(1024)S(1)} %bitcast.393), kind=kOutput, calls=%fused_computation.57 | convolution fusion | flops 8593080320 | bytes 25169920 | tf_op jit(solution)/shard_map/dot_general | solution.py:40
  339.8 10.6 %collective-permute-done.26 = bf16[512,1024]{1,0:T(8,128)(2,1)} collective-permute-done((bf16[512,1024]{1,0:T(8,128)(2,1)}, bf16[512,1024]{1,0:T(8,128)(2,1)}, u32[]{:S(2)}, u32[]{:S(2)}) %collective-permute-start.26) | collective-permute-done | bytes 1048608 | tf_op jit(solution)/shard_map/ppermute | solution.py:806
  357.7 11.4 %convolution_convert_fusion.3 = bf16[1024,4096]{1,0:T(8,128)(2,1)} fusion(bf16[1024,1024]{1,0:T(8,128)(2,1)S(1)} %get-tuple-element.134, bf16[1024,4096]{1,0:T(8,128)(2,1)S(1)} %bitcast.397), kind=kOutput, calls=%fused_computation.31 | convolution fusion | flops 8594128896 | bytes 18874368 | tf_op jit(solution)/shard_map/dot_general | solution.py:44
  369.2 20.2 %fusion.70 = (f32[4096]{0:T(1024)}, bf16[1024,4096]{1,0:T(8,128)(2,1)}) fusion(bf16[1024,4096]{1,0:T(8,128)(2,1)} %get-tuple-element.135, bf16[1024,1024]{1,0:T(8,128)(2,1)S(1)} %get-tuple-element.134, bf16[1,4096,1024]{2,1,0:T(8,128)(2,1)} %all-gather.14.cloned.1.call-done), kind=kOutput, calls=%fused_computation.216 | convolution fusion | flops 8636067840 | bytes 27279360 | tf_op jit(solution)/shard_map/dot_general | solution.py:48
  389.4 15.3 %convolution_convert_fusion.2 = bf16[4096,1024]{1,0:T(8,128)(2,1)} fusion(bf16[1024,4096]{1,0:T(8,128)(2,1)} %get-tuple-element.136, bf16[1024,1024]{1,0:T(8,128)(2,1)S(1)} %copy-done.71), kind=kOutput, calls=%fused_computation.30 | convolution fusion | flops 8594128896 | bytes 18874368 | tf_op jit(solution)/shard_map/dot_general | solution.py:44
  404.8 13.6 %fusion.17.grad_ref = f32[1024,1024]{1,0:T(8,128)S(1)} fusion(bf16[1024,4096]{1,0:T(8,128)(2,1)} %get-tuple-element.136, bf16[1024,7168]{1,0:T(8,128)(2,1)} %all-gather.10.cloned.1.call-done), kind=kOutput, calls=%fused_computation.32 | convolution fusion | flops 8589934592 | bytes 20971520 | tf_op jit(solution)/shard_map/dot_general | solution.py:48
  422.6 5.8 fusion.47.grad_ref
  436.1 22.3 %shard_map.274 = (bf16[2,1024,1024]{2,1,0:T(8,128)(2,1)}, f32[31,1024]{1,0:T(8,128)}) custom-call(f32[1024,1024]{1,0:T(8,128)} %copy-done.14, bf16[1024,1024]{1,0:T(8,128)(2,1)} %fusion.37.u_ref, bf16[1024,2048]{1,0:T(8,128)(2,1)} %get-tuple-element.140.pre_a_ref.pre_b_ref, bf16[1024,2048]{1,0:T(8,128)(2,1)} %get-tuple-element.140.pre_a_ref.pre_b_ref, ...), custom_call_target="tpu_custom_call" | custom-call | flops 130023424 | bytes 14680064 | tf_op jit(solution)/shard_map/pallas_call | solution.py:781
  463.9 8.5 shard_map.275
  480.5 6.6 fusion.33.grad_ref
  497.1 99.4 %shard_map.277 = (bf16[3,1024,1024]{2,1,0:T(8,128)(2,1)}, f32[128,1024]{1,0:T(8,128)S(1)}, f32[8,1024]{1,0:T(8,128)S(1)}) custom-call(bf16[1024,3072]{1,0:T(8,128)(2,1)} %copy-done.57, bf16[1024,3072]{1,0:T(8,128)(2,1)} %copy-done.57, bf16[1024,3072]{1,0:T(8,128)(2,1)} %copy-done.57, bf16[1024,1024]{1,0:T(8,128)(2,1)S(1)} %copy-done.55, ...), custom_call_target="tpu_custom_call" | custom-call | flops 42949672960 | bytes 25165824 | tf_op jit(solution)/shard_map/pallas_call | solution.py:676
  614.1 11.3 %shard_map.278 = bf16[4096,1024]{1,0:T(8,128)(2,1)} custom-call(bf16[3,1024,1024]{2,1,0:T(8,128)(2,1)S(1)} %copy-done.13, bf16[1024,1024]{1,0:T(8,128)(2,1)S(1)} %copy-done.50, bf16[1024,1024]{1,0:T(8,128)(2,1)S(1)} %copy-done.27, bf16[1024,1024]{1,0:T(8,128)(2,1)S(1)} %copy-done.56), custom_call_target="tpu_custom_call" | custom-call | flops 8589934592 | bytes 20971520 | tf_op jit(solution)/shard_map/pallas_call | solution.py:1126
  631.0 10.6 %fusion.21.grad_ref = f32[1024,1024]{1,0:T(8,128)S(1)} fusion(bf16[1024,1024]{1,0:T(8,128)(2,1)} %get-tuple-element.265, bf16[1024,1024]{1,0:T(8,128)(2,1)} %get-tuple-element.266, bf16[1024,1024]{1,0:T(8,128)(2,1)S(1)} %get-tuple-element.264, bf16[1024,4096]{1,0:T(8,128)(2,1)} %all-gather.8.cloned.1.call-done), kind=kOutput, calls=%fused_computation.36 | convolution fusion | flops 6461325312 | bytes 16777216 | tf_op jit(solution)/shard_map/dot_general | solution.py:48
  646.0 16.9 %convolution_convert_fusion.1 = bf16[4096,1024]{1,0:T(8,128)(2,1)} fusion(bf16[1024,4096]{1,0:T(8,128)(2,1)} %get-tuple-element.122, bf16[1024,1024]{1,0:T(8,128)(2,1)S(1)} %get-tuple-element.158), kind=kOutput, calls=%fused_computation.29 | convolution fusion | flops 8594128896 | bytes 18874368 | tf_op jit(solution)/shard_map/dot_general | solution.py:44
  662.9 6.9 constant_dynamic-slice_fusion.5
  674.9 19.3 %fusion.69 = (f32[4096]{0:T(1024)S(1)}, bf16[1024,4096]{1,0:T(8,128)(2,1)}) fusion(bf16[1024,4096]{1,0:T(8,128)(2,1)} %get-tuple-element.159, bf16[1024,1024]{1,0:T(8,128)(2,1)} %copy-done.51, bf16[4096,1024]{1,0:T(8,128)(2,1)} %copy-done.12), kind=kOutput, calls=%fused_computation.215 | convolution fusion | flops 8636067840 | bytes 27279360 | tf_op jit(solution)/shard_map/dot_general | solution.py:48
  694.2 6.3 fusion.13
  707.3 11.4 %convolution_convert_fusion = bf16[1024,4096]{1,0:T(8,128)(2,1)} fusion(bf16[1024,1024]{1,0:T(8,128)(2,1)S(1)} %copy-done.70, bf16[1024,4096]{1,0:T(8,128)(2,1)S(1)} %copy-done.84), kind=kOutput, calls=%fused_computation.28 | convolution fusion | flops 8594128896 | bytes 18874368 | tf_op jit(solution)/shard_map/dot_general | solution.py:44
  718.6 27.1 %collective-permute-done.30 = bf16[4,2,64,1024]{3,2,0,1:T(8,128)(2,1)S(1)} collective-permute-done((bf16[4,2,64,1024]{3,2,0,1:T(8,128)(2,1)S(1)}, bf16[4,2,64,1024]{3,2,0,1:T(8,128)(2,1)S(1)}, u32[]{:S(2)}, u32[]{:S(2)}) %collective-permute-start.30) | collective-permute-done | bytes 1048608 | tf_op jit(solution)/shard_map/ppermute | solution.py:894
  746.6 8.6 constant_dynamic-slice_fusion.2
  762.0 12.8 %fusion.87.grad_ref = f32[1024,1024]{1,0:T(8,128)} fusion(bf16[1024,4096]{1,0:T(8,128)(2,1)} %get-tuple-element.165, bf16[1024,4096]{1,0:T(8,128)(2,1)S(1)} %bitcast.314), kind=kOutput, calls=%fused_computation.233 | convolution fusion | flops 8589934592 | bytes 20971520 | tf_op jit(solution)/shard_map/dot_general | solution.py:48
  777.4 5.8 fusion.12
  814.3 10.3 %collective-permute-start.44 = (f32[64,256]{1,0:T(8,128)S(1)}, f32[64,256]{1,0:T(8,128)S(1)}, u32[]{:S(2)}, u32[]{:S(2)}) collective-permute-start(f32[64,256]{1,0:T(8,128)S(1)} %get-tuple-element.285), channel_id=1, source_target_pairs={{0,2},{2,4},{4,6},{6,0},{1,3},{3,5},{5,7},{7,1},{8,10},{10,12},{12... | collective-permute-start | bytes 196616 | tf_op jit(solution)/shard_map/ppermute | solution.py:806
  824.7 8.8 collective-permute-done.44
  842.1 28.0 %collective-permute-done.38 = bf16[4,2,16,4096]{3,2,0,1:T(8,128)(2,1)S(1)} collective-permute-done((bf16[4,2,16,4096]{3,2,0,1:T(8,128)(2,1)S(1)}, bf16[4,2,16,4096]{3,2,0,1:T(8,128)(2,1)S(1)}, u32[]{:S(2)}, u32[]{:S(2)}) %collective-permute-start.38) | collective-permute-done | bytes 1048608 | tf_op jit(solution)/shard_map/ppermute | solution.py:894
  878.0 8.4 collective-permute-done.41
  891.8 9.3 collective-permute-done.43
  917.7 6.0 collective-permute-start.50
  927.4 18.0 %collective-permute-done.50 = bf16[32,4096]{1,0:T(8,128)(2,1)S(1)} collective-permute-done((bf16[32,4096]{1,0:T(8,128)(2,1)S(1)}, bf16[32,4096]{1,0:T(8,128)(2,1)S(1)}, u32[]{:S(2)}, u32[]{:S(2)}) %collective-permute-start.50) | collective-permute-done | bytes 262176 | tf_op jit(solution)/shard_map/ppermute | solution.py:806
  959.7 9.1 shard_map.282
  968.9 6.9 shard_map.283
  989.8 6.9 shard_map.284
  996.7 6.7 shard_map.285
  (519 shorter events, 303.9 us)
Async XLA Ops:
  7.2 195.3 %all-gather.8.cloned.1.call-start = ((), (), s32[]{:S(2)}) async-start(), calls=%async_computation.6 | async-start | bytes 8650752 | tf_op jit(solution)/shard_map/all_gather | solution.py:1143
  8.9 254.9 %all-gather.10.cloned.1.call-start = ((), (), s32[]{:S(2)}) async-start(), calls=%async_computation.7 | async-start | bytes 15138816 | tf_op jit(solution)/shard_map/all_gather | solution.py:1143
  14.1 310.8 %all-gather.14.cloned.1.call-start = ((), (), s32[]{:S(2)}) async-start(), calls=%async_computation.15 | async-start | bytes 8650752 | tf_op jit(solution)/shard_map/all_gather | solution.py:1143
  14.2 37.7 %collective-permute-start.2 = (bf16[32,4096]{1,0:T(8,128)(2,1)S(1)}, bf16[32,4096]{1,0:T(8,128)(2,1)S(1)}, u32[]{:S(2)}, u32[]{:S(2)}) collective-permute-start(bf16[32,4096]{1,0:T(8,128)(2,1)S(1)} %dynamic-slice_bitcast_fusion.16), channel_id=1, source_target_pairs={{0,6},{2,0},{4,2},{6,4},{1,7},{3,1},{5,3},{7,5},{8,14},{10,8},{12,... | collective-permute-start | bytes 786440 | tf_op jit(solution)/shard_map/ppermute | solution.py:806
  19.3 32.6 %collective-permute-start.1 = (bf16[32,4096]{1,0:T(8,128)(2,1)S(1)}, bf16[32,4096]{1,0:T(8,128)(2,1)S(1)}, u32[]{:S(2)}, u32[]{:S(2)}) collective-permute-start(bf16[32,4096]{1,0:T(8,128)(2,1)S(1)} %dynamic-slice_bitcast_fusion.16), channel_id=1, source_target_pairs={{0,4},{2,6},{4,0},{6,2},{1,5},{3,7},{5,1},{7,3},{8,12},{10,14},{12... | collective-permute-start | bytes 786440 | tf_op jit(solution)/shard_map/ppermute | solution.py:806
  19.3 32.7 %collective-permute-start = (bf16[32,4096]{1,0:T(8,128)(2,1)S(1)}, bf16[32,4096]{1,0:T(8,128)(2,1)S(1)}, u32[]{:S(2)}, u32[]{:S(2)}) collective-permute-start(bf16[32,4096]{1,0:T(8,128)(2,1)S(1)} %dynamic-slice_bitcast_fusion.16), channel_id=1, source_target_pairs={{0,2},{2,4},{4,6},{6,0},{1,3},{3,5},{5,7},{7,1},{8,10},{10,12},{12... | collective-permute-start | bytes 786440 | tf_op jit(solution)/shard_map/ppermute | solution.py:806
  28.9 21.4 %collective-permute-start.12 = (bf16[64,256]{1,0:T(8,128)(2,1)S(1)}, bf16[64,256]{1,0:T(8,128)(2,1)S(1)}, u32[]{:S(2)}, u32[]{:S(2)}) collective-permute-start(bf16[64,256]{1,0:T(8,128)(2,1)S(1)} %reshape.268), channel_id=1, source_target_pairs={{0,4},{2,6},{4,0},{6,2},{1,5},{3,7},{5,1},{7,3},{8,12},{10,14},{12... | collective-permute-start | bytes 98312 | tf_op jit(solution)/shard_map/ppermute | solution.py:806
  34.9 437.4 %reduce-scatter.7.cloned.1.call-start = ((), (), s32[]{:S(2)}) async-start(), calls=%async_computation.8 | async-start | bytes 9437184 | tf_op jit(solution)/shard_map/reduce_scatter | solution.py:1147
  50.3 40.7 %collective-permute-start.10 = (bf16[512,1024]{1,0:T(8,128)(2,1)}, bf16[512,1024]{1,0:T(8,128)(2,1)S(1)}, u32[]{:S(2)}, u32[]{:S(2)}) collective-permute-start(bf16[512,1024]{1,0:T(8,128)(2,1)} %dynamic-slice_bitcast_fusion.5), channel_id=1, source_target_pairs={{0,1},{1,0},{2,3},{3,2},{4,5},{5,4},{6,7},{7,6},{8,9},{9,8},{10,11... | collective-permute-start | bytes 3145736 | tf_op jit(solution)/shard_map/ppermute | solution.py:806
  56.7 33.4 %collective-permute-start.8 = (bf16[128,1024]{1,0:T(8,128)(2,1)}, bf16[128,1024]{1,0:T(8,128)(2,1)S(1)}, u32[]{:S(2)}, u32[]{:S(2)}) collective-permute-start(bf16[128,1024]{1,0:T(8,128)(2,1)} %dynamic-slice_bitcast_fusion.17), channel_id=1, source_target_pairs={{0,4},{2,6},{4,0},{6,2},{1,5},{3,7},{5,1},{7,3},{8,12},{10,14},{12... | collective-permute-start | bytes 786440 | tf_op jit(solution)/shard_map/ppermute | solution.py:806
  57.5 32.7 %collective-permute-start.7 = (bf16[128,1024]{1,0:T(8,128)(2,1)}, bf16[128,1024]{1,0:T(8,128)(2,1)S(1)}, u32[]{:S(2)}, u32[]{:S(2)}) collective-permute-start(bf16[128,1024]{1,0:T(8,128)(2,1)} %dynamic-slice_bitcast_fusion.17), channel_id=1, source_target_pairs={{0,2},{2,4},{4,6},{6,0},{1,3},{3,5},{5,7},{7,1},{8,10},{10,12},{12... | collective-permute-start | bytes 786440 | tf_op jit(solution)/shard_map/ppermute | solution.py:806
  66.0 22.5 %collective-permute-start.5 = (bf16[3,16,4096]{2,1,0:T(8,128)(2,1)S(1)}, bf16[3,16,4096]{2,1,0:T(8,128)(2,1)S(1)}, u32[]{:S(2)}, u32[]{:S(2)}) collective-permute-start(bf16[3,16,4096]{2,1,0:T(8,128)(2,1)S(1)} %get-tuple-element.111), channel_id=1, source_target_pairs={{0,1},{1,0},{2,3},{3,2},{4,5},{5,4},{6,7},{7,6},{8,9},{9,8},{10,11... | collective-permute-start | bytes 1179656 | tf_op jit(solution)/shard_map/ppermute | solution.py:801
  69.7 48.0 %collective-permute-start.4 = (bf16[2,3,16,4096]{3,2,1,0:T(8,128)(2,1)S(1)}, bf16[2,3,16,4096]{3,2,1,0:T(8,128)(2,1)S(1)}, u32[]{:S(2)}, u32[]{:S(2)}) collective-permute-start(bf16[2,3,16,4096]{3,2,1,0:T(8,128)(2,1)S(1)} %pad_maximum_fusion.5.refs_0_), channel_id=1, source_target_pairs={{0,1},{1,0},{2,3},{3,2},{4,5},{5,4},{6,7},{7,6},{8,9},{9,8},{10,11... | collective-permute-start | bytes 2359304 | tf_op jit(solution)/shard_map/ppermute | solution.py:801
  88.6 30.7 %collective-permute-start.6 = (bf16[2,3,16,4096]{3,2,1,0:T(8,128)(2,1)S(1)}, bf16[2,3,16,4096]{3,2,1,0:T(8,128)(2,1)S(1)}, u32[]{:S(2)}, u32[]{:S(2)}) collective-permute-start(bf16[2,3,16,4096]{3,2,1,0:T(8,128)(2,1)S(1)} %pad_maximum_fusion.6.refs_2_), channel_id=1, source_target_pairs={{0,16},{8,24},{16,0},{24,8},{1,17},{9,25},{17,1},{25,9},{2,18},{10... | collective-permute-start | bytes 2359304 | tf_op jit(solution)/shard_map/ppermute | solution.py:801
  121.4 29.7 %collective-permute-start.14 = (bf16[2,3,16,4096]{3,2,1,0:T(8,128)(2,1)S(1)}, bf16[2,3,16,4096]{3,2,1,0:T(8,128)(2,1)}, u32[]{:S(2)}, u32[]{:S(2)}) collective-permute-start(bf16[2,3,16,4096]{3,2,1,0:T(8,128)(2,1)S(1)} %pad_maximum_fusion.5.refs_0_), channel_id=1, source_target_pairs={{0,8},{8,0},{16,24},{24,16},{1,9},{9,1},{17,25},{25,17},{2,10},{10... | collective-permute-start | bytes 2359304 | tf_op jit(solution)/shard_map/ppermute | solution.py:801
  121.4 30.1 %collective-permute-start.15 = (bf16[2,3,16,4096]{3,2,1,0:T(8,128)(2,1)}, bf16[2,3,16,4096]{3,2,1,0:T(8,128)(2,1)}, u32[]{:S(2)}, u32[]{:S(2)}) collective-permute-start(bf16[2,3,16,4096]{3,2,1,0:T(8,128)(2,1)} %copy-done.32), channel_id=1, source_target_pairs={{0,8},{8,0},{16,24},{24,16},{1,9},{9,1},{17,25},{25,17},{2,10},{10... | collective-permute-start | bytes 2359304 | tf_op jit(solution)/shard_map/ppermute | solution.py:801
  122.0 29.6 %collective-permute-start.16 = (bf16[2,3,16,4096]{3,2,1,0:T(8,128)(2,1)}, bf16[2,3,16,4096]{3,2,1,0:T(8,128)(2,1)}, u32[]{:S(2)}, u32[]{:S(2)}) collective-permute-start(bf16[2,3,16,4096]{3,2,1,0:T(8,128)(2,1)} %copy-done.25), channel_id=1, source_target_pairs={{0,8},{8,0},{16,24},{24,16},{1,9},{9,1},{17,25},{25,17},{2,10},{10... | collective-permute-start | bytes 2359304 | tf_op jit(solution)/shard_map/ppermute | solution.py:801
  122.0 29.6 %collective-permute-start.17 = (bf16[2,3,16,4096]{3,2,1,0:T(8,128)(2,1)}, bf16[2,3,16,4096]{3,2,1,0:T(8,128)(2,1)}, u32[]{:S(2)}, u32[]{:S(2)}) collective-permute-start(bf16[2,3,16,4096]{3,2,1,0:T(8,128)(2,1)} %copy-done.34), channel_id=1, source_target_pairs={{0,8},{8,0},{16,24},{24,16},{1,9},{9,1},{17,25},{25,17},{2,10},{10... | collective-permute-start | bytes 2359304 | tf_op jit(solution)/shard_map/ppermute | solution.py:801
  146.6 30.0 %collective-permute-start.19 = (bf16[2,3,64,1024]{3,2,1,0:T(8,128)(2,1)}, bf16[2,3,64,1024]{3,2,1,0:T(8,128)(2,1)}, u32[]{:S(2)}, u32[]{:S(2)}) collective-permute-start(bf16[2,3,64,1024]{3,2,1,0:T(8,128)(2,1)} %pad_maximum_fusion.7.refs_0_), channel_id=1, source_target_pairs={{0,1},{1,0},{2,3},{3,2},{4,5},{5,4},{6,7},{7,6},{8,9},{9,8},{10,11... | collective-permute-start | bytes 2359304 | tf_op jit(solution)/shard_map/ppermute | solution.py:801
  151.1 25.5 %collective-permute-start.21 = (bf16[2,3,64,1024]{3,2,1,0:T(8,128)(2,1)}, bf16[2,3,64,1024]{3,2,1,0:T(8,128)(2,1)}, u32[]{:S(2)}, u32[]{:S(2)}) collective-permute-start(bf16[2,3,64,1024]{3,2,1,0:T(8,128)(2,1)} %pad_maximum_fusion.8.refs_2_), channel_id=1, source_target_pairs={{0,16},{8,24},{16,0},{24,8},{1,17},{9,25},{17,1},{25,9},{2,18},{10... | collective-permute-start | bytes 2359304 | tf_op jit(solution)/shard_map/ppermute | solution.py:801
  324.8 25.5 %collective-permute-start.26 = (bf16[512,1024]{1,0:T(8,128)(2,1)}, bf16[512,1024]{1,0:T(8,128)(2,1)}, u32[]{:S(2)}, u32[]{:S(2)}) collective-permute-start(bf16[512,1024]{1,0:T(8,128)(2,1)} %dynamic-slice_bitcast_fusion.4), channel_id=1, source_target_pairs={{0,1},{1,0},{2,3},{3,2},{4,5},{5,4},{6,7},{7,6},{8,9},{9,8},{10,11... | collective-permute-start | bytes 3145736 | tf_op jit(solution)/shard_map/ppermute | solution.py:806
  369.2 227.3 %reduce-scatter.9.cloned.1.call-start = ((), (), s32[]{:S(2)}) async-start(), calls=%async_computation.9 | async-start | bytes 9437184 | tf_op jit(solution)/shard_map/reduce_scatter | solution.py:1147
  404.8 191.7 %reduce-scatter.11.cloned.1.call-start = ((), (), s32[]{:S(2)}) async-start(), calls=%async_computation.10 | async-start | bytes 7077888 | tf_op jit(solution)/shard_map/reduce_scatter | solution.py:1147
  472.4 228.1 %reduce-scatter.13.cloned.1.call-start = ((), (), s32[]{:S(2)}) async-start(), calls=%async_computation.11 | async-start | bytes 3604480 | tf_op jit(solution)/shard_map/reduce_scatter | solution.py:1157
  605.0 178.2 %reduce-scatter.15.cloned.1.call-start = ((), (), s32[]{:S(2)}) async-start(), calls=%async_computation.12 | async-start | bytes 9437184 | tf_op jit(solution)/shard_map/reduce_scatter | solution.py:1147
  607.5 65.1 %collective-permute-start.28 = (bf16[512,1024]{1,0:T(8,128)(2,1)}, bf16[512,1024]{1,0:T(8,128)(2,1)}, u32[]{:S(2)}, u32[]{:S(2)}) collective-permute-start(bf16[512,1024]{1,0:T(8,128)(2,1)} %constant_dynamic-slice_fusion.3), channel_id=1, source_target_pairs={{0,1},{1,0},{2,3},{3,2},{4,5},{5,4},{6,7},{7,6},{8,9},{9,8},{10,11... | collective-permute-start | bytes 3145736 | tf_op jit(solution)/shard_map/ppermute | solution.py:806
  672.5 21.6 %collective-permute-start.27 = (bf16[4,2,2,128,1024]{4,3,0,1,2:T(8,128)(2,1)}, bf16[4,2,2,128,1024]{4,3,0,1,2:T(8,128)(2,1)}, u32[]{:S(2)}, u32[]{:S(2)}) collective-permute-start(bf16[4,2,2,128,1024]{4,3,0,1,2:T(8,128)(2,1)} %bitcast.305), channel_id=1, source_target_pairs={{0,8},{1,9},{8,0},{9,1},{16,24},{17,25},{24,16},{25,17},{2,10},{3,... | collective-permute-start | bytes 12582920 | tf_op jit(solution)/shard_map/ppermute | solution.py:894
  674.8 230.1 %reduce-scatter.17.cloned.1.call-start = ((), (), s32[]{:S(2)}) async-start(), calls=%async_computation.13 | async-start | bytes 1310720 | tf_op jit(solution)/shard_map/reduce_scatter | solution.py:1157
  703.6 42.6 %collective-permute-start.29 = (bf16[4,2,64,1024]{3,2,0,1:T(8,128)(2,1)S(1)}, bf16[4,2,64,1024]{3,2,0,1:T(8,128)(2,1)S(1)}, u32[]{:S(2)}, u32[]{:S(2)}) collective-permute-start(bf16[4,2,64,1024]{3,2,0,1:T(8,128)(2,1)S(1)} %dynamic-slice_bitcast_fusion.3), channel_id=1, source_target_pairs={{0,16},{1,17},{8,24},{9,25},{16,0},{17,1},{24,8},{25,9},{2,18},{3,... | collective-permute-start | bytes 3145736 | tf_op jit(solution)/shard_map/ppermute | solution.py:894
  705.0 40.8 %collective-permute-start.30 = (bf16[4,2,64,1024]{3,2,0,1:T(8,128)(2,1)S(1)}, bf16[4,2,64,1024]{3,2,0,1:T(8,128)(2,1)S(1)}, u32[]{:S(2)}, u32[]{:S(2)}) collective-permute-start(bf16[4,2,64,1024]{3,2,0,1:T(8,128)(2,1)S(1)} %dynamic-slice_bitcast_fusion.2), channel_id=1, source_target_pairs={{0,1},{1,0},{8,9},{9,8},{16,17},{17,16},{24,25},{25,24},{2,3},{3,2... | collective-permute-start | bytes 3145736 | tf_op jit(solution)/shard_map/ppermute | solution.py:894
  760.1 16.7 %collective-permute-start.33 = (bf16[4,2,2,32,4096]{4,3,0,1,2:T(8,128)(2,1)}, bf16[4,2,2,32,4096]{4,3,0,1,2:T(8,128)(2,1)}, u32[]{:S(2)}, u32[]{:S(2)}) collective-permute-start(bf16[4,2,2,32,4096]{4,3,0,1,2:T(8,128)(2,1)} %bitcast.304), channel_id=1, source_target_pairs={{0,8},{1,9},{8,0},{9,1},{16,24},{17,25},{24,16},{25,17},{2,10},{3,... | collective-permute-start | bytes 12582920 | tf_op jit(solution)/shard_map/ppermute | solution.py:894
  785.5 174.2 %all-gather.16.cloned.1.call-start = ((), (), s32[]{:S(2)}) async-start(), calls=%async_computation.16 | async-start | bytes 6488064 | tf_op jit(solution)/shard_map/all_gather | solution.py:1161
  786.3 210.3 %all-gather.12.cloned.1.call-start = ((), (), s32[]{:S(2)}) async-start(), calls=%async_computation.14 | async-start | bytes 2359296 | tf_op jit(solution)/shard_map/all_gather | solution.py:1161
  791.8 48.9 %collective-permute-start.37 = (bf16[4,2,16,4096]{3,2,0,1:T(8,128)(2,1)}, bf16[4,2,16,4096]{3,2,0,1:T(8,128)(2,1)}, u32[]{:S(2)}, u32[]{:S(2)}) collective-permute-start(bf16[4,2,16,4096]{3,2,0,1:T(8,128)(2,1)} %dynamic-slice_bitcast_fusion.1), channel_id=1, source_target_pairs={{0,16},{1,17},{8,24},{9,25},{16,0},{17,1},{24,8},{25,9},{2,18},{3,... | collective-permute-start | bytes 3145736 | tf_op jit(solution)/shard_map/ppermute | solution.py:894
  804.9 30.1 %collective-permute-start.36 = (bf16[128,1024]{1,0:T(8,128)(2,1)S(1)}, bf16[128,1024]{1,0:T(8,128)(2,1)S(1)}, u32[]{:S(2)}, u32[]{:S(2)}) collective-permute-start(bf16[128,1024]{1,0:T(8,128)(2,1)S(1)} %get-tuple-element.283), channel_id=1, source_target_pairs={{0,6},{2,0},{4,2},{6,4},{1,7},{3,1},{5,3},{7,5},{8,14},{10,8},{12,... | collective-permute-start | bytes 786440 | tf_op jit(solution)/shard_map/ppermute | solution.py:806
  806.0 33.5 %collective-permute-start.35 = (bf16[128,1024]{1,0:T(8,128)(2,1)S(1)}, bf16[128,1024]{1,0:T(8,128)(2,1)S(1)}, u32[]{:S(2)}, u32[]{:S(2)}) collective-permute-start(bf16[128,1024]{1,0:T(8,128)(2,1)S(1)} %get-tuple-element.284), channel_id=1, source_target_pairs={{0,4},{2,6},{4,0},{6,2},{1,5},{3,7},{5,1},{7,3},{8,12},{10,14},{12... | collective-permute-start | bytes 786440 | tf_op jit(solution)/shard_map/ppermute | solution.py:806
  808.1 31.4 %collective-permute-start.34 = (bf16[128,1024]{1,0:T(8,128)(2,1)S(1)}, bf16[128,1024]{1,0:T(8,128)(2,1)S(1)}, u32[]{:S(2)}, u32[]{:S(2)}) collective-permute-start(bf16[128,1024]{1,0:T(8,128)(2,1)S(1)} %get-tuple-element.282), channel_id=1, source_target_pairs={{0,2},{2,4},{4,6},{6,0},{1,3},{3,5},{5,7},{7,1},{8,10},{10,12},{12... | collective-permute-start | bytes 786440 | tf_op jit(solution)/shard_map/ppermute | solution.py:806
  814.3 19.2 %collective-permute-start.44 = (f32[64,256]{1,0:T(8,128)S(1)}, f32[64,256]{1,0:T(8,128)S(1)}, u32[]{:S(2)}, u32[]{:S(2)}) collective-permute-start(f32[64,256]{1,0:T(8,128)S(1)} %get-tuple-element.285), channel_id=1, source_target_pairs={{0,2},{2,4},{4,6},{6,0},{1,3},{3,5},{5,7},{7,1},{8,10},{10,12},{12... | collective-permute-start | bytes 196616 | tf_op jit(solution)/shard_map/ppermute | solution.py:806
  833.5 36.6 %collective-permute-start.38 = (bf16[4,2,16,4096]{3,2,0,1:T(8,128)(2,1)S(1)}, bf16[4,2,16,4096]{3,2,0,1:T(8,128)(2,1)S(1)}, u32[]{:S(2)}, u32[]{:S(2)}) collective-permute-start(bf16[4,2,16,4096]{3,2,0,1:T(8,128)(2,1)S(1)} %dynamic-slice_bitcast_fusion), channel_id=1, source_target_pairs={{0,1},{1,0},{8,9},{9,8},{16,17},{17,16},{24,25},{25,24},{2,3},{3,2... | collective-permute-start | bytes 3145736 | tf_op jit(solution)/shard_map/ppermute | solution.py:894
  870.4 16.1 %collective-permute-start.41 = (bf16[128,1024]{1,0:T(8,128)(2,1)S(1)}, bf16[128,1024]{1,0:T(8,128)(2,1)S(1)}, u32[]{:S(2)}, u32[]{:S(2)}) collective-permute-start(bf16[128,1024]{1,0:T(8,128)(2,1)S(1)} %fusion.61), channel_id=1, source_target_pairs={{0,17},{1,16},{8,25},{9,24},{16,1},{17,0},{24,9},{25,8},{2,19},{3,... | collective-permute-start | bytes 786440 | tf_op jit(solution)/shard_map/ppermute | solution.py:894
  873.8 17.9 %collective-permute-start.40 = (bf16[128,1024]{1,0:T(8,128)(2,1)S(1)}, bf16[128,1024]{1,0:T(8,128)(2,1)S(1)}, u32[]{:S(2)}, u32[]{:S(2)}) collective-permute-start(bf16[128,1024]{1,0:T(8,128)(2,1)S(1)} %fusion.61), channel_id=1, source_target_pairs={{0,1},{1,0},{8,9},{9,8},{16,17},{17,16},{24,25},{25,24},{2,3},{3,2... | collective-permute-start | bytes 786440 | tf_op jit(solution)/shard_map/ppermute | solution.py:894
  873.8 17.9 %collective-permute-start.39 = (bf16[128,1024]{1,0:T(8,128)(2,1)S(1)}, bf16[128,1024]{1,0:T(8,128)(2,1)S(1)}, u32[]{:S(2)}, u32[]{:S(2)}) collective-permute-start(bf16[128,1024]{1,0:T(8,128)(2,1)S(1)} %fusion.61), channel_id=1, source_target_pairs={{0,16},{1,17},{8,24},{9,25},{16,0},{17,1},{24,8},{25,9},{2,18},{3,... | collective-permute-start | bytes 786440 | tf_op jit(solution)/shard_map/ppermute | solution.py:894
  874.4 26.7 %collective-permute-start.43 = (bf16[4,16,4096]{2,1,0:T(8,128)(2,1)S(1)}, bf16[4,16,4096]{2,1,0:T(8,128)(2,1)S(1)}, u32[]{:S(2)}, u32[]{:S(2)}) collective-permute-start(bf16[4,16,4096]{2,1,0:T(8,128)(2,1)S(1)} %dynamic-slice_bitcast_fusion.6), channel_id=1, source_target_pairs={{0,16},{1,17},{8,24},{9,25},{16,0},{17,1},{24,8},{25,9},{2,18},{3,... | collective-permute-start | bytes 1572872 | tf_op jit(solution)/shard_map/ppermute | solution.py:894
  875.9 28.0 %collective-permute-start.42 = (bf16[4,16,4096]{2,1,0:T(8,128)(2,1)S(1)}, bf16[4,16,4096]{2,1,0:T(8,128)(2,1)S(1)}, u32[]{:S(2)}, u32[]{:S(2)}) collective-permute-start(bf16[4,16,4096]{2,1,0:T(8,128)(2,1)S(1)} %dynamic-slice_bitcast_fusion.7), channel_id=1, source_target_pairs={{0,1},{1,0},{8,9},{9,8},{16,17},{17,16},{24,25},{25,24},{2,3},{3,2... | collective-permute-start | bytes 1572872 | tf_op jit(solution)/shard_map/ppermute | solution.py:894
  917.7 27.8 %collective-permute-start.50 = (bf16[32,4096]{1,0:T(8,128)(2,1)S(1)}, bf16[32,4096]{1,0:T(8,128)(2,1)S(1)}, u32[]{:S(2)}, u32[]{:S(2)}) collective-permute-start(bf16[32,4096]{1,0:T(8,128)(2,1)S(1)} %get-tuple-element.281), channel_id=1, source_target_pairs={{0,4},{2,6},{4,0},{6,2},{1,5},{3,7},{5,1},{7,3},{8,12},{10,14},{12... | collective-permute-start | bytes 786440 | tf_op jit(solution)/shard_map/ppermute | solution.py:806
  923.7 21.7 %collective-permute-start.49 = (bf16[32,4096]{1,0:T(8,128)(2,1)S(1)}, bf16[32,4096]{1,0:T(8,128)(2,1)S(1)}, u32[]{:S(2)}, u32[]{:S(2)}) collective-permute-start(bf16[32,4096]{1,0:T(8,128)(2,1)S(1)} %get-tuple-element.279), channel_id=1, source_target_pairs={{0,2},{2,4},{4,6},{6,0},{1,3},{3,5},{5,7},{7,1},{8,10},{10,12},{12... | collective-permute-start | bytes 786440 | tf_op jit(solution)/shard_map/ppermute | solution.py:806
  924.2 21.4 %collective-permute-start.48 = (bf16[4,128,1024]{2,1,0:T(8,128)(2,1)S(1)}, bf16[4,128,1024]{2,1,0:T(8,128)(2,1)S(1)}, u32[]{:S(2)}, u32[]{:S(2)}) collective-permute-start(bf16[4,128,1024]{2,1,0:T(8,128)(2,1)S(1)} %pad_maximum_fusion.2.near_ref), channel_id=1, source_target_pairs={{0,8},{1,9},{8,0},{9,1},{16,24},{17,25},{24,16},{25,17},{2,10},{3,... | collective-permute-start | bytes 3145736 | tf_op jit(solution)/shard_map/ppermute | solution.py:894
  949.3 36.4 %collective-permute-start.47 = (bf16[512,1024]{1,0:T(8,128)(2,1)S(1)}, bf16[512,1024]{1,0:T(8,128)(2,1)S(1)}, u32[]{:S(2)}, u32[]{:S(2)}) collective-permute-start(bf16[512,1024]{1,0:T(8,128)(2,1)S(1)} %constant_dynamic-slice_fusion), channel_id=1, source_target_pairs={{0,1},{1,0},{2,3},{3,2},{4,5},{5,4},{6,7},{7,6},{8,9},{9,8},{10,11... | collective-permute-start | bytes 3145736 | tf_op jit(solution)/shard_map/ppermute | solution.py:806
  (117 other events, 1858.4 us)
Sparse Core Ops, SparseCore 0:
  11.1 118.3 all-gather.7
  132.4 109.0 all-gather.9
  244.6 75.5 all-gather.13
  369.3 68.9 reduce-scatter.6
  442.0 71.2 reduce-scatter.8
  516.5 61.9 reduce-scatter.10
  605.1 53.3 reduce-scatter.12
  674.9 90.1 reduce-scatter.14
  785.6 33.7 reduce-scatter.16
  821.3 76.1 all-gather.15
  906.8 34.0 all-gather.11

commit v3 on v2

--- a/solution.py
+++ b/solution.py
@@ -1366,12 +1366,12 @@
     t_out0 = reduce_second(at, t_out0)
     t_in0 = reduce_cores(at, d_in0)
     grad_normed = right_t(lin_low, f_in0)
-    grad_normed, t_out0, t_in0, p_attn = tie((grad_normed, t_out0, t_in0, p_attn))
-    attn = to_replicas(reduce_groups(by_groups(p_attn)))
+    grad_normed, t_out0, t_in0 = tie((grad_normed, t_out0, t_in0))
     t_out0 = reduce_along(at, t_out0)
     t_in0 = reduce_first(at, t_in0)
     grad_start, start_low, sums_zero = norm_bwd(values, grad_normed, gains[0], shifts[0], grad_first)
-    start_low, t_out0, t_in0 = tie((start_low, t_out0, t_in0))
+    start_low, t_out0, t_in0, p_attn = tie((start_low, t_out0, t_in0, p_attn))
+    attn = to_replicas(reduce_groups(by_groups(p_attn)))
 
     sums = [sums_zero, sums_one, sums_two, sums_three, sums_four, sums_five]
     small = split_small(
@@ -1388,17 +1388,16 @@
     )
     near = spread_plane(t_out0)
     t_in0 = reduce_second(at, t_in0)
-    small = reduce_planes(small)
     near, t_in0, start_low, small = tie((near, t_in0, start_low, small))
     t_in0 = reduce_along(at, t_in0)
+    small = reduce_planes(small)
+    grad_start = swap_out(grad_start, micro, HIGH, start_low)
     far = across(near, CORE)
+    near, far, t_in0, small = tie((near, far, t_in0, small))
+    near_in = spread_plane(t_in0)
     small = sum_replicas(small)
-    grad_start = swap_out(grad_start, micro, HIGH, start_low)
-    far, t_in0, small = tie((far, t_in0, small))
-    near_in = spread_plane(t_in0)
     grad_out, grad_in, g_conv = turn_early(early, width, lin_low.shape[1])
     grad_out = finish_first(at, near, far, grad_out)
-    near_in, grad_out = tie((near_in, grad_out))
     grad_in = finish_first(at, near_in, across(near_in, CORE), grad_in)
     g_qkv, g_o = turn_attn(attn, width)
     shapes = [(6, shard), (6, shard), (2, 4 * shard), (2, shard), (3, shard), (KERNEL, shard), (LEFT + RIGHT + 1, HD // groups)]

time: 1020 us -> 997 us (0.977)
  starting transfers between devices: 94.4 us -> 78 us
  waiting for transfers between devices: 211 us -> 200 us
    ppermute x22, starting transfers between devices: 53.5 us -> 39.3 us  [ring(): lax.ppermute(value, axis, [(i, (i + steps) % count) for i in range(count)])]
    unnamed x210 -> x220, local copies, waits for them, and re-layouts: 29.6 us -> 34.3 us
  transfers between devices with their start and end apart: 74 -> 74, of which waited for: 30 -> 28; matrix products, arithmetic and copies ran while one was open for 35% -> 35% of each run, Pallas kernels for 28% -> 28%
where the time goes in v3:
time: 997 us; the launch traced here: 990 us
  Pallas kernels  291 us (29%)
  matrix products  239 us (24%)
  waiting for transfers between devices  200 us (20%)
  local copies, waits for them, and re-layouts  127 us (13%)
  starting transfers between devices  78 us (8%)
  other arithmetic  39.6 us (4%)
  between operations  16 us (2%)
    pallas_call x1, Pallas kernels, attn_backward_call(): pl.pallas_call(attn_bwd_kernel, grid=(pairs,), in_specs=[col(0), col(1),...  99.4 us
    dot_general x8, matrix products, right_t(): lax.dot_general(left, right, (((1,), (1,)), ((), ())), preferred_element_...  94 us
    dot_general x8, matrix products, matmul(): return jnp.dot(left, right, preferred_element_type=HIGH)  90.5 us
    ppermute x25, waiting for transfers between devices, across(): return lax.ppermute(value, REPLICAS, [(i, i ^ flip) for i in range(pieces)])  89.2 us
    ppermute x16, waiting for transfers between devices, hop(): lax.ppermute(value, axis, [(i, i ^ flip) for i in range(lax.axis_size(axi...  61.1 us
    dot_general x4, matrix products, left_t(): lax.dot_general(left, right, (((0,), (0,)), ((), ())), preferred_element_...  54.3 us
    ppermute x22, waiting for transfers between devices, ring(): lax.ppermute(value, axis, [(i, (i + steps) % count) for i in range(count)])  49.1 us
    ppermute x22, starting transfers between devices, ring(): lax.ppermute(value, axis, [(i, (i + steps) % count) for i in range(count)])  39.3 us
  transfers between devices with their start and end apart: 74, of which 28 were waited for; matrix products, arithmetic and copies ran while one was open for 35% of the time, Pallas kernels for 28%

profile of v3, /device:TPU:0, one launch (start us, length us, event | category | flops | bytes accessed | tf_op | source)
XLA Modules:
  0.0 989.8 jit_solution(9402927019253086238)
XLA Ops:
  41.0 9.3 collective-permute-start.13
  57.5 8.6 collective-permute-done.9
  71.3 17.2 %collective-permute-done.5 = bf16[3,16,4096]{2,1,0:T(8,128)(2,1)S(1)} collective-permute-done((bf16[3,16,4096]{2,1,0:T(8,128)(2,1)S(1)}, bf16[3,16,4096]{2,1,0:T(8,128)(2,1)S(1)}, u32[]{:S(2)}, u32[]{:S(2)}) %collective-permute-start.5) | collective-permute-done | bytes 393248 | tf_op jit(solution)/shard_map/ppermute | solution.py:801
  91.1 26.5 %collective-permute-done.4.refs_1_ = bf16[2,3,16,4096]{3,2,1,0:T(8,128)(2,1)S(1)} collective-permute-done((bf16[2,3,16,4096]{3,2,1,0:T(8,128)(2,1)S(1)}, bf16[2,3,16,4096]{3,2,1,0:T(8,128)(2,1)S(1)}, u32[]{:S(2)}, u32[]{:S(2)}) %collective-permute-start.4) | collective-permute-done | bytes 786464 | tf_op jit(solution)/shard_map/ppermute | solution.py:801
  124.5 9.3 collective-permute-done.18
  155.0 7.4 shard_map.263
  162.4 14.2 %add_convert_fusion.1 = (bf16[1024,4096]{1,0:T(8,128)(2,1)}, bf16[1024,4096]{1,0:T(8,128)(2,1)}) fusion(f32[4096]{0:T(1024)S(1)} %bitcast.388, bf16[1024,1024]{1,0:T(8,128)(2,1)S(1)} %copy-done.72, bf16[1024,4096]{1,0:T(8,128)(2,1)S(1)} %shard_map.263), kind=kOutput, calls=%fused_computation.19 | convolution fusion | flops 8619294720 | bytes 27279360 | tf_op jit(solution)/shard_map/dot_general | solution.py:40
  187.2 10.4 %multiply_add_fusion.1.x_ref = f32[1024,1024]{1,0:T(8,128)} fusion(bf16[1024,1024]{1,0:T(8,128)(2,1)S(1)} %copy-done.2, f32[1024]{0:T(1024)S(1)} %bitcast.395, bf16[1024,4096]{1,0:T(8,128)(2,1)S(1)} %bitcast.400, bf16[4096,1024]{1,0:T(8,128)(2,1)S(1)} %shard_map.264), kind=kOutput, calls=%fused_computation.59 | convolution fusion | flops 8594128896 | bytes 23072768 | tf_op jit(solution)/shard_map/dot_general | solution.py:40
  202.5 9.5 add_convert_fusion.2.q_ref.k_ref.v_ref
  212.0 39.3 %shard_map.266 = (bf16[1024,1024]{1,0:T(8,128)(2,1)S(1)}, f32[1024,1024]{1,0:T(8,128)S(1)}) custom-call(bf16[1024,3072]{1,0:T(8,128)(2,1)S(1)} %add_convert_fusion.2.q_ref.k_ref.v_ref, bf16[1024,3072]{1,0:T(8,128)(2,1)S(1)} %add_convert_fusion.2.q_ref.k_ref.v_ref, bf16[1024,3072]{1,0:T(8,128)(2,1)S(1)} %add_convert_fusion.2.q_ref.k_ref.v_ref, ...), custom_call_target="tpu_custom_call" | custom-call | flops 17179869184 | bytes 12582912 | tf_op jit(solution)/shard_map/pallas_call | solution.py:563
  251.3 7.5 add_add_fusion.x_ref
  263.6 9.4 fusion.86
  275.6 13.3 %shard_map.268.x_ref = f32[1024,1024]{1,0:T(8,128)} custom-call(bf16[1024,1024]{1,0:T(8,128)(2,1)} %fusion.37.u_ref, f32[31,1024]{1,0:T(8,128)} %bitcast.354), custom_call_target="tpu_custom_call" | custom-call | flops 65011712 | bytes 6291456 | tf_op jit(solution)/shard_map/pallas_call | solution.py:740
  293.9 7.8 convolution_add_fusion.x_ref
  306.6 17.4 %add_convert_fusion = (bf16[1024,4096]{1,0:T(8,128)(2,1)}, bf16[1024,4096]{1,0:T(8,128)(2,1)}) fusion(f32[4096]{0:T(1024)S(1)} %bitcast.387, bf16[1024,1024]{1,0:T(8,128)(2,1)} %shard_map.270, bf16[1024,7168]{1,0:T(8,128)(2,1)} %all-gather.10.cloned.1.call-done), kind=kOutput, calls=%fused_computation.18 | convolution fusion | flops 8619294720 | bytes 27279360 | tf_op jit(solution)/shard_map/dot_general | solution.py:40
  325.2 14.4 %multiply_add_fusion.x_ref = f32[1024,1024]{1,0:T(8,128)S(1)} fusion(f32[1024,1024]{1,0:T(8,128)} %convolution_add_fusion.x_ref, bf16[1024,4096]{1,0:T(8,128)(2,1)} %get-tuple-element.130, bf16[1,4096,1024]{2,1,0:T(8,128)(2,1)} %all-gather.14.cloned.1.call-done, f32[1024]{0:T(1024)S(1)} %bitcast.394), kind=kOutput, calls=%fused_computation.57 | convolution fusion | flops 8593080320 | bytes 25169920 | tf_op jit(solution)/shard_map/dot_general | solution.py:40
  340.0 10.7 %collective-permute-done.26 = bf16[512,1024]{1,0:T(8,128)(2,1)} collective-permute-done((bf16[512,1024]{1,0:T(8,128)(2,1)}, bf16[512,1024]{1,0:T(8,128)(2,1)}, u32[]{:S(2)}, u32[]{:S(2)}) %collective-permute-start.26) | collective-permute-done | bytes 1048608 | tf_op jit(solution)/shard_map/ppermute | solution.py:806
  358.0 11.5 %convolution_convert_fusion.3 = bf16[1024,4096]{1,0:T(8,128)(2,1)} fusion(bf16[1024,1024]{1,0:T(8,128)(2,1)S(1)} %get-tuple-element.133, bf16[1024,4096]{1,0:T(8,128)(2,1)S(1)} %bitcast.398), kind=kOutput, calls=%fused_computation.31 | convolution fusion | flops 8594128896 | bytes 18874368 | tf_op jit(solution)/shard_map/dot_general | solution.py:44
  369.6 20.2 %fusion.70 = (f32[4096]{0:T(1024)}, bf16[1024,4096]{1,0:T(8,128)(2,1)}) fusion(bf16[1024,4096]{1,0:T(8,128)(2,1)} %get-tuple-element.134, bf16[1024,1024]{1,0:T(8,128)(2,1)S(1)} %get-tuple-element.133, bf16[1,4096,1024]{2,1,0:T(8,128)(2,1)} %all-gather.14.cloned.1.call-done), kind=kOutput, calls=%fused_computation.216 | convolution fusion | flops 8636067840 | bytes 27279360 | tf_op jit(solution)/shard_map/dot_general | solution.py:48
  389.9 15.3 %convolution_convert_fusion.2 = bf16[4096,1024]{1,0:T(8,128)(2,1)} fusion(bf16[1024,4096]{1,0:T(8,128)(2,1)} %get-tuple-element.135, bf16[1024,1024]{1,0:T(8,128)(2,1)S(1)} %copy-done.74), kind=kOutput, calls=%fused_computation.30 | convolution fusion | flops 8594128896 | bytes 18874368 | tf_op jit(solution)/shard_map/dot_general | solution.py:44
  405.3 13.5 %fusion.17.grad_ref = f32[1024,1024]{1,0:T(8,128)S(1)} fusion(bf16[1024,4096]{1,0:T(8,128)(2,1)} %get-tuple-element.135, bf16[1024,7168]{1,0:T(8,128)(2,1)} %all-gather.10.cloned.1.call-done), kind=kOutput, calls=%fused_computation.32 | convolution fusion | flops 8589934592 | bytes 20971520 | tf_op jit(solution)/shard_map/dot_general | solution.py:48
  422.9 5.8 fusion.47.grad_ref
  428.8 5.6 shard_map.273
  436.5 22.3 %shard_map.274 = (bf16[2,1024,1024]{2,1,0:T(8,128)(2,1)}, f32[31,1024]{1,0:T(8,128)}) custom-call(f32[1024,1024]{1,0:T(8,128)} %copy-done.14, bf16[1024,1024]{1,0:T(8,128)(2,1)} %fusion.37.u_ref, bf16[1024,2048]{1,0:T(8,128)(2,1)} %get-tuple-element.139.pre_a_ref.pre_b_ref, bf16[1024,2048]{1,0:T(8,128)(2,1)} %get-tuple-element.139.pre_a_ref.pre_b_ref, ...), custom_call_target="tpu_custom_call" | custom-call | flops 130023424 | bytes 14680064 | tf_op jit(solution)/shard_map/pallas_call | solution.py:781
  464.3 8.4 shard_map.275
  480.9 6.5 fusion.33.grad_ref
  491.6 5.7 convolution_convert_fusion.4.do_ref
  497.3 99.4 %shard_map.277 = (bf16[3,1024,1024]{2,1,0:T(8,128)(2,1)}, f32[128,1024]{1,0:T(8,128)S(1)}, f32[8,1024]{1,0:T(8,128)S(1)}) custom-call(bf16[1024,3072]{1,0:T(8,128)(2,1)} %copy-done.58, bf16[1024,3072]{1,0:T(8,128)(2,1)} %copy-done.58, bf16[1024,3072]{1,0:T(8,128)(2,1)} %copy-done.58, bf16[1024,1024]{1,0:T(8,128)(2,1)S(1)} %copy-done.56, ...), custom_call_target="tpu_custom_call" | custom-call | flops 42949672960 | bytes 25165824 | tf_op jit(solution)/shard_map/pallas_call | solution.py:676
  614.3 11.2 %shard_map.278 = bf16[4096,1024]{1,0:T(8,128)(2,1)} custom-call(bf16[3,1024,1024]{2,1,0:T(8,128)(2,1)S(1)} %copy-done.13, bf16[1024,1024]{1,0:T(8,128)(2,1)S(1)} %copy-done.52, bf16[1024,1024]{1,0:T(8,128)(2,1)S(1)} %copy-done.27, bf16[1024,1024]{1,0:T(8,128)(2,1)S(1)} %copy-done.57), custom_call_target="tpu_custom_call" | custom-call | flops 8589934592 | bytes 20971520 | tf_op jit(solution)/shard_map/pallas_call | solution.py:1126
  625.6 5.6 slice_bitcast_fusion.2
  631.2 10.6 %fusion.21.grad_ref = f32[1024,1024]{1,0:T(8,128)S(1)} fusion(bf16[1024,1024]{1,0:T(8,128)(2,1)} %get-tuple-element.263, bf16[1024,1024]{1,0:T(8,128)(2,1)} %get-tuple-element.264, bf16[1024,1024]{1,0:T(8,128)(2,1)S(1)} %get-tuple-element.262, bf16[1024,4096]{1,0:T(8,128)(2,1)} %all-gather.8.cloned.1.call-done), kind=kOutput, calls=%fused_computation.36 | convolution fusion | flops 6461325312 | bytes 16777216 | tf_op jit(solution)/shard_map/dot_general | solution.py:48
  646.2 16.1 %convolution_convert_fusion.1 = bf16[4096,1024]{1,0:T(8,128)(2,1)} fusion(bf16[1024,4096]{1,0:T(8,128)(2,1)} %get-tuple-element.121, bf16[1024,1024]{1,0:T(8,128)(2,1)S(1)} %get-tuple-element.157), kind=kOutput, calls=%fused_computation.29 | convolution fusion | flops 8594128896 | bytes 18874368 | tf_op jit(solution)/shard_map/dot_general | solution.py:44
  662.3 6.9 constant_dynamic-slice_fusion.5
  674.3 19.1 %fusion.69 = (f32[4096]{0:T(1024)S(1)}, bf16[1024,4096]{1,0:T(8,128)(2,1)}) fusion(bf16[1024,4096]{1,0:T(8,128)(2,1)} %get-tuple-element.158, bf16[1024,1024]{1,0:T(8,128)(2,1)S(1)} %get-tuple-element.157, bf16[4096,1024]{1,0:T(8,128)(2,1)} %copy-done.12), kind=kOutput, calls=%fused_computation.215 | convolution fusion | flops 8636067840 | bytes 27279360 | tf_op jit(solution)/shard_map/dot_general | solution.py:48
  693.4 6.3 fusion.13
  707.1 11.4 %convolution_convert_fusion = bf16[1024,4096]{1,0:T(8,128)(2,1)} fusion(bf16[1024,1024]{1,0:T(8,128)(2,1)S(1)} %copy-done.73, bf16[1024,4096]{1,0:T(8,128)(2,1)S(1)} %copy-done.89), kind=kOutput, calls=%fused_computation.28 | convolution fusion | flops 8594128896 | bytes 18874368 | tf_op jit(solution)/shard_map/dot_general | solution.py:44
  718.4 27.1 %collective-permute-done.30 = bf16[4,2,64,1024]{3,2,0,1:T(8,128)(2,1)S(1)} collective-permute-done((bf16[4,2,64,1024]{3,2,0,1:T(8,128)(2,1)S(1)}, bf16[4,2,64,1024]{3,2,0,1:T(8,128)(2,1)S(1)}, u32[]{:S(2)}, u32[]{:S(2)}) %collective-permute-start.30) | collective-permute-done | bytes 1048608 | tf_op jit(solution)/shard_map/ppermute | solution.py:894
  748.3 7.2 constant_dynamic-slice_fusion.2
  760.5 12.6 %fusion.87.grad_ref = f32[1024,1024]{1,0:T(8,128)} fusion(bf16[1024,4096]{1,0:T(8,128)(2,1)} %get-tuple-element.164, bf16[1024,4096]{1,0:T(8,128)(2,1)S(1)} %bitcast.314), kind=kOutput, calls=%fused_computation.233 | convolution fusion | flops 8589934592 | bytes 20971520 | tf_op jit(solution)/shard_map/dot_general | solution.py:48
  807.6 7.0 collective-permute-done.35
  840.0 7.0 collective-permute-done.43
  863.1 21.5 %collective-permute-done.50 = f32[64,256]{1,0:T(8,128)S(1)} collective-permute-done((f32[64,256]{1,0:T(8,128)S(1)}, f32[64,256]{1,0:T(8,128)S(1)}, u32[]{:S(2)}, u32[]{:S(2)}) %collective-permute-start.50) | collective-permute-done | bytes 65568 | tf_op jit(solution)/shard_map/ppermute | solution.py:806
  891.8 6.6 collective-permute-done.61
  898.4 29.1 %collective-permute-done.60 = bf16[32,4096]{1,0:T(8,128)(2,1)S(1)} collective-permute-done((bf16[32,4096]{1,0:T(8,128)(2,1)S(1)}, bf16[32,4096]{1,0:T(8,128)(2,1)S(1)}, u32[]{:S(2)}, u32[]{:S(2)}) %collective-permute-start.60) | collective-permute-done | bytes 262176 | tf_op jit(solution)/shard_map/ppermute | solution.py:894
  947.4 8.8 shard_map.282
  961.6 6.9 shard_map.284
  969.4 6.9 shard_map.283
  976.3 6.7 shard_map.285
  (529 shorter events, 293.1 us)
Async XLA Ops:
  7.2 195.3 %all-gather.8.cloned.1.call-start = ((), (), s32[]{:S(2)}) async-start(), calls=%async_computation.6 | async-start | bytes 8650752 | tf_op jit(solution)/shard_map/all_gather | solution.py:1143
  8.9 254.7 %all-gather.10.cloned.1.call-start = ((), (), s32[]{:S(2)}) async-start(), calls=%async_computation.7 | async-start | bytes 15138816 | tf_op jit(solution)/shard_map/all_gather | solution.py:1143
  14.1 311.1 %all-gather.14.cloned.1.call-start = ((), (), s32[]{:S(2)}) async-start(), calls=%async_computation.15 | async-start | bytes 8650752 | tf_op jit(solution)/shard_map/all_gather | solution.py:1143
  14.2 37.7 %collective-permute-start.2 = (bf16[32,4096]{1,0:T(8,128)(2,1)S(1)}, bf16[32,4096]{1,0:T(8,128)(2,1)S(1)}, u32[]{:S(2)}, u32[]{:S(2)}) collective-permute-start(bf16[32,4096]{1,0:T(8,128)(2,1)S(1)} %dynamic-slice_bitcast_fusion.16), channel_id=1, source_target_pairs={{0,6},{2,0},{4,2},{6,4},{1,7},{3,1},{5,3},{7,5},{8,14},{10,8},{12,... | collective-permute-start | bytes 786440 | tf_op jit(solution)/shard_map/ppermute | solution.py:806
  19.3 32.6 %collective-permute-start.1 = (bf16[32,4096]{1,0:T(8,128)(2,1)S(1)}, bf16[32,4096]{1,0:T(8,128)(2,1)S(1)}, u32[]{:S(2)}, u32[]{:S(2)}) collective-permute-start(bf16[32,4096]{1,0:T(8,128)(2,1)S(1)} %dynamic-slice_bitcast_fusion.16), channel_id=1, source_target_pairs={{0,4},{2,6},{4,0},{6,2},{1,5},{3,7},{5,1},{7,3},{8,12},{10,14},{12... | collective-permute-start | bytes 786440 | tf_op jit(solution)/shard_map/ppermute | solution.py:806
  19.3 32.6 %collective-permute-start = (bf16[32,4096]{1,0:T(8,128)(2,1)S(1)}, bf16[32,4096]{1,0:T(8,128)(2,1)S(1)}, u32[]{:S(2)}, u32[]{:S(2)}) collective-permute-start(bf16[32,4096]{1,0:T(8,128)(2,1)S(1)} %dynamic-slice_bitcast_fusion.16), channel_id=1, source_target_pairs={{0,2},{2,4},{4,6},{6,0},{1,3},{3,5},{5,7},{7,1},{8,10},{10,12},{12... | collective-permute-start | bytes 786440 | tf_op jit(solution)/shard_map/ppermute | solution.py:806
  28.9 21.3 %collective-permute-start.12 = (bf16[64,256]{1,0:T(8,128)(2,1)S(1)}, bf16[64,256]{1,0:T(8,128)(2,1)S(1)}, u32[]{:S(2)}, u32[]{:S(2)}) collective-permute-start(bf16[64,256]{1,0:T(8,128)(2,1)S(1)} %reshape.268), channel_id=1, source_target_pairs={{0,4},{2,6},{4,0},{6,2},{1,5},{3,7},{5,1},{7,3},{8,12},{10,14},{12... | collective-permute-start | bytes 98312 | tf_op jit(solution)/shard_map/ppermute | solution.py:806
  35.0 437.8 %reduce-scatter.7.cloned.1.call-start = ((), (), s32[]{:S(2)}) async-start(), calls=%async_computation.8 | async-start | bytes 9437184 | tf_op jit(solution)/shard_map/reduce_scatter | solution.py:1147
  50.2 40.8 %collective-permute-start.10 = (bf16[512,1024]{1,0:T(8,128)(2,1)}, bf16[512,1024]{1,0:T(8,128)(2,1)S(1)}, u32[]{:S(2)}, u32[]{:S(2)}) collective-permute-start(bf16[512,1024]{1,0:T(8,128)(2,1)} %dynamic-slice_bitcast_fusion.5), channel_id=1, source_target_pairs={{0,1},{1,0},{2,3},{3,2},{4,5},{5,4},{6,7},{7,6},{8,9},{9,8},{10,11... | collective-permute-start | bytes 3145736 | tf_op jit(solution)/shard_map/ppermute | solution.py:806
  56.7 33.4 %collective-permute-start.8 = (bf16[128,1024]{1,0:T(8,128)(2,1)}, bf16[128,1024]{1,0:T(8,128)(2,1)S(1)}, u32[]{:S(2)}, u32[]{:S(2)}) collective-permute-start(bf16[128,1024]{1,0:T(8,128)(2,1)} %dynamic-slice_bitcast_fusion.17), channel_id=1, source_target_pairs={{0,4},{2,6},{4,0},{6,2},{1,5},{3,7},{5,1},{7,3},{8,12},{10,14},{12... | collective-permute-start | bytes 786440 | tf_op jit(solution)/shard_map/ppermute | solution.py:806
  57.5 32.7 %collective-permute-start.7 = (bf16[128,1024]{1,0:T(8,128)(2,1)}, bf16[128,1024]{1,0:T(8,128)(2,1)S(1)}, u32[]{:S(2)}, u32[]{:S(2)}) collective-permute-start(bf16[128,1024]{1,0:T(8,128)(2,1)} %dynamic-slice_bitcast_fusion.17), channel_id=1, source_target_pairs={{0,2},{2,4},{4,6},{6,0},{1,3},{3,5},{5,7},{7,1},{8,10},{10,12},{12... | collective-permute-start | bytes 786440 | tf_op jit(solution)/shard_map/ppermute | solution.py:806
  66.1 22.4 %collective-permute-start.5 = (bf16[3,16,4096]{2,1,0:T(8,128)(2,1)S(1)}, bf16[3,16,4096]{2,1,0:T(8,128)(2,1)S(1)}, u32[]{:S(2)}, u32[]{:S(2)}) collective-permute-start(bf16[3,16,4096]{2,1,0:T(8,128)(2,1)S(1)} %get-tuple-element.110), channel_id=1, source_target_pairs={{0,1},{1,0},{2,3},{3,2},{4,5},{5,4},{6,7},{7,6},{8,9},{9,8},{10,11... | collective-permute-start | bytes 1179656 | tf_op jit(solution)/shard_map/ppermute | solution.py:801
  69.7 47.9 %collective-permute-start.4 = (bf16[2,3,16,4096]{3,2,1,0:T(8,128)(2,1)S(1)}, bf16[2,3,16,4096]{3,2,1,0:T(8,128)(2,1)S(1)}, u32[]{:S(2)}, u32[]{:S(2)}) collective-permute-start(bf16[2,3,16,4096]{3,2,1,0:T(8,128)(2,1)S(1)} %pad_maximum_fusion.5.refs_0_), channel_id=1, source_target_pairs={{0,1},{1,0},{2,3},{3,2},{4,5},{5,4},{6,7},{7,6},{8,9},{9,8},{10,11... | collective-permute-start | bytes 2359304 | tf_op jit(solution)/shard_map/ppermute | solution.py:801
  88.6 30.6 %collective-permute-start.6 = (bf16[2,3,16,4096]{3,2,1,0:T(8,128)(2,1)S(1)}, bf16[2,3,16,4096]{3,2,1,0:T(8,128)(2,1)S(1)}, u32[]{:S(2)}, u32[]{:S(2)}) collective-permute-start(bf16[2,3,16,4096]{3,2,1,0:T(8,128)(2,1)S(1)} %pad_maximum_fusion.6.refs_2_), channel_id=1, source_target_pairs={{0,16},{8,24},{16,0},{24,8},{1,17},{9,25},{17,1},{25,9},{2,18},{10... | collective-permute-start | bytes 2359304 | tf_op jit(solution)/shard_map/ppermute | solution.py:801
  121.3 29.7 %collective-permute-start.14 = (bf16[2,3,16,4096]{3,2,1,0:T(8,128)(2,1)S(1)}, bf16[2,3,16,4096]{3,2,1,0:T(8,128)(2,1)}, u32[]{:S(2)}, u32[]{:S(2)}) collective-permute-start(bf16[2,3,16,4096]{3,2,1,0:T(8,128)(2,1)S(1)} %pad_maximum_fusion.5.refs_0_), channel_id=1, source_target_pairs={{0,8},{8,0},{16,24},{24,16},{1,9},{9,1},{17,25},{25,17},{2,10},{10... | collective-permute-start | bytes 2359304 | tf_op jit(solution)/shard_map/ppermute | solution.py:801
  121.3 30.2 %collective-permute-start.15 = (bf16[2,3,16,4096]{3,2,1,0:T(8,128)(2,1)}, bf16[2,3,16,4096]{3,2,1,0:T(8,128)(2,1)}, u32[]{:S(2)}, u32[]{:S(2)}) collective-permute-start(bf16[2,3,16,4096]{3,2,1,0:T(8,128)(2,1)} %copy-done.32), channel_id=1, source_target_pairs={{0,8},{8,0},{16,24},{24,16},{1,9},{9,1},{17,25},{25,17},{2,10},{10... | collective-permute-start | bytes 2359304 | tf_op jit(solution)/shard_map/ppermute | solution.py:801
  121.9 29.7 %collective-permute-start.16 = (bf16[2,3,16,4096]{3,2,1,0:T(8,128)(2,1)}, bf16[2,3,16,4096]{3,2,1,0:T(8,128)(2,1)}, u32[]{:S(2)}, u32[]{:S(2)}) collective-permute-start(bf16[2,3,16,4096]{3,2,1,0:T(8,128)(2,1)} %copy-done.25), channel_id=1, source_target_pairs={{0,8},{8,0},{16,24},{24,16},{1,9},{9,1},{17,25},{25,17},{2,10},{10... | collective-permute-start | bytes 2359304 | tf_op jit(solution)/shard_map/ppermute | solution.py:801
  121.9 29.7 %collective-permute-start.17 = (bf16[2,3,16,4096]{3,2,1,0:T(8,128)(2,1)}, bf16[2,3,16,4096]{3,2,1,0:T(8,128)(2,1)}, u32[]{:S(2)}, u32[]{:S(2)}) collective-permute-start(bf16[2,3,16,4096]{3,2,1,0:T(8,128)(2,1)} %copy-done.34), channel_id=1, source_target_pairs={{0,8},{8,0},{16,24},{24,16},{1,9},{9,1},{17,25},{25,17},{2,10},{10... | collective-permute-start | bytes 2359304 | tf_op jit(solution)/shard_map/ppermute | solution.py:801
  146.5 30.1 %collective-permute-start.19 = (bf16[2,3,64,1024]{3,2,1,0:T(8,128)(2,1)}, bf16[2,3,64,1024]{3,2,1,0:T(8,128)(2,1)}, u32[]{:S(2)}, u32[]{:S(2)}) collective-permute-start(bf16[2,3,64,1024]{3,2,1,0:T(8,128)(2,1)} %pad_maximum_fusion.7.refs_0_), channel_id=1, source_target_pairs={{0,1},{1,0},{2,3},{3,2},{4,5},{5,4},{6,7},{7,6},{8,9},{9,8},{10,11... | collective-permute-start | bytes 2359304 | tf_op jit(solution)/shard_map/ppermute | solution.py:801
  151.1 25.5 %collective-permute-start.21 = (bf16[2,3,64,1024]{3,2,1,0:T(8,128)(2,1)}, bf16[2,3,64,1024]{3,2,1,0:T(8,128)(2,1)}, u32[]{:S(2)}, u32[]{:S(2)}) collective-permute-start(bf16[2,3,64,1024]{3,2,1,0:T(8,128)(2,1)} %pad_maximum_fusion.8.refs_2_), channel_id=1, source_target_pairs={{0,16},{8,24},{16,0},{24,8},{1,17},{9,25},{17,1},{25,9},{2,18},{10... | collective-permute-start | bytes 2359304 | tf_op jit(solution)/shard_map/ppermute | solution.py:801
  325.0 25.7 %collective-permute-start.26 = (bf16[512,1024]{1,0:T(8,128)(2,1)}, bf16[512,1024]{1,0:T(8,128)(2,1)}, u32[]{:S(2)}, u32[]{:S(2)}) collective-permute-start(bf16[512,1024]{1,0:T(8,128)(2,1)} %dynamic-slice_bitcast_fusion.4), channel_id=1, source_target_pairs={{0,1},{1,0},{2,3},{3,2},{4,5},{5,4},{6,7},{7,6},{8,9},{9,8},{10,11... | collective-permute-start | bytes 3145736 | tf_op jit(solution)/shard_map/ppermute | solution.py:806
  369.6 227.1 %reduce-scatter.9.cloned.1.call-start = ((), (), s32[]{:S(2)}) async-start(), calls=%async_computation.9 | async-start | bytes 9437184 | tf_op jit(solution)/shard_map/reduce_scatter | solution.py:1147
  405.2 191.5 %reduce-scatter.11.cloned.1.call-start = ((), (), s32[]{:S(2)}) async-start(), calls=%async_computation.10 | async-start | bytes 7077888 | tf_op jit(solution)/shard_map/reduce_scatter | solution.py:1147
  472.8 227.0 %reduce-scatter.13.cloned.1.call-start = ((), (), s32[]{:S(2)}) async-start(), calls=%async_computation.11 | async-start | bytes 3604480 | tf_op jit(solution)/shard_map/reduce_scatter | solution.py:1157
  605.2 213.8 %reduce-scatter.15.cloned.1.call-start = ((), (), s32[]{:S(2)}) async-start(), calls=%async_computation.12 | async-start | bytes 9437184 | tf_op jit(solution)/shard_map/reduce_scatter | solution.py:1147
  607.7 64.3 %collective-permute-start.28 = (bf16[512,1024]{1,0:T(8,128)(2,1)}, bf16[512,1024]{1,0:T(8,128)(2,1)}, u32[]{:S(2)}, u32[]{:S(2)}) collective-permute-start(bf16[512,1024]{1,0:T(8,128)(2,1)} %constant_dynamic-slice_fusion.3), channel_id=1, source_target_pairs={{0,1},{1,0},{2,3},{3,2},{4,5},{5,4},{6,7},{7,6},{8,9},{9,8},{10,11... | collective-permute-start | bytes 3145736 | tf_op jit(solution)/shard_map/ppermute | solution.py:806
  672.0 21.5 %collective-permute-start.27 = (bf16[4,2,2,128,1024]{4,3,0,1,2:T(8,128)(2,1)}, bf16[4,2,2,128,1024]{4,3,0,1,2:T(8,128)(2,1)}, u32[]{:S(2)}, u32[]{:S(2)}) collective-permute-start(bf16[4,2,2,128,1024]{4,3,0,1,2:T(8,128)(2,1)} %bitcast.305), channel_id=1, source_target_pairs={{0,8},{1,9},{8,0},{9,1},{16,24},{17,25},{24,16},{25,17},{2,10},{3,... | collective-permute-start | bytes 12582920 | tf_op jit(solution)/shard_map/ppermute | solution.py:894
  674.3 176.7 %reduce-scatter.17.cloned.1.call-start = ((), (), s32[]{:S(2)}) async-start(), calls=%async_computation.13 | async-start | bytes 1310720 | tf_op jit(solution)/shard_map/reduce_scatter | solution.py:1157
  702.8 44.1 %collective-permute-start.29 = (bf16[4,2,64,1024]{3,2,0,1:T(8,128)(2,1)S(1)}, bf16[4,2,64,1024]{3,2,0,1:T(8,128)(2,1)S(1)}, u32[]{:S(2)}, u32[]{:S(2)}) collective-permute-start(bf16[4,2,64,1024]{3,2,0,1:T(8,128)(2,1)S(1)} %dynamic-slice_bitcast_fusion.3), channel_id=1, source_target_pairs={{0,16},{1,17},{8,24},{9,25},{16,0},{17,1},{24,8},{25,9},{2,18},{3,... | collective-permute-start | bytes 3145736 | tf_op jit(solution)/shard_map/ppermute | solution.py:894
  704.6 40.9 %collective-permute-start.30 = (bf16[4,2,64,1024]{3,2,0,1:T(8,128)(2,1)S(1)}, bf16[4,2,64,1024]{3,2,0,1:T(8,128)(2,1)S(1)}, u32[]{:S(2)}, u32[]{:S(2)}) collective-permute-start(bf16[4,2,64,1024]{3,2,0,1:T(8,128)(2,1)S(1)} %dynamic-slice_bitcast_fusion.2), channel_id=1, source_target_pairs={{0,1},{1,0},{8,9},{9,8},{16,17},{17,16},{24,25},{25,24},{2,3},{3,2... | collective-permute-start | bytes 3145736 | tf_op jit(solution)/shard_map/ppermute | solution.py:894
  758.1 18.8 %collective-permute-start.33 = (bf16[4,2,2,32,4096]{4,3,0,1,2:T(8,128)(2,1)S(1)}, bf16[4,2,2,32,4096]{4,3,0,1,2:T(8,128)(2,1)S(1)}, u32[]{:S(2)}, u32[]{:S(2)}) collective-permute-start(bf16[4,2,2,32,4096]{4,3,0,1,2:T(8,128)(2,1)S(1)} %bitcast.343), channel_id=1, source_target_pairs={{0,8},{1,9},{8,0},{9,1},{16,24},{17,25},{24,16},{25,17},{2,10},{3,... | collective-permute-start | bytes 12582920 | tf_op jit(solution)/shard_map/ppermute | solution.py:894
  786.6 29.2 %collective-permute-start.37 = (bf16[4,2,16,4096]{3,2,0,1:T(8,128)(2,1)}, bf16[4,2,16,4096]{3,2,0,1:T(8,128)(2,1)}, u32[]{:S(2)}, u32[]{:S(2)}) collective-permute-start(bf16[4,2,16,4096]{3,2,0,1:T(8,128)(2,1)} %dynamic-slice_bitcast_fusion.1), channel_id=1, source_target_pairs={{0,16},{1,17},{8,24},{9,25},{16,0},{17,1},{24,8},{25,9},{2,18},{3,... | collective-permute-start | bytes 3145736 | tf_op jit(solution)/shard_map/ppermute | solution.py:894
  792.4 22.2 %collective-permute-start.35 = (bf16[128,1024]{1,0:T(8,128)(2,1)S(1)}, bf16[128,1024]{1,0:T(8,128)(2,1)S(1)}, u32[]{:S(2)}, u32[]{:S(2)}) collective-permute-start(bf16[128,1024]{1,0:T(8,128)(2,1)S(1)} %get-tuple-element.282), channel_id=1, source_target_pairs={{0,4},{2,6},{4,0},{6,2},{1,5},{3,7},{5,1},{7,3},{8,12},{10,14},{12... | collective-permute-start | bytes 786440 | tf_op jit(solution)/shard_map/ppermute | solution.py:806
  792.4 22.2 %collective-permute-start.34 = (bf16[128,1024]{1,0:T(8,128)(2,1)S(1)}, bf16[128,1024]{1,0:T(8,128)(2,1)S(1)}, u32[]{:S(2)}, u32[]{:S(2)}) collective-permute-start(bf16[128,1024]{1,0:T(8,128)(2,1)S(1)} %get-tuple-element.280), channel_id=1, source_target_pairs={{0,2},{2,4},{4,6},{6,0},{1,3},{3,5},{5,7},{7,1},{8,10},{10,12},{12... | collective-permute-start | bytes 786440 | tf_op jit(solution)/shard_map/ppermute | solution.py:806
  794.8 23.9 %collective-permute-start.38 = (bf16[4,2,16,4096]{3,2,0,1:T(8,128)(2,1)S(1)}, bf16[4,2,16,4096]{3,2,0,1:T(8,128)(2,1)S(1)}, u32[]{:S(2)}, u32[]{:S(2)}) collective-permute-start(bf16[4,2,16,4096]{3,2,0,1:T(8,128)(2,1)S(1)} %dynamic-slice_bitcast_fusion), channel_id=1, source_target_pairs={{0,1},{1,0},{8,9},{9,8},{16,17},{17,16},{24,25},{25,24},{2,3},{3,2... | collective-permute-start | bytes 3145736 | tf_op jit(solution)/shard_map/ppermute | solution.py:894
  821.6 125.8 %all-gather.16.cloned.1.call-start = ((), (), s32[]{:S(2)}) async-start(), calls=%async_computation.16 | async-start | bytes 6488064 | tf_op jit(solution)/shard_map/all_gather | solution.py:1161
  822.2 154.1 %all-gather.12.cloned.1.call-start = ((), (), s32[]{:S(2)}) async-start(), calls=%async_computation.14 | async-start | bytes 2359296 | tf_op jit(solution)/shard_map/all_gather | solution.py:1161
  827.3 19.8 %collective-permute-start.43 = (bf16[4,16,4096]{2,1,0:T(8,128)(2,1)S(1)}, bf16[4,16,4096]{2,1,0:T(8,128)(2,1)S(1)}, u32[]{:S(2)}, u32[]{:S(2)}) collective-permute-start(bf16[4,16,4096]{2,1,0:T(8,128)(2,1)S(1)} %dynamic-slice_bitcast_fusion.6), channel_id=1, source_target_pairs={{0,16},{1,17},{8,24},{9,25},{16,0},{17,1},{24,8},{25,9},{2,18},{3,... | collective-permute-start | bytes 1572872 | tf_op jit(solution)/shard_map/ppermute | solution.py:894
  828.3 20.8 %collective-permute-start.42 = (bf16[4,16,4096]{2,1,0:T(8,128)(2,1)S(1)}, bf16[4,16,4096]{2,1,0:T(8,128)(2,1)S(1)}, u32[]{:S(2)}, u32[]{:S(2)}) collective-permute-start(bf16[4,16,4096]{2,1,0:T(8,128)(2,1)S(1)} %dynamic-slice_bitcast_fusion.7), channel_id=1, source_target_pairs={{0,1},{1,0},{8,9},{9,8},{16,17},{17,16},{24,25},{25,24},{2,3},{3,2... | collective-permute-start | bytes 1572872 | tf_op jit(solution)/shard_map/ppermute | solution.py:894
  857.5 28.1 %collective-permute-start.48 = (bf16[32,4096]{1,0:T(8,128)(2,1)S(1)}, bf16[32,4096]{1,0:T(8,128)(2,1)S(1)}, u32[]{:S(2)}, u32[]{:S(2)}) collective-permute-start(bf16[32,4096]{1,0:T(8,128)(2,1)S(1)} %get-tuple-element.278), channel_id=1, source_target_pairs={{0,6},{2,0},{4,2},{6,4},{1,7},{3,1},{5,3},{7,5},{8,14},{10,8},{12,... | collective-permute-start | bytes 786440 | tf_op jit(solution)/shard_map/ppermute | solution.py:806
  858.6 27.1 %collective-permute-start.47 = (bf16[32,4096]{1,0:T(8,128)(2,1)S(1)}, bf16[32,4096]{1,0:T(8,128)(2,1)S(1)}, u32[]{:S(2)}, u32[]{:S(2)}) collective-permute-start(bf16[32,4096]{1,0:T(8,128)(2,1)S(1)} %get-tuple-element.279), channel_id=1, source_target_pairs={{0,4},{2,6},{4,0},{6,2},{1,5},{3,7},{5,1},{7,3},{8,12},{10,14},{12... | collective-permute-start | bytes 786440 | tf_op jit(solution)/shard_map/ppermute | solution.py:806
  858.6 27.1 %collective-permute-start.46 = (bf16[32,4096]{1,0:T(8,128)(2,1)S(1)}, bf16[32,4096]{1,0:T(8,128)(2,1)S(1)}, u32[]{:S(2)}, u32[]{:S(2)}) collective-permute-start(bf16[32,4096]{1,0:T(8,128)(2,1)S(1)} %get-tuple-element.277), channel_id=1, source_target_pairs={{0,2},{2,4},{4,6},{6,0},{1,3},{3,5},{5,7},{7,1},{8,10},{10,12},{12... | collective-permute-start | bytes 786440 | tf_op jit(solution)/shard_map/ppermute | solution.py:806
  860.2 24.4 %collective-permute-start.50 = (f32[64,256]{1,0:T(8,128)S(1)}, f32[64,256]{1,0:T(8,128)S(1)}, u32[]{:S(2)}, u32[]{:S(2)}) collective-permute-start(f32[64,256]{1,0:T(8,128)S(1)} %get-tuple-element.285), channel_id=1, source_target_pairs={{0,4},{2,6},{4,0},{6,2},{1,5},{3,7},{5,1},{7,3},{8,12},{10,14},{12... | collective-permute-start | bytes 196616 | tf_op jit(solution)/shard_map/ppermute | solution.py:806
  862.6 23.1 %collective-permute-start.49 = (f32[64,256]{1,0:T(8,128)S(1)}, f32[64,256]{1,0:T(8,128)S(1)}, u32[]{:S(2)}, u32[]{:S(2)}) collective-permute-start(f32[64,256]{1,0:T(8,128)S(1)} %get-tuple-element.283), channel_id=1, source_target_pairs={{0,2},{2,4},{4,6},{6,0},{1,3},{3,5},{5,7},{7,1},{8,10},{10,12},{12... | collective-permute-start | bytes 196616 | tf_op jit(solution)/shard_map/ppermute | solution.py:806
  884.6 50.4 %collective-permute-start.44 = (bf16[512,1024]{1,0:T(8,128)(2,1)S(1)}, bf16[512,1024]{1,0:T(8,128)(2,1)S(1)}, u32[]{:S(2)}, u32[]{:S(2)}) collective-permute-start(bf16[512,1024]{1,0:T(8,128)(2,1)S(1)} %constant_dynamic-slice_fusion), channel_id=1, source_target_pairs={{0,1},{1,0},{2,3},{3,2},{4,5},{5,4},{6,7},{7,6},{8,9},{9,8},{10,11... | collective-permute-start | bytes 3145736 | tf_op jit(solution)/shard_map/ppermute | solution.py:806
  889.8 37.7 %collective-permute-start.60 = (bf16[32,4096]{1,0:T(8,128)(2,1)S(1)}, bf16[32,4096]{1,0:T(8,128)(2,1)S(1)}, u32[]{:S(2)}, u32[]{:S(2)}) collective-permute-start(bf16[32,4096]{1,0:T(8,128)(2,1)S(1)} %fusion.58), channel_id=1, source_target_pairs={{0,1},{1,0},{8,9},{9,8},{16,17},{17,16},{24,25},{25,24},{2,3},{3,2... | collective-permute-start | bytes 786440 | tf_op jit(solution)/shard_map/ppermute | solution.py:894
  891.2 36.2 %collective-permute-start.59 = (bf16[32,4096]{1,0:T(8,128)(2,1)S(1)}, bf16[32,4096]{1,0:T(8,128)(2,1)S(1)}, u32[]{:S(2)}, u32[]{:S(2)}) collective-permute-start(bf16[32,4096]{1,0:T(8,128)(2,1)S(1)} %fusion.58), channel_id=1, source_target_pairs={{0,16},{1,17},{8,24},{9,25},{16,0},{17,1},{24,8},{25,9},{2,18},{3,... | collective-permute-start | bytes 786440 | tf_op jit(solution)/shard_map/ppermute | solution.py:894
  927.6 40.8 %collective-permute-start.62 = (bf16[4,32,4096]{2,1,0:T(8,128)(2,1)S(1)}, bf16[4,32,4096]{2,1,0:T(8,128)(2,1)S(1)}, u32[]{:S(2)}, u32[]{:S(2)}) collective-permute-start(bf16[4,32,4096]{2,1,0:T(8,128)(2,1)S(1)} %pad_maximum_fusion.4.near_ref), channel_id=1, source_target_pairs={{0,8},{1,9},{8,0},{9,1},{16,24},{17,25},{24,16},{25,17},{2,10},{3,... | collective-permute-start | bytes 3145736 | tf_op jit(solution)/shard_map/ppermute | solution.py:894
  (122 other events, 1929.7 us)
Sparse Core Ops, SparseCore 0:
  11.1 118.2 all-gather.7
  132.3 109.0 all-gather.9
  244.5 75.5 all-gather.13
  369.7 68.9 reduce-scatter.6
  442.4 71.2 reduce-scatter.8
  517.0 61.8 reduce-scatter.10
  605.3 53.5 reduce-scatter.12
  674.4 94.0 reduce-scatter.14
  821.7 27.1 reduce-scatter.16
  850.8 53.2 all-gather.15
  906.2 37.3 all-gather.11
